TPU v7x, 32 devices: a whole 2x2x4 slice. The times are simulated.
32 devices in a mesh: exp: 8 (over z, x), rep: 4 (over y, core).
Axes of the slice: x: 2, y: 2, z: 4, core: 2. Of those that a mesh axis runs over, the one named last changes fastest.
Arguments:
- tokens: bfloat16 [18432, 768], P(('exp', 'rep')), may hold values from -6 to 6
- ln1_gain: bfloat16 [768], P(('exp', 'rep')), may hold values from 0.3984375 to 1.59375
- ln1_bias: bfloat16 [768], P(('exp', 'rep')), may hold values from -1.1953125 to 1.1953125
- w_qkv: bfloat16 [768, 2304], P(('exp', 'rep')), may hold values from -0.21875 to 0.21875
- w_out: bfloat16 [768, 768], P(('exp', 'rep')), may hold values from -2.5 to 2.5
- ln2_gain: bfloat16 [768], P(('exp', 'rep')), may hold values from 0.3984375 to 1.59375
- ln2_bias: bfloat16 [768], P(('exp', 'rep')), may hold values from -0.59765625 to 0.59765625
- w_router: bfloat16 [768, 8], P(('exp', 'rep')), may hold values from -0.109375 to 0.109375
- w_in: bfloat16 [8, 768, 3072], P('exp'), may hold values from -0.21875 to 0.21875
- b_in: bfloat16 [8, 3072], P('exp'), may hold values from -1.796875 to 1.796875
- w_back: bfloat16 [8, 3072, 768], P('exp'), may hold values from -0.625 to 0.625
- b_back: bfloat16 [8, 768], P('exp'), may hold values from -2.390625 to 2.390625
- lengths: int32 [32, 3], P(('exp', 'rep')), may hold values from 1 to 400, 576 in all within a row
- routes: int32 [18432, 2], P(('exp', 'rep')), may hold values from 0 to 7, all different within a row
- priority: int32 [18432], P(('exp', 'rep')), may hold values from 0 to 575, as said below
- padding: int32 [18432], P(('exp', 'rep')), may hold values 0 or 1
- cotangent: bfloat16 [18432, 768], P(('exp', 'rep')), may hold values from -6 to 6
Outputs:
- output: bfloat16 [18432, 768], P(('exp', 'rep'))
- grad_tokens: float32 [18432, 768], P(('exp', 'rep'))
- grad_ln1_gain: float32 [768], P(('exp', 'rep'))
- grad_ln1_bias: float32 [768], P(('exp', 'rep'))
- grad_w_qkv: float32 [768, 2304], P(('exp', 'rep'))
- grad_w_out: float32 [768, 768], P(('exp', 'rep'))
- grad_ln2_gain: float32 [768], P(('exp', 'rep'))
- grad_ln2_bias: float32 [768], P(('exp', 'rep'))
- grad_w_router: float32 [768, 8], P(('exp', 'rep'))
- grad_w_in: float32 [8, 768, 3072], P('exp')
- grad_b_in: float32 [8, 3072], P('exp')
- grad_w_back: float32 [8, 3072, 768], P('exp')
- grad_b_back: float32 [8, 768], P('exp')
Inputs may be any that keep to these rules, and one draw needn't show every extreme that they name: `routes`: each row names two different experts. `priority`: in each aligned group of 576 patches every value 0 to 575 appears once. `lengths`: each row sums to 576; its largest entry is 400.
All inputs are finite; a program needn't handle non-finite values. No bound on the sum of `padding` on one device may be relied on, other than what follows from the above.
Results may differ from a plain program's by a relative error of at most 0.014.
Values may be sent and summed in bfloat16 or wider, within the bound.
A program may use at most 192 MiB of HBM per device.

v0:
```python
import jax
import jax.numpy as jnp
from jax import lax
from jax.sharding import PartitionSpec as P

D = 768
HEADS = 12
HEAD = 64
SLOTS = 576
ROWS_DEV = 1
TOK_DEV = 576


root_half = 0.7071067811865476
inverse_root_tau = 0.3989422804014327
contract_first = (((0,), (0,)), ((), ()))
contract_last = (((1,), (1,)), ((), ()))


def norm_forward(inputs, gain, offset):
    center = inputs - jnp.mean(inputs, axis=-1, keepdims=True)
    inverse = lax.rsqrt(jnp.mean(center * center, axis=-1, keepdims=True) + 1e-06)
    normal = center * inverse
    return (normal * gain.astype(jnp.float32) + offset.astype(jnp.float32), normal, inverse)


def norm_backward(grad, normal, inverse, gain):
    scaled = grad * gain.astype(jnp.float32)
    grad_in = inverse * (
        scaled
        - jnp.mean(scaled, axis=-1, keepdims=True)
        - normal * jnp.mean(scaled * normal, axis=-1, keepdims=True)
    )
    return (grad_in, jnp.sum(grad * normal, axis=0), jnp.sum(grad, axis=0))


def gelu_slope(pre):
    return 0.5 * (1.0 + lax.erf(pre * root_half)) + pre * inverse_root_tau * jnp.exp(
        -0.5 * pre * pre
    )


def row_masks(lengths, padding):
    bounds = jnp.cumsum(lengths, axis=1)
    places = jnp.arange(SLOTS, dtype=jnp.int32)
    segments = jnp.sum((places[None, :, None] >= bounds[:, None, :]).astype(jnp.int32), axis=2)
    live = padding.reshape(ROWS_DEV, SLOTS) == 1
    same = segments[:, :, None] == segments[:, None, :]
    diagonal = places[:, None] == places[None, :]
    return same & (live[:, None, :] | diagonal[None])


def split_heads(qkv_row):
    query = qkv_row[:, :D].reshape(SLOTS, HEADS, HEAD)
    keys = qkv_row[:, D : 2 * D].reshape(SLOTS, HEADS, HEAD)
    values = qkv_row[:, 2 * D :].reshape(SLOTS, HEADS, HEAD)
    return (query, keys, values)


def masked_scores(query, keys, allowed_row):
    scores = jnp.einsum("qhc,khc->hqk", query, keys, preferred_element_type=jnp.float32) * HEAD ** (
        -0.5
    )
    return jnp.where(allowed_row[None], scores, -1e30)


def attend_forward(qkv_row, allowed_row):
    query, keys, values = split_heads(qkv_row)
    scores = masked_scores(query, keys, allowed_row)
    top = jnp.max(scores, axis=-1, keepdims=True)
    expo = jnp.exp(scores - top)
    total = jnp.sum(expo, axis=-1, keepdims=True)
    probs = (expo / total).astype(jnp.bfloat16)
    mixed = jnp.einsum("hqk,khc->qhc", probs, values, preferred_element_type=jnp.float32)
    return (mixed.reshape(SLOTS, D), top + jnp.log(total))


def attend_backward(qkv_row, allowed_row, lse_row, grad_row):
    query, keys, values = split_heads(qkv_row)
    probs = jnp.exp(masked_scores(query, keys, allowed_row) - lse_row)
    grad_mixed = grad_row.reshape(SLOTS, HEADS, HEAD)
    grad_probs = jnp.einsum("qhc,khc->hqk", grad_mixed, values, preferred_element_type=jnp.float32)
    grad_values = jnp.einsum(
        "hqk,qhc->khc", probs.astype(jnp.bfloat16), grad_mixed, preferred_element_type=jnp.float32
    )
    grad_scores = (
        probs * (grad_probs - jnp.sum(probs * grad_probs, axis=-1, keepdims=True))
    ).astype(jnp.bfloat16)
    grad_query = jnp.einsum(
        "hqk,khc->qhc", grad_scores, keys, preferred_element_type=jnp.float32
    ) * HEAD ** (-0.5)
    grad_keys = jnp.einsum(
        "hqk,qhc->khc", grad_scores, query, preferred_element_type=jnp.float32
    ) * HEAD ** (-0.5)
    joined = jnp.concatenate(
        [grad_query.reshape(SLOTS, D), grad_keys.reshape(SLOTS, D), grad_values.reshape(SLOTS, D)],
        axis=1,
    )
    return joined.astype(jnp.bfloat16)


def dispatch_tables(routes, priority, padding, experts, capacity):
    labels = jnp.arange(experts, dtype=jnp.int32)
    first_hot = (routes[:, 0:1] == labels[None, :]).astype(jnp.bfloat16)
    second_hot = (routes[:, 1:2] == labels[None, :]).astype(jnp.bfloat16)
    live = padding[:, None].astype(jnp.bfloat16)
    earlier = (priority[None, :] < priority[:, None]).astype(jnp.bfloat16)
    before_first = jnp.dot(earlier, first_hot * live, preferred_element_type=jnp.float32)
    first_counts = jnp.sum((first_hot * live).astype(jnp.float32), axis=0)
    before_second = (
        jnp.dot(earlier, second_hot * live, preferred_element_type=jnp.float32)
        + first_counts[None, :]
    )
    place_first = jnp.sum(before_first * first_hot, axis=1).astype(jnp.int32)
    place_second = jnp.sum(before_second * second_hot, axis=1).astype(jnp.int32)
    kept_first = (padding == 1) & (place_first < capacity)
    kept_second = (padding == 1) & (place_second < capacity)
    slot_labels = jnp.arange(experts * capacity, dtype=jnp.int32)
    slot_first = routes[:, 0] * capacity + place_first
    slot_second = routes[:, 1] * capacity + place_second
    pick_first = ((slot_first[:, None] == slot_labels[None, :]) & kept_first[:, None]).astype(
        jnp.bfloat16
    )
    pick_second = ((slot_second[:, None] == slot_labels[None, :]) & kept_second[:, None]).astype(
        jnp.bfloat16
    )
    return (first_hot.astype(jnp.float32), second_hot.astype(jnp.float32), pick_first, pick_second)


def on_device(
    tokens,
    ln1_gain,
    ln1_bias,
    w_qkv,
    w_out,
    ln2_gain,
    ln2_bias,
    w_router,
    w_in,
    b_in,
    w_back,
    b_back,
    lengths,
    routes,
    priority,
    padding,
    cotangent,
):
    experts = lax.axis_size("exp")
    capacity = (TOK_DEV * 210 + experts * 100 - 1) // (experts * 100)
    dense = (
        lax.all_gather(ln1_gain, ("exp", "rep"), axis=0, tiled=True),
        lax.all_gather(ln1_bias, ("exp", "rep"), axis=0, tiled=True),
        lax.all_gather(w_qkv, ("exp", "rep"), axis=0, tiled=True),
        lax.all_gather(w_out, ("exp", "rep"), axis=0, tiled=True),
        lax.all_gather(ln2_gain, ("exp", "rep"), axis=0, tiled=True),
        lax.all_gather(ln2_bias, ("exp", "rep"), axis=0, tiled=True),
        lax.all_gather(w_router, ("exp", "rep"), axis=0, tiled=True),
    )
    gain_one, bias_one, qkv_weight, out_weight, gain_two, bias_two, router_weight = dense
    inputs = tokens.astype(jnp.float32)
    normed, normal_one, inverse_one = norm_forward(inputs, gain_one, bias_one)
    normed_low = normed.astype(jnp.bfloat16)
    qkv = (
        jnp.dot(normed_low, qkv_weight, preferred_element_type=jnp.float32)
        .astype(jnp.bfloat16)
        .reshape(ROWS_DEV, SLOTS, 3 * D)
    )
    allowed = row_masks(lengths, padding)
    mixed, lse = lax.map(lambda pair: attend_forward(pair[0], pair[1]), (qkv, allowed))
    mixed_low = mixed.reshape(TOK_DEV, D).astype(jnp.bfloat16)
    resid = inputs + jnp.dot(mixed_low, out_weight, preferred_element_type=jnp.float32)
    routed_float, normal_two, inverse_two = norm_forward(resid, gain_two, bias_two)
    routed = routed_float.astype(jnp.bfloat16)
    logits = jnp.dot(routed, router_weight, preferred_element_type=jnp.float32)
    probs = jax.nn.softmax(logits, axis=-1)
    first_hot, second_hot, pick_first, pick_second = dispatch_tables(
        routes, priority, padding, experts, capacity
    )
    picks = pick_first + pick_second
    buffer = lax.dot_general(picks, routed, contract_first, preferred_element_type=jnp.float32)
    buffer = buffer.astype(jnp.bfloat16).reshape(experts, capacity, D)
    received_part = lax.all_to_all(buffer, "exp", split_axis=0, concat_axis=0, tiled=True)
    pre_part = jnp.einsum(
        "scd,df->scf", received_part, w_in[0], preferred_element_type=jnp.float32
    ) + b_in[0].astype(jnp.float32)
    active_part = jax.nn.gelu(pre_part, approximate=False).astype(jnp.bfloat16)
    result_part = jnp.einsum(
        "scf,fd->scd", active_part, w_back[0], preferred_element_type=jnp.float32
    ) + b_back[0].astype(jnp.float32)
    returned = lax.all_to_all(
        result_part.astype(jnp.bfloat16), "exp", split_axis=0, concat_axis=0, tiled=True
    )
    returned_flat = returned.reshape(experts * capacity, D)
    picked_first = jnp.dot(pick_first, returned_flat, preferred_element_type=jnp.float32)
    picked_second = jnp.dot(pick_second, returned_flat, preferred_element_type=jnp.float32)
    gate_first = jnp.sum(probs * first_hot, axis=1)
    gate_second = jnp.sum(probs * second_hot, axis=1)
    output = resid + gate_first[:, None] * picked_first + gate_second[:, None] * picked_second
    grad_out = cotangent.astype(jnp.float32)
    gated_first = (gate_first[:, None] * grad_out).astype(jnp.bfloat16)
    gated_second = (gate_second[:, None] * grad_out).astype(jnp.bfloat16)
    grad_slots = lax.dot_general(
        pick_first, gated_first, contract_first, preferred_element_type=jnp.float32
    )
    grad_slots = grad_slots + lax.dot_general(
        pick_second, gated_second, contract_first, preferred_element_type=jnp.float32
    )
    grad_results = lax.all_to_all(
        grad_slots.astype(jnp.bfloat16).reshape(experts, capacity, D),
        "exp",
        split_axis=0,
        concat_axis=0,
        tiled=True,
    )
    pre = jnp.einsum(
        "scd,df->scf", received_part, w_in[0], preferred_element_type=jnp.float32
    ) + b_in[0].astype(jnp.float32)
    active = jax.nn.gelu(pre, approximate=False).astype(jnp.bfloat16)
    grad_w_back = jnp.einsum(
        "scf,scd->fd", active, grad_results, preferred_element_type=jnp.float32
    )
    grad_b_back = jnp.sum(grad_results.astype(jnp.float32), axis=(0, 1))
    grad_active = jnp.einsum(
        "scd,fd->scf", grad_results, w_back[0], preferred_element_type=jnp.float32
    )
    grad_pre = (grad_active * gelu_slope(pre)).astype(jnp.bfloat16)
    grad_w_in = jnp.einsum(
        "scd,scf->df", received_part, grad_pre, preferred_element_type=jnp.float32
    )
    grad_b_in = jnp.sum(grad_pre.astype(jnp.float32), axis=(0, 1))
    expert_sums = (
        lax.psum(grad_w_in.astype(jnp.bfloat16), "rep").astype(jnp.float32),
        lax.psum(grad_b_in.astype(jnp.bfloat16), "rep").astype(jnp.float32),
        lax.psum(grad_w_back.astype(jnp.bfloat16), "rep").astype(jnp.float32),
        lax.psum(grad_b_back.astype(jnp.bfloat16), "rep").astype(jnp.float32),
    )
    grad_received = jnp.einsum(
        "scf,df->scd", grad_pre, w_in[0], preferred_element_type=jnp.float32
    ).astype(jnp.bfloat16)
    grad_buffer = lax.all_to_all(
        grad_received, "exp", split_axis=0, concat_axis=0, tiled=True
    ).reshape(experts * capacity, D)
    grad_gate_first = jnp.sum(grad_out * picked_first, axis=1)
    grad_gate_second = jnp.sum(grad_out * picked_second, axis=1)
    grad_probs = grad_gate_first[:, None] * first_hot + grad_gate_second[:, None] * second_hot
    grad_logits = (
        probs * (grad_probs - jnp.sum(probs * grad_probs, axis=1, keepdims=True))
    ).astype(jnp.bfloat16)
    dense_back = (
        lax.all_gather(ln1_gain, ("exp", "rep"), axis=0, tiled=True),
        lax.all_gather(ln1_bias, ("exp", "rep"), axis=0, tiled=True),
        lax.all_gather(w_qkv, ("exp", "rep"), axis=0, tiled=True),
        lax.all_gather(w_out, ("exp", "rep"), axis=0, tiled=True),
        lax.all_gather(ln2_gain, ("exp", "rep"), axis=0, tiled=True),
        lax.all_gather(ln2_bias, ("exp", "rep"), axis=0, tiled=True),
        lax.all_gather(w_router, ("exp", "rep"), axis=0, tiled=True),
    )
    gain_one, bias_one, qkv_weight, out_weight, gain_two, bias_two, router_weight = dense_back
    grad_router = lax.dot_general(
        routed, grad_logits, contract_first, preferred_element_type=jnp.float32
    )
    grad_routed = jnp.dot(picks, grad_buffer, preferred_element_type=jnp.float32)
    grad_routed = grad_routed + lax.dot_general(
        grad_logits, router_weight, contract_last, preferred_element_type=jnp.float32
    )
    grad_norm_two, grad_gain_two, grad_bias_two = norm_backward(
        grad_routed, normal_two, inverse_two, gain_two
    )
    grad_resid = grad_out + grad_norm_two
    grad_attn = grad_resid.astype(jnp.bfloat16)
    grad_out_weight = lax.dot_general(
        mixed_low, grad_attn, contract_first, preferred_element_type=jnp.float32
    )
    grad_mixed = lax.dot_general(
        grad_attn, out_weight, contract_last, preferred_element_type=jnp.float32
    )
    grad_mixed = grad_mixed.astype(jnp.bfloat16).reshape(ROWS_DEV, SLOTS, D)
    grad_qkv = lax.map(
        lambda group: attend_backward(group[0], group[1], group[2], group[3]),
        (qkv, allowed, lse, grad_mixed),
    )
    grad_qkv = grad_qkv.reshape(TOK_DEV, 3 * D)
    grad_qkv_weight = lax.dot_general(
        normed_low, grad_qkv, contract_first, preferred_element_type=jnp.float32
    )
    grad_normed = lax.dot_general(
        grad_qkv, qkv_weight, contract_last, preferred_element_type=jnp.float32
    )
    grad_norm_one, grad_gain_one, grad_bias_one = norm_backward(
        grad_normed, normal_one, inverse_one, gain_one
    )
    grad_tokens = grad_resid + grad_norm_one
    dense_grads = (
        lax.psum_scatter(grad_gain_one, ("exp", "rep"), scatter_dimension=0, tiled=True),
        lax.psum_scatter(grad_bias_one, ("exp", "rep"), scatter_dimension=0, tiled=True),
        lax.psum_scatter(grad_qkv_weight, ("exp", "rep"), scatter_dimension=0, tiled=True),
        lax.psum_scatter(grad_out_weight, ("exp", "rep"), scatter_dimension=0, tiled=True),
        lax.psum_scatter(grad_gain_two, ("exp", "rep"), scatter_dimension=0, tiled=True),
        lax.psum_scatter(grad_bias_two, ("exp", "rep"), scatter_dimension=0, tiled=True),
        lax.psum_scatter(grad_router, ("exp", "rep"), scatter_dimension=0, tiled=True),
    )
    return (
        output.astype(jnp.bfloat16),
        grad_tokens,
        dense_grads[0],
        dense_grads[1],
        dense_grads[2],
        dense_grads[3],
        dense_grads[4],
        dense_grads[5],
        dense_grads[6],
        expert_sums[0][None],
        expert_sums[1][None],
        expert_sums[2][None],
        expert_sums[3][None],
    )


def solution(mesh):
    return jax.shard_map(
        on_device,
        mesh=mesh,
        in_specs=(
            P(("exp", "rep"), None),
            P(("exp", "rep")),
            P(("exp", "rep")),
            P(("exp", "rep"), None),
            P(("exp", "rep"), None),
            P(("exp", "rep")),
            P(("exp", "rep")),
            P(("exp", "rep"), None),
            P("exp", None, None),
            P("exp", None),
            P("exp", None, None),
            P("exp", None),
            P(("exp", "rep"), None),
            P(("exp", "rep"), None),
            P(("exp", "rep")),
            P(("exp", "rep")),
            P(("exp", "rep"), None),
        ),
        out_specs=(
            P(("exp", "rep"), None),
            P(("exp", "rep"), None),
            P(("exp", "rep")),
            P(("exp", "rep")),
            P(("exp", "rep"), None),
            P(("exp", "rep"), None),
            P(("exp", "rep")),
            P(("exp", "rep")),
            P(("exp", "rep"), None),
            P("exp", None, None),
            P("exp", None),
            P("exp", None, None),
            P("exp", None),
        ),
        check_vma=False,
    )
```

profile of v0, /device:TPU:0, one launch (start us, length us, event | category | flops | bytes accessed | tf_op | source)
XLA Modules:
  0.0 835.7 jit_solution(4616695605341948638)
XLA Ops:
  10.2 1.2 fusion.102
  12.1 0.8 dynamic-update-slice.3
  13.0 0.8 dynamic-update-slice
  13.8 0.8 dynamic-update-slice.1
  14.6 0.8 dynamic-update-slice.2
  15.5 42.2 %all-reduce.10 = (bf16[768]{0:T(1024)(128)(2,1)S(1)}, bf16[768]{0:T(1024)(128)(2,1)S(1)}, bf16[768]{0:T(1024)(128)(2,1)S(1)}, bf16[768]{0:T(1024)(128)(2,1)S(1)}) all-reduce(bf16[768]{0:T(1024)(128)(2,1)S(1)} %dynamic-update-slice.1, bf16[768]{0:T(1024)(128)(2,1)S(1)} %dynamic-update-slice, ...), channel_id=1, replica_groups=mesh['exp'=8,'rep'=4] {'exp','rep'}, use_global_device_ids=true, to_apply=%add.1 | all-reduce | flops 3072 | bytes 12288
  58.6 1.4 convert_reduce_fusion
  60.0 1.6 fusion.65
  62.4 1.2 fusion.99
  64.7 9.0 %all-gather.4.cloned.1.call-done = bf16[768,2304]{1,0:T(8,128)(2,1)} async-done(((bf16[24,2304]{1,0:T(8,128)(2,1)}), bf16[768,2304]{1,0:T(8,128)(2,1)}) %all-gather.4.cloned.1.call-update) | async-done | bytes 3538960 | tf_op jit(solution)/shard_map/all_gather | solution.py:154
  73.7 4.7 convolution_convert_fusion
  78.4 1.1 fusion.140
  80.1 1.9 copy.61
  82.0 1.4 copy.60
  83.4 8.0 fusion.141
  91.4 8.6 %fusion = f32[12,576]{1,0:T(8,128)S(1)} fusion(f32[12,576,576]{1,2,0:T(8,128)} %get-tuple-element.84, f32[12,576]{1,0:T(8,128)S(1)} %get-tuple-element.83), kind=kLoop, calls=%fused_computation.8 | loop fusion | flops 7955712 | bytes 15980544 | tf_op jit(solution)/shard_map/while/body/eval_jaxpr/reduce_sum | solution.py:72
  100.0 10.3 %fusion.81 = bf16[12,64,576]{2,1,0:T(8,128)(2,1)} fusion(bf16[576,12,64]{0,2,1:T(8,128)(2,1)S(1)} %bitcast.102, f32[12,576,576]{1,2,0:T(8,128)} %get-tuple-element.84, f32[12,576]{1,0:T(8,128)S(1)} %fusion, f32[12,576]{1,0:T(8,128)S(1)} %get-tuple-element.83), kind=kOutput, calls=%fused_computation.121 | convolution fusion | flops 521994240 | bytes 17750016 | tf_op jit(solution)/shard_map/while/body/eval_jaxpr/hqk,khc->qhc/dot_general | solution.py:74
  110.3 19.1 %all-gather.6.cloned.1.call-done = bf16[768,768]{1,0:T(8,128)(2,1)} async-done(((bf16[24,768]{1,0:T(8,128)(2,1)}), bf16[768,768]{1,0:T(8,128)(2,1)}) %all-gather.6.cloned.1.call-update) | async-done | bytes 1179664 | tf_op jit(solution)/shard_map/all_gather | solution.py:155
  129.4 2.6 fusion.142
  132.7 3.5 convolution_convert_fusion.1
  136.2 5.1 all-to-all-start
  141.4 43.8 %all-to-all-done = bf16[8,152,768]{2,1,0:T(8,128)(2,1)} async-done(((bf16[8,152,768]{2,1,0:T(8,128)(2,1)}), bf16[8,152,768]{2,1,0:T(8,128)(2,1)}, u32[]{:S(2)}, u32[]{:S(2)}) %all-to-all-start) | async-done | bytes 1867808 | tf_op jit(solution)/shard_map/all_to_all | solution.py:183
  185.1 12.7 %fusion.30 = (u8[152,3072]{1,0:T(8,128)(4,1)S(1)}, u8[152,3072]{1,0:T(8,128)(4,1)S(1)}, f32[8,152,3072]{2,1,0:T(8,128)S(1)}) fusion(f32[3072]{0:T(1024)S(1)} %bitcast.113, bf16[8,152,768]{2,1,0:T(8,128)(2,1)} %all-to-all-done, bf16[1,768,3072]{2,1,0:T(8,128)(2,1)} %param.25), kind=kOutput, calls=%fused_computation.54 | convolution fusion | flops 5789171712 | bytes 22474752 | tf_op jit(solution)/shard_map/scd,df->scf/dot_general | solution.py:184
  197.9 34.1 %fusion.3 = bf16[8,152,3072]{2,1,0:T(8,128)(2,1)S(1)} fusion(f32[8,152,3072]{2,1,0:T(8,128)S(1)} %get-tuple-element.87, f32[3072]{0:T(1024)S(1)} %bitcast.114, u8[152,3072]{1,0:T(8,128)(4,1)S(1)} %get-tuple-element.47, u8[152,3072]{1,0:T(8,128)(4,1)S(1)} %get-tuple-element.46), kind=kLoop, calls=%fused_computation.11 | loop fusion | flops 265224192 | bytes 23359488 | tf_op jit(solution)/shard_map/convert_element_type | solution.py:187
  232.0 3.1 copy-done.10
  235.1 9.4 %add_convert_fusion = bf16[8,152,768]{2,1,0:T(8,128)(2,1)} fusion(f32[768]{0:T(1024)S(1)} %convert_reduce_fusion.2, bf16[8,152,3072]{2,1,0:T(8,128)(2,1)S(1)} %fusion.3, bf16[1,3072,768]{2,1,0:T(8,128)(2,1)} %param.27), kind=kOutput, calls=%fused_computation.52 | convolution fusion | flops 5739675648 | bytes 14060544 | tf_op jit(solution)/shard_map/scf,fd->scd/dot_general | solution.py:188
  244.5 4.4 all-to-all-start.1
  249.0 65.3 %all-gather = bf16[32,24,8]{1,2,0:T(8,128)(2,1)S(1)} all-gather(bf16[1,24,8]{1,2,0:T(8,128)(2,1)S(1)} %bitcast.116), channel_id=1, replica_groups=mesh['exp'=8,'rep'=4] {'exp','rep'}, dimensions={0}, use_global_device_ids=true | all-gather | bytes 12672 | tf_op jit(solution)/shard_map/all_gather | solution.py:158
  314.9 3.1 fusion.40
  318.0 5.0 fusion.68
  323.1 2.1 fusion.33
  325.2 2.2 fusion.31
  327.5 50.3 %all_to_all.20 = bf16[8,152,768]{2,1,0:T(8,128)(2,1)S(1)} all-to-all(bf16[8,152,768]{2,1,0:T(8,128)(2,1)S(1)} %bitcast.106), channel_id=1, replica_groups=mesh['exp'=8,'rep'=4] {'exp'}, dimensions={0} | all-to-all | bytes 3735552 | tf_op jit(solution)/shard_map/all_to_all | solution.py:209
  377.9 12.3 %fusion.144 = (bf16[3072]{0:T(1024)(128)(2,1)}, bf16[8,152,3072]{2,1,0:T(8,128)(2,1)}) fusion(f32[8,152,3072]{2,1,0:T(8,128)S(1)} %bitcast.94, f32[3072]{0:T(1024)S(1)} %bitcast.115, bf16[8,152,768]{2,1,0:T(8,128)(2,1)S(1)} %all_to_all.20, bf16[1,3072,768]{2,1,0:T(8,128)(2,1)S(1)} %bitcast.119), kind=kOutput, calls=%fused_computation.194 | convolution fusion | flops 5782631424 | bytes 29018112 | tf_op jit(solution)/shard_map/scd,fd->scf/dot_general | solution.py:224
  390.2 10.7 %fusion.55 = bf16[8,152,768]{2,1,0:T(8,128)(2,1)} fusion(bf16[8,152,3072]{2,1,0:T(8,128)(2,1)} %get-tuple-element.96, bf16[1,768,3072]{2,1,0:T(8,128)(2,1)} %param.25), kind=kOutput, calls=%fused_computation.87 | convolution fusion | flops 5738741760 | bytes 14057472 | tf_op jit(solution)/shard_map/scf,df->scd/dot_general | solution.py:238
  400.9 4.3 all-to-all-start.3
  405.5 10.7 %fusion.28 = bf16[1,3072,768]{2,1,0:T(8,128)(2,1)} fusion(bf16[8,152,3072]{2,1,0:T(8,128)(2,1)} %copy-done.10, bf16[8,152,768]{2,1,0:T(8,128)(2,1)} %copy-done.11), kind=kOutput, calls=%fused_computation.50 | convolution fusion | flops 5740167168 | bytes 14057472 | tf_op jit(solution)/shard_map/scf,scd->fd/dot_general | solution.py:220
  416.2 10.6 %fusion.27 = bf16[1,768,3072]{2,1,0:T(8,128)(2,1)} fusion(bf16[8,152,768]{2,1,0:T(8,128)(2,1)} %all-to-all-done, bf16[8,152,3072]{2,1,0:T(8,128)(2,1)} %get-tuple-element.96), kind=kOutput, calls=%fused_computation.49 | convolution fusion | flops 5740167168 | bytes 14057472 | tf_op jit(solution)/shard_map/scd,scf->df/dot_general | solution.py:228
  427.5 20.3 %all-to-all-done.3 = bf16[8,152,768]{2,1,0:T(8,128)(2,1)} async-done(((bf16[8,152,768]{2,1,0:T(8,128)(2,1)}), bf16[8,152,768]{2,1,0:T(8,128)(2,1)}, u32[]{:S(2)}, u32[]{:S(2)}) %all-to-all-start.3) | async-done | bytes 1867808 | tf_op jit(solution)/shard_map/all_to_all | solution.py:241
  447.7 3.6 fusion.85
  451.4 1.6 multiply_reduce_fusion.1
  453.7 2.8 convert_add_fusion
  456.4 1.8 convolution_convert_fusion.2
  458.3 1.5 copy.65
  459.8 3.7 fusion.113
  464.1 12.5 %multiply_reduce_fusion = (f32[12,576]{1,0:T(8,128)S(1)}, f32[12,576,576]{1,2,0:T(8,128)}) fusion(f32[12,576,576]{1,2,0:T(8,128)} %get-tuple-element.84, f32[12,576]{1,0:T(8,128)S(1)} %copy-done.22, bf16[576,12,64]{0,2,1:T(8,128)(2,1)S(1)} %bitcast.97, bf16[576,12,64]{0,2,1:T(8,128)(2,1)} %bitcast.101), kind=kOutput, calls=%fused_computation.3 | convolution fusion | flops 521544960 | bytes 33675264 | tf_op jit(solution)/shard_map/while/body/eval_jaxpr/qhc,khc->hqk/dot_general | solution.py:82
  476.6 12.7 %multiply_convert_fusion = bf16[12,576,576]{1,2,0:T(8,128)(2,1)S(1)} fusion(f32[12,576,576]{1,2,0:T(8,128)} %get-tuple-element.93, f32[12,576,576]{1,2,0:T(8,128)} %get-tuple-element.84, f32[12,576]{1,0:T(8,128)S(1)} %get-tuple-element.92, f32[12,576]{1,0:T(8,128)S(1)} %copy-done.22), kind=kLoop, calls=%fused_computation.2 | loop fusion | flops 15925248 | bytes 39868416 | tf_op jit(solution)/shard_map/while/body/eval_jaxpr/convert_element_type | solution.py:88
  489.3 2.7 multiply_convert_fusion.1
  492.0 1.7 multiply_convert_fusion.2
  493.8 9.2 %fusion.82 = bf16[12,64,576]{2,1,0:T(8,128)(2,1)S(1)} fusion(bf16[576,12,64]{0,2,1:T(8,128)(2,1)S(1)} %bitcast.98, f32[12,576,576]{1,2,0:T(8,128)} %get-tuple-element.84, f32[12,576]{1,0:T(8,128)S(1)} %copy-done.22), kind=kOutput, calls=%fused_computation.122 | convolution fusion | flops 518012928 | bytes 17722368 | tf_op jit(solution)/shard_map/while/body/eval_jaxpr/hqk,qhc->khc/dot_general | solution.py:83
  503.1 0.9 copy-done.18
  504.0 6.3 fusion.88
  510.4 1.1 copy-done.6
  511.5 0.8 fusion.145
  512.3 1.8 reduce_sum.267
  514.9 11.2 %all-reduce.11 = (bf16[1,3072]{1,0:T(2,128)(2,1)S(1)}, bf16[1,768]{1,0:T(2,128)(2,1)S(1)}) all-reduce(bf16[1,3072]{1,0:T(2,128)(2,1)S(1)} %broadcast_in_dim.62, bf16[1,768]{1,0:T(2,128)(2,1)S(1)} %broadcast_in_dim.66), channel_id=1, replica_groups=mesh['exp'=8,'rep'=4] {'rep'}, use_global_device_ids=true, to_apply=%region_36.37 | all-reduce | flops 3840 | bytes 15360 | tf_op jit(solution)/shard_map/psum | solution.py:234
  527.3 6.9 fusion.64
  534.3 39.1 %all-reduce.9 = (f32[768]{0:T(1024)S(1)}, f32[768]{0:T(1024)S(1)}, f32[768]{0:T(1024)S(1)}, f32[768]{0:T(1024)S(1)}, f32[768,8]{0,1:T(8,128)S(1)}) all-reduce(f32[768]{0:T(1024)S(1)} %get-tuple-element.50, f32[768]{0:T(1024)S(1)} %get-tuple-element.55, f32[768]{0:T(1024)S(1)} %copy-done.32, ...), channel_id=2, replica_groups=mesh['exp'=8,'rep'=4] {'exp','rep'}, use_global_device_ids=true, to_apply=%region_24.25.clone | all-reduce | flops 9216 | bytes 73728
  576.4 3.3 fusion.63
  579.7 19.2 %all-reduce.15.cloned.1.call-done = (bf16[1,768,3072]{2,1,0:T(8,128)(2,1)}, bf16[1,3072,768]{2,1,0:T(8,128)(2,1)}) async-done(((bf16[1,768,3072]{2,1,0:T(8,128)(2,1)}, bf16[1,3072,768]{2,1,0:T(8,128)(2,1)}), (bf16[1,768,3072]{2,1,0:T(8,128)(2,1)}, bf16[1,3072,768]{2,1,0:T(8,128)(2,1)})) %all-reduce.15.cloned.1.call-update) | async-done | bytes 9437200 | tf_op jit(solution)/shard_map/psum | solution.py:233
  598.8 7.5 broadcast_in_dim.61
  606.4 4.5 broadcast_in_dim.65
  610.8 93.4 %reduce-scatter.6.cloned.1.call-done = f32[24,768]{1,0:T(8,128)} async-done(((f32[768,768]{1,0:T(8,128)}), f32[24,768]{1,0:T(8,128)}) %reduce-scatter.6.cloned.1.call-update) | async-done | bytes 73744 | tf_op jit(solution)/shard_map/reduce_scatter | solution.py:298
  704.2 124.8 %reduce-scatter.4.cloned.1.call-done = f32[24,2304]{1,0:T(8,128)} async-done(((f32[768,2304]{1,0:T(8,128)}), f32[24,2304]{1,0:T(8,128)}) %reduce-scatter.4.cloned.1.call-update) | async-done | bytes 221200 | tf_op jit(solution)/shard_map/reduce_scatter | solution.py:297
  (162 shorter events, 15.7 us)
Async XLA Ops:
  7.2 66.5 %all-gather.4.cloned.1.call-start = ((), (), s32[]{:S(2)}) async-start(), calls=%async_computation.6 | async-start | bytes 3649536 | tf_op jit(solution)/shard_map/all_gather | solution.py:154
  7.9 121.5 %all-gather.6.cloned.1.call-start = ((), (), s32[]{:S(2)}) async-start(), calls=%async_computation.7 | async-start | bytes 1216512 | tf_op jit(solution)/shard_map/all_gather | solution.py:155
  57.7 20.7 %copy-start.41 = (f32[768]{0:T(1024)}, f32[768]{0:T(1024)S(1)}, u32[]{:S(2)}) copy-start(f32[768]{0:T(1024)S(1)} %convert_element_type.191) | copy-start | bytes 9220
  58.6 19.8 %copy-start.34 = (f32[768]{0:T(1024)}, f32[768]{0:T(1024)S(1)}, u32[]{:S(2)}) copy-start(f32[768]{0:T(1024)S(1)} %convert_element_type.190) | copy-start | bytes 9220
  58.6 392.7 %copy-start.24 = (f32[768]{0:T(1024)}, f32[768]{0:T(1024)S(1)}, u32[]{:S(2)}) copy-start(f32[768]{0:T(1024)S(1)} %convert_element_type.199) | copy-start | bytes 9220
  60.0 18.4 %copy-start.26 = (f32[576]{0:T(1024)}, f32[576]{0:T(1024)S(1)}, u32[]{:S(2)}) copy-start(f32[576]{0:T(1024)S(1)} %broadcast_multiply_fusion.5) | copy-start | bytes 6916
  61.6 16.8 %copy-start.37 = (f32[576]{0:T(1024)}, f32[576]{0:T(1024)S(1)}, u32[]{:S(2)}) copy-start(f32[576]{0:T(1024)S(1)} %add_rsqrt_fusion.1) | copy-start | bytes 6916
  80.1 11.2 %copy-start.1 = (bf16[576,768]{0,1:T(8,128)(2,1)}, bf16[576,768]{0,1:T(8,128)(2,1)S(1)}, u32[]{:S(2)}) copy-start(bf16[576,768]{0,1:T(8,128)(2,1)S(1)} %copy.62) | copy-start | bytes 2654212
  82.0 9.4 %copy-start.3 = (bf16[576,768]{0,1:T(8,128)(2,1)}, bf16[576,768]{0,1:T(8,128)(2,1)S(1)}, u32[]{:S(2)}) copy-start(bf16[576,768]{0,1:T(8,128)(2,1)S(1)} %copy.61) | copy-start | bytes 2654212
  91.4 8.6 %copy-start.13 = (bf16[576,768]{0,1:T(8,128)(2,1)S(1)}, bf16[576,768]{0,1:T(8,128)(2,1)}, u32[]{:S(2)}) copy-start(bf16[576,768]{0,1:T(8,128)(2,1)} %copy.60) | copy-start | bytes 2654212
  100.0 29.4 %copy-start.7 = (bf16[576,768]{1,0:T(8,128)(2,1)S(1)}, bf16[576,768]{1,0:T(8,128)(2,1)}, u32[]{:S(2)}) copy-start(bf16[576,768]{1,0:T(8,128)(2,1)} %param.17) | copy-start | bytes 2654212
  132.3 319.0 %copy-start.25 = (f32[576]{0:T(1024)}, f32[576]{0:T(1024)S(1)}, u32[]{:S(2)}) copy-start(f32[576]{0:T(1024)S(1)} %add_rsqrt_fusion) | copy-start | bytes 6916
  132.6 181.8 %copy-start.5 = (bf16[576,768]{1,0:T(8,128)(2,1)}, bf16[576,768]{1,0:T(8,128)(2,1)S(1)}, u32[]{:S(2)}) copy-start(bf16[576,768]{1,0:T(8,128)(2,1)S(1)} %add_convert_fusion.2) | copy-start | bytes 2654212
  136.2 5.1 copy-start.40
  136.2 5.2 copy-start.43
  136.2 49.0 %all-to-all-start = ((bf16[8,152,768]{2,1,0:T(8,128)(2,1)}), bf16[8,152,768]{2,1,0:T(8,128)(2,1)}, u32[]{:S(2)}, u32[]{:S(2)}) async-start(bf16[8,152,768]{2,1,0:T(8,128)(2,1)} %bitcast.105), calls=%async_computation | async-start | bytes 3735552 | tf_op jit(solution)/shard_map/all_to_all | solution.py:183
  197.9 34.2 %copy-start = (f32[8,152,3072]{2,1,0:T(8,128)}, f32[8,152,3072]{2,1,0:T(8,128)S(1)}, u32[]{:S(2)}) copy-start(f32[8,152,3072]{2,1,0:T(8,128)S(1)} %get-tuple-element.87) | copy-start | bytes 44826628
  232.0 3.1 copy-start.10
  244.5 4.5 copy-start.44
  244.5 70.3 %all-to-all-start.1 = ((bf16[8,152,768]{2,1,0:T(8,128)(2,1)}), bf16[8,152,768]{2,1,0:T(8,128)(2,1)}, u32[]{:S(2)}, u32[]{:S(2)}) async-start(bf16[8,152,768]{2,1,0:T(8,128)(2,1)} %add_convert_fusion), calls=%async_computation.1 | async-start | bytes 3735552 | tf_op jit(solution)/shard_map/all_to_all | solution.py:191
  314.9 3.1 copy-start.20
  318.0 5.0 copy-start.15
  318.0 59.8 %slice-start = ((s8[14942208]{0:T(1024)(128)(4,1)}), s8[4194304]{0:T(1024)(128)(4,1)S(1)}, s32[]{:S(2)}) async-start(s8[14942208]{0:T(1024)(128)(4,1)} %bitcast.93), calls=%async_computation.11 | async-start | bytes 8388608
  318.0 59.8 %slice-start.1 = ((s8[14942208]{0:T(1024)(128)(4,1)}), s8[4194304]{0:T(1024)(128)(4,1)S(1)}, s32[]{:S(2)}) async-start(s8[14942208]{0:T(1024)(128)(4,1)} %bitcast.93), calls=%async_computation.12 | async-start | bytes 8388608
  323.0 2.2 copy-start.28
  323.0 2.2 copy-start.30
  323.1 54.7 %slice-start.2 = ((s8[14942208]{0:T(1024)(128)(4,1)}), s8[4194304]{0:T(1024)(128)(4,1)S(1)}, s32[]{:S(2)}) async-start(s8[14942208]{0:T(1024)(128)(4,1)} %bitcast.93), calls=%async_computation.13 | async-start | bytes 8388608
  323.1 54.7 %slice-start.4 = ((s8[4718592]{0:T(1024)(128)(4,1)}), s8[4194304]{0:T(1024)(128)(4,1)S(1)}, s32[]{:S(2)}) async-start(s8[4718592]{0:T(1024)(128)(4,1)} %bitcast.118), calls=%async_computation.15 | async-start | bytes 8388608
  325.2 52.6 %slice-start.3 = ((s8[14942208]{0:T(1024)(128)(4,1)}), s8[2359296]{0:T(1024)(128)(4,1)S(1)}, s32[]{:S(2)}) async-start(s8[14942208]{0:T(1024)(128)(4,1)} %bitcast.93), calls=%async_computation.14 | async-start | bytes 4718592
  325.2 52.6 %slice-start.5 = ((s8[4718592]{0:T(1024)(128)(4,1)}), s8[524288]{0:T(1024)(128)(4,1)S(1)}, s32[]{:S(2)}) async-start(s8[4718592]{0:T(1024)(128)(4,1)} %bitcast.118), calls=%async_computation.16 | async-start | bytes 1048576
  377.8 12.3 %copy-start.11 = (bf16[8,152,768]{2,1,0:T(8,128)(2,1)}, bf16[8,152,768]{2,1,0:T(8,128)(2,1)S(1)}, u32[]{:S(2)}) copy-start(bf16[8,152,768]{2,1,0:T(8,128)(2,1)S(1)} %all_to_all.20) | copy-start | bytes 5603332
  400.9 46.9 %all-to-all-start.3 = ((bf16[8,152,768]{2,1,0:T(8,128)(2,1)}), bf16[8,152,768]{2,1,0:T(8,128)(2,1)}, u32[]{:S(2)}, u32[]{:S(2)}) async-start(bf16[8,152,768]{2,1,0:T(8,128)(2,1)} %fusion.55), calls=%async_computation.3 | async-start | bytes 3735552 | tf_op jit(solution)/shard_map/all_to_all | solution.py:241
  405.2 193.6 %all-reduce.15.cloned.1.call-start = ((), (), s32[]{:S(2)}) async-start(), calls=%async_computation.10 | async-start | bytes 18874368 | tf_op jit(solution)/shard_map/psum | solution.py:233
  426.8 277.5 %reduce-scatter.6.cloned.1.call-start = ((), (), s32[]{:S(2)}) async-start(), calls=%async_computation.9 | async-start | bytes 2433024 | tf_op jit(solution)/shard_map/reduce_scatter | solution.py:298
  451.3 1.7 copy-start.16
  451.3 2.1 copy-start.17
  451.3 2.3 copy-start.21
  451.4 2.3 copy-start.29
  451.4 2.3 copy-start.31
  453.7 2.8 copy-start.45
  459.8 4.2 copy-start.22
  463.6 365.4 %reduce-scatter.4.cloned.1.call-start = ((), (), s32[]{:S(2)}) async-start(), calls=%async_computation.8 | async-start | bytes 7299072 | tf_op jit(solution)/shard_map/reduce_scatter | solution.py:297
  476.6 12.7 %copy-start.4 = (bf16[576,768]{0,1:T(8,128)(2,1)S(1)}, bf16[576,768]{0,1:T(8,128)(2,1)}, u32[]{:S(2)}) copy-start(bf16[576,768]{0,1:T(8,128)(2,1)} %copy-done.3) | copy-start | bytes 2654212
  489.3 2.7 copy-start.2
  492.0 11.0 %copy-start.19 = (bf16[12,64,576]{2,1,0:T(8,128)(2,1)}, bf16[12,64,576]{2,1,0:T(8,128)(2,1)S(1)}, u32[]{:S(2)}) copy-start(bf16[12,64,576]{2,1,0:T(8,128)(2,1)S(1)} %multiply_convert_fusion.1) | copy-start | bytes 2654212
  493.7 9.3 %copy-start.14 = (bf16[12,64,576]{2,1,0:T(8,128)(2,1)}, bf16[12,64,576]{2,1,0:T(8,128)(2,1)S(1)}, u32[]{:S(2)}) copy-start(bf16[12,64,576]{2,1,0:T(8,128)(2,1)S(1)} %multiply_convert_fusion.2) | copy-start | bytes 2654212
  493.7 10.3 %copy-start.8 = (bf16[576,768]{1,0:T(8,128)(2,1)S(1)}, bf16[576,768]{1,0:T(8,128)(2,1)}, u32[]{:S(2)}) copy-start(bf16[576,768]{1,0:T(8,128)(2,1)} %param.17) | copy-start | bytes 2654212
  493.7 10.2 %copy-start.27 = (f32[576]{0:T(1024)S(1)}, f32[576]{0:T(1024)}, u32[]{:S(2)}) copy-start(f32[576]{0:T(1024)} %copy-done.26) | copy-start | bytes 6916
  493.8 10.2 %copy-start.35 = (f32[768]{0:T(1024)S(1)}, f32[768]{0:T(1024)}, u32[]{:S(2)}) copy-start(f32[768]{0:T(1024)} %copy-done.34) | copy-start | bytes 9220
  493.8 10.2 %copy-start.38 = (f32[576]{0:T(1024)S(1)}, f32[576]{0:T(1024)}, u32[]{:S(2)}) copy-start(f32[576]{0:T(1024)} %copy-done.37) | copy-start | bytes 6916
  493.8 10.2 %copy-start.42 = (f32[768]{0:T(1024)S(1)}, f32[768]{0:T(1024)}, u32[]{:S(2)}) copy-start(f32[768]{0:T(1024)} %copy-done.41) | copy-start | bytes 9220
  503.0 0.9 copy-start.18
  510.3 1.2 copy-start.6
  510.3 17.0 %copy-start.9 = (bf16[576,768]{1,0:T(8,128)(2,1)S(1)}, bf16[576,768]{1,0:T(8,128)(2,1)}, u32[]{:S(2)}) copy-start(bf16[576,768]{1,0:T(8,128)(2,1)} %param.17) | copy-start | bytes 2654212
  527.3 7.0 copy-start.23
  527.3 7.0 copy-start.32
  527.3 7.0 copy-start.33
  527.3 49.1 %copy-start.36 = (f32[768]{0:T(1024)S(1)}, f32[768]{0:T(1024)}, u32[]{:S(2)}) copy-start(f32[768]{0:T(1024)} %copy-done.34) | copy-start | bytes 9220
  527.3 49.1 %copy-start.39 = (f32[576]{0:T(1024)S(1)}, f32[576]{0:T(1024)}, u32[]{:S(2)}) copy-start(f32[576]{0:T(1024)} %copy-done.37) | copy-start | bytes 6916
  598.8 7.5 copy-start.12
Sparse Core Ops, SparseCore 0:
  10.9 62.7 all-gather.3
  76.6 52.7 all-gather.5
  426.9 171.9 all-reduce.14
  604.6 99.6 reduce-scatter.5
  710.3 118.6 reduce-scatter.3
where the time goes:
time: 843 us; the launch traced here: 836 us
  waiting for transfers between devices  331 us (39%)
  blocking collectives  208 us (25%)
  matrix products  162 us (19%)
  other arithmetic  85.2 us (10%)
  local copies, waits for them, and re-layouts  20.4 us (2%)
  between operations  14.8 us (2%)
  starting transfers between devices  14.7 us (2%)
    reduce_scatter x1, waiting for transfers between devices, on_device(): lax.psum_scatter(grad_qkv_weight, ('exp', 'rep'), scatter_dimension=0, ti...  125 us
    reduce_scatter x1, waiting for transfers between devices, on_device(): lax.psum_scatter(grad_out_weight, ('exp', 'rep'), scatter_dimension=0, ti...  93.4 us
    unnamed x2, blocking collectives  81.3 us
    all_gather x1, blocking collectives, on_device(): lax.all_gather(w_router, ('exp', 'rep'), axis=0, tiled=True)  65.3 us
    all_to_all x1, blocking collectives, on_device(): lax.all_to_all(grad_slots.astype(jnp.bfloat16).reshape(experts, capacity,...  50.3 us
    all_to_all x1, waiting for transfers between devices, on_device(): lax.all_to_all(buffer, 'exp', split_axis=0, concat_axis=0, tiled=True)  43.8 us
    convert_element_type x1, other arithmetic, on_device(): active_part = jax.nn.gelu(pre_part, approximate=False).astype(jnp.bfloat16)  34.1 us
    all_to_all x1, waiting for transfers between devices, on_device(): lax.all_to_all(grad_received, 'exp', split_axis=0, concat_axis=0, tiled=T...  20.3 us
  transfers between devices with their start and end apart: 8, of which 7 were waited for; matrix products, arithmetic and copies ran while one was open for 19% of the time, Pallas kernels for 0%

commit v1 on v0

--- a/solution.py
+++ b/solution.py
@@ -1,6 +1,10 @@
+import functools
+
 import jax
 import jax.numpy as jnp
 from jax import lax
+from jax.experimental import pallas as pl
+from jax.experimental.pallas import tpu as pltpu
 from jax.sharding import PartitionSpec as P
 
 D = 768
@@ -125,6 +129,298 @@
         jnp.bfloat16
     )
     return (first_hot.astype(jnp.float32), second_hot.astype(jnp.float32), pick_first, pick_second)
+
+
+LANES = 128
+MESH_ID = pl.DeviceIdType.MESH
+
+
+def bit_count(number):
+    return number.bit_length() - 1
+
+
+def flip(position, bit):
+    step = 1 << bit
+    return position + (1 - 2 * lax.rem(lax.div(position, step), 2)) * step
+
+
+def coordinates(position, reps):
+    return (lax.div(position, reps), lax.rem(position, reps))
+
+
+def greet(bits, me, reps):
+    barrier = pltpu.get_barrier_semaphore()
+    for bit in range(bits):
+        pl.semaphore_signal(
+            barrier, inc=1, device_id=coordinates(flip(me, bit), reps), device_id_type=MESH_ID
+        )
+    pl.semaphore_wait(barrier, bits)
+
+
+def lowest_bit(number):
+    return (number & -number).bit_length() - 1
+
+
+def gather_kernel(devices, reps, own_ref, all_ref, send_sem, recv_sem, local_sem):
+    bits = bit_count(devices)
+    me = lax.axis_index("exp") * reps + lax.axis_index("rep")
+    greet(bits, me, reps)
+    local = pltpu.make_async_copy(own_ref, all_ref.at[me], local_sem)
+    local.start()
+
+    def owner_of(distance):
+        found = me
+        for bit in range(bits):
+            if distance >> bit & 1:
+                found = flip(found, bit)
+        return found
+
+    def transfer(source_ref, distance, bit):
+        owner = owner_of(distance)
+        index = distance + (1 << bit)
+        return pltpu.make_async_remote_copy(
+            src_ref=source_ref,
+            dst_ref=all_ref.at[owner],
+            send_sem=send_sem.at[index],
+            recv_sem=recv_sem.at[index],
+            device_id=coordinates(flip(me, bit), reps),
+            device_id_type=MESH_ID,
+        )
+
+    def arrival(distance):
+        owner = owner_of(distance)
+        return pltpu.make_async_remote_copy(
+            src_ref=all_ref.at[owner],
+            dst_ref=all_ref.at[owner],
+            send_sem=send_sem.at[distance],
+            recv_sem=recv_sem.at[distance],
+            device_id=coordinates(flip(me, lowest_bit(distance)), reps),
+            device_id_type=MESH_ID,
+        )
+
+    sent = []
+    for bit in range(bits):
+        copy = transfer(own_ref, 0, bit)
+        copy.start()
+        sent.append(copy)
+    order = sorted(range(1, devices), key=lambda d: (bin(d).count("1"), -d))
+    last = []
+    for distance in order:
+        low = lowest_bit(distance)
+        if low == 0:
+            last.append(distance)
+            continue
+        arrival(distance).wait_recv()
+        for bit in range(low):
+            copy = transfer(all_ref.at[owner_of(distance)], distance, bit)
+            copy.start()
+            sent.append(copy)
+    for distance in last:
+        arrival(distance).wait_recv()
+    for copy in sent:
+        copy.wait_send()
+    local.wait()
+
+
+def gather_blocks(block, devices, reps):
+    return pl.pallas_call(
+        functools.partial(gather_kernel, devices, reps),
+        out_shape=jax.ShapeDtypeStruct((devices,) + block.shape, block.dtype),
+        in_specs=[pl.BlockSpec(memory_space=pl.ANY)],
+        out_specs=pl.BlockSpec(memory_space=pl.ANY),
+        scratch_shapes=[
+            pltpu.SemaphoreType.DMA((devices,)),
+            pltpu.SemaphoreType.DMA((devices,)),
+            pltpu.SemaphoreType.DMA,
+        ],
+        compiler_params=pltpu.CompilerParams(collective_id=0, has_side_effects=True),
+        name="gather_dense",
+    )(block)
+
+
+def scatter_plan(devices, reps):
+    bits = bit_count(devices)
+    low = min(bit_count(reps) + 1, bits)
+    return (bits, low, list(range(low)) + list(range(bits - 1, low - 1, -1)))
+
+
+def reverse_bits(number, width):
+    return sum((number >> bit & 1) << (width - 1 - bit) for bit in range(width))
+
+
+def scatter_kernel(devices, reps, chunks, arrays, *refs):
+    bits, low, plan = scatter_plan(devices, reps)
+    ins, outs, refs = (refs[:arrays], refs[arrays : 2 * arrays], refs[2 * arrays :])
+    count = len(chunks)
+    owns, refs = (refs[:count], refs[count:])
+    recvs, refs = ([refs[c * bits : (c + 1) * bits] for c in range(count)], refs[count * bits :])
+    send_sem, recv_sem, local_sem = refs
+    me = lax.axis_index("exp") * reps + lax.axis_index("rep")
+    greet(bits, me, reps)
+    high = devices >> low
+    rows = owns[0].shape[1]
+    my_bit = [lax.rem(lax.div(me, 1 << bit), 2) for bit in range(bits)]
+    firsts = 1 << (low - 1)
+    stride = firsts + bits - 1
+
+    def first_copies(c):
+        array, start, width = chunks[c]
+        columns = pl.ds(start, width)
+        copies, local = ([], [])
+        for rest in range(firsts):
+            place = reverse_bits(rest, low - 1) * high
+            index = c * stride + rest
+            copies.append(
+                pltpu.make_async_remote_copy(
+                    src_ref=ins[array].at[:, 2 * rest + 1 - my_bit[0], :, columns],
+                    dst_ref=recvs[c][0].at[pl.ds(place, high)],
+                    send_sem=send_sem.at[index],
+                    recv_sem=recv_sem.at[index],
+                    device_id=coordinates(flip(me, plan[0]), reps),
+                    device_id_type=MESH_ID,
+                )
+            )
+            local.append(
+                pltpu.make_async_copy(
+                    ins[array].at[:, 2 * rest + my_bit[0], :, columns],
+                    owns[c].at[pl.ds(place, high)],
+                    local_sem.at[c * firsts + rest],
+                )
+            )
+        return (copies, local)
+
+    def later_copy(c, phase):
+        half = devices >> (phase + 1)
+        index = c * stride + firsts + phase - 1
+        return pltpu.make_async_remote_copy(
+            src_ref=recvs[c][phase - 1].at[pl.ds((1 - my_bit[plan[phase]]) * half, half)],
+            dst_ref=recvs[c][phase],
+            send_sem=send_sem.at[index],
+            recv_sem=recv_sem.at[index],
+            device_id=coordinates(flip(me, plan[phase]), reps),
+            device_id_type=MESH_ID,
+        )
+
+    started = [first_copies(c) for c in range(count)]
+    for copies, local in started:
+        for copy in copies + local:
+            copy.start()
+    current = [None] * count
+    sent = []
+
+    def absorb(c, phase):
+        half = devices >> (phase + 1)
+        if phase == 0:
+            for copy in started[c][0]:
+                copy.wait_recv()
+            for copy in started[c][1]:
+                copy.wait()
+            held, base = (owns[c], 0)
+        else:
+            current[c].wait_recv()
+            held, base = (recvs[c][phase - 1], my_bit[plan[phase]] * half)
+        into = recvs[c][phase]
+        if phase == bits - 1:
+            array, start, width = chunks[c]
+            outs[array][:, pl.ds(start, width)] = into[0].astype(jnp.float32) + held[base].astype(
+                jnp.float32
+            )
+            return
+
+        def one(i, carry):
+            total = into[i].astype(jnp.float32) + held[base + i].astype(jnp.float32)
+            into[i] = total.astype(into.dtype)
+            return carry
+
+        lax.fori_loop(0, half, one, 0)
+        copy = later_copy(c, phase + 1)
+        copy.start()
+        sent.append(copy)
+        current[c] = copy
+
+    for step in range(bits + count - 1):
+        for c in range(count):
+            phase = step - c
+            if 0 <= phase < bits:
+                absorb(c, phase)
+    for copies, local in started:
+        for copy in copies:
+            copy.wait_send()
+    for copy in sent:
+        copy.wait_send()
+
+
+def scatter_sums(parts, devices, reps):
+    bits, low, plan = scatter_plan(devices, reps)
+    high = devices >> low
+    rows = parts[0].shape[0] // devices
+    chunks = []
+    for array, part in enumerate(parts):
+        width = part.shape[1] if part.shape[1] < D else D
+        for start in range(0, part.shape[1], width):
+            chunks.append((array, start, width))
+    scratch = [pltpu.VMEM((devices // 2, rows, width), jnp.bfloat16) for _, _, width in chunks]
+    for _, _, width in chunks:
+        for phase in range(bits):
+            scratch.append(pltpu.VMEM((devices >> (phase + 1), rows, width), jnp.bfloat16))
+    firsts = 1 << (low - 1)
+    total = len(chunks) * (firsts + bits - 1)
+    return pl.pallas_call(
+        functools.partial(scatter_kernel, devices, reps, chunks, len(parts)),
+        out_shape=[jax.ShapeDtypeStruct((rows, part.shape[1]), jnp.float32) for part in parts],
+        in_specs=[pl.BlockSpec(memory_space=pl.ANY)] * len(parts),
+        out_specs=[pl.BlockSpec(memory_space=pltpu.VMEM)] * len(parts),
+        scratch_shapes=scratch
+        + [
+            pltpu.SemaphoreType.DMA((total,)),
+            pltpu.SemaphoreType.DMA((total,)),
+            pltpu.SemaphoreType.DMA((len(chunks) * firsts,)),
+        ],
+        compiler_params=pltpu.CompilerParams(
+            collective_id=1, has_side_effects=True, vmem_limit_bytes=60 * 1024 * 1024
+        ),
+        name="scatter_dense",
+    )(*[part.reshape(high, 1 << low, rows, part.shape[1]) for part in parts])
+
+
+def rep_pairs(reps, bit):
+    return [(source, source ^ (1 << bit)) for source in range(reps)]
+
+
+def rep_reduce(partial, reps):
+    mine = lax.axis_index("rep")
+    for bit in range(bit_count(reps)):
+        half = partial.shape[0] // 2
+        mine_bit = lax.rem(lax.div(mine, 1 << bit), 2)
+        away = lax.dynamic_slice_in_dim(partial, (1 - mine_bit) * half, half, 0)
+        kept = lax.dynamic_slice_in_dim(partial, mine_bit * half, half, 0)
+        arrived = lax.ppermute(away, "rep", rep_pairs(reps, bit))
+        partial = (kept.astype(jnp.float32) + arrived.astype(jnp.float32)).astype(jnp.bfloat16)
+    return partial
+
+
+def rep_spread(piece, reps):
+    mine = lax.axis_index("rep")
+    for bit in reversed(range(bit_count(reps))):
+        mine_bit = lax.rem(lax.div(mine, 1 << bit), 2)
+        arrived = lax.ppermute(piece, "rep", rep_pairs(reps, bit))
+        piece = jnp.where(
+            mine_bit == 0,
+            jnp.concatenate([piece, arrived], axis=0),
+            jnp.concatenate([arrived, piece], axis=0),
+        )
+    return piece
+
+
+def rep_total(small, reps):
+    for bit in range(bit_count(reps)):
+        arrived = lax.ppermute(small, "rep", rep_pairs(reps, bit))
+        small = small + arrived
+    return small
+
+
+def exchange(blocks):
+    return lax.all_to_all(blocks, "exp", split_axis=0, concat_axis=0, tiled=True)
 
 
 def on_device(
@@ -147,17 +443,32 @@
     cotangent,
 ):
     experts = lax.axis_size("exp")
+    reps = lax.axis_size("rep")
+    devices = experts * reps
     capacity = (TOK_DEV * 210 + experts * 100 - 1) // (experts * 100)
-    dense = (
-        lax.all_gather(ln1_gain, ("exp", "rep"), axis=0, tiled=True),
-        lax.all_gather(ln1_bias, ("exp", "rep"), axis=0, tiled=True),
-        lax.all_gather(w_qkv, ("exp", "rep"), axis=0, tiled=True),
-        lax.all_gather(w_out, ("exp", "rep"), axis=0, tiled=True),
-        lax.all_gather(ln2_gain, ("exp", "rep"), axis=0, tiled=True),
-        lax.all_gather(ln2_bias, ("exp", "rep"), axis=0, tiled=True),
-        lax.all_gather(w_router, ("exp", "rep"), axis=0, tiled=True),
-    )
-    gain_one, bias_one, qkv_weight, out_weight, gain_two, bias_two, router_weight = dense
+    rows = w_qkv.shape[0]
+    small = jnp.concatenate(
+        [w_router, jnp.stack([ln1_gain, ln1_bias, ln2_gain, ln2_bias], axis=1)], axis=1
+    )
+    small = jnp.pad(small, ((0, 0), (0, LANES - small.shape[1])))
+    packed = jnp.concatenate([w_qkv, w_out, small], axis=1)
+    gathered = gather_blocks(packed, devices, reps).reshape(D, packed.shape[1])
+    qkv_weight = gathered[:, : 3 * D]
+    out_weight = gathered[:, 3 * D : 4 * D]
+    router_weight = gathered[:, 4 * D : 4 * D + experts]
+    vectors = gathered[:, 4 * D + experts : 4 * D + experts + 4].T
+    gain_one, bias_one, gain_two, bias_two = (vectors[0], vectors[1], vectors[2], vectors[3])
+
+    first_hot, second_hot, pick_first, pick_second = dispatch_tables(
+        routes, priority, padding, experts, capacity
+    )
+    picks = pick_first + pick_second
+    grad_blocks = lax.dot_general(picks, cotangent, contract_first, preferred_element_type=jnp.float32)
+    grad_blocks = grad_blocks.astype(jnp.bfloat16).reshape(experts, capacity, D)
+    grad_blocks, gathered_done = lax.optimization_barrier((grad_blocks, qkv_weight))
+    qkv_weight = gathered_done
+    grad_arrived = exchange(grad_blocks).reshape(experts * capacity, D)
+
     inputs = tokens.astype(jnp.float32)
     normed, normal_one, inverse_one = norm_forward(inputs, gain_one, bias_one)
     normed_low = normed.astype(jnp.bfloat16)
@@ -167,96 +478,71 @@
         .reshape(ROWS_DEV, SLOTS, 3 * D)
     )
     allowed = row_masks(lengths, padding)
-    mixed, lse = lax.map(lambda pair: attend_forward(pair[0], pair[1]), (qkv, allowed))
-    mixed_low = mixed.reshape(TOK_DEV, D).astype(jnp.bfloat16)
+    mixed, lse = attend_forward(qkv[0], allowed[0])
+    mixed_low = mixed.astype(jnp.bfloat16)
     resid = inputs + jnp.dot(mixed_low, out_weight, preferred_element_type=jnp.float32)
     routed_float, normal_two, inverse_two = norm_forward(resid, gain_two, bias_two)
     routed = routed_float.astype(jnp.bfloat16)
     logits = jnp.dot(routed, router_weight, preferred_element_type=jnp.float32)
     probs = jax.nn.softmax(logits, axis=-1)
-    first_hot, second_hot, pick_first, pick_second = dispatch_tables(
-        routes, priority, padding, experts, capacity
-    )
-    picks = pick_first + pick_second
+    gate_first = jnp.sum(probs * first_hot, axis=1)
+    gate_second = jnp.sum(probs * second_hot, axis=1)
     buffer = lax.dot_general(picks, routed, contract_first, preferred_element_type=jnp.float32)
     buffer = buffer.astype(jnp.bfloat16).reshape(experts, capacity, D)
-    received_part = lax.all_to_all(buffer, "exp", split_axis=0, concat_axis=0, tiled=True)
-    pre_part = jnp.einsum(
-        "scd,df->scf", received_part, w_in[0], preferred_element_type=jnp.float32
-    ) + b_in[0].astype(jnp.float32)
-    active_part = jax.nn.gelu(pre_part, approximate=False).astype(jnp.bfloat16)
-    result_part = jnp.einsum(
-        "scf,fd->scd", active_part, w_back[0], preferred_element_type=jnp.float32
-    ) + b_back[0].astype(jnp.float32)
-    returned = lax.all_to_all(
-        result_part.astype(jnp.bfloat16), "exp", split_axis=0, concat_axis=0, tiled=True
-    )
-    returned_flat = returned.reshape(experts * capacity, D)
-    picked_first = jnp.dot(pick_first, returned_flat, preferred_element_type=jnp.float32)
-    picked_second = jnp.dot(pick_second, returned_flat, preferred_element_type=jnp.float32)
-    gate_first = jnp.sum(probs * first_hot, axis=1)
-    gate_second = jnp.sum(probs * second_hot, axis=1)
-    output = resid + gate_first[:, None] * picked_first + gate_second[:, None] * picked_second
+    received = exchange(buffer).reshape(experts * capacity, D)
+    slot_gates = jnp.sum(
+        pick_first.astype(jnp.float32) * gate_first[:, None]
+        + pick_second.astype(jnp.float32) * gate_second[:, None],
+        axis=0,
+    )
+    gates = exchange(slot_gates.reshape(experts, capacity)).reshape(experts * capacity, 1)
+
+    first_weight, second_weight = (w_in[0], w_back[0])
+    pre = jnp.dot(received, first_weight, preferred_element_type=jnp.float32) + b_in[0].astype(
+        jnp.float32
+    )
+    active = jax.nn.gelu(pre, approximate=False).astype(jnp.bfloat16)
+    grad_results = (gates * grad_arrived.astype(jnp.float32)).astype(jnp.bfloat16)
+    grad_active = lax.dot_general(
+        grad_results, second_weight, contract_last, preferred_element_type=jnp.float32
+    )
+    grad_pre = (grad_active * gelu_slope(pre)).astype(jnp.bfloat16)
+    result = (
+        jnp.dot(active, second_weight, preferred_element_type=jnp.float32)
+        + b_back[0].astype(jnp.float32)
+    ).astype(jnp.bfloat16)
+    grad_received = lax.dot_general(
+        grad_pre, first_weight, contract_last, preferred_element_type=jnp.float32
+    ).astype(jnp.bfloat16)
+    slot_grad_gates = jnp.sum(grad_arrived.astype(jnp.float32) * result.astype(jnp.float32), axis=1)
+    grad_gate_slots = exchange(slot_grad_gates.reshape(experts, capacity)).reshape(
+        1, experts * capacity
+    )
+    grad_buffer = exchange(grad_received.reshape(experts, capacity, D)).reshape(
+        experts * capacity, D
+    )
+    returned = exchange(result.reshape(experts, capacity, D)).reshape(experts * capacity, D)
+
+    grad_w_back = lax.dot_general(
+        active, grad_results, contract_first, preferred_element_type=jnp.float32
+    ).astype(jnp.bfloat16)
+    grad_w_in = lax.dot_general(
+        received, grad_pre, contract_first, preferred_element_type=jnp.float32
+    ).astype(jnp.bfloat16)
+    grad_b_back = jnp.sum(grad_results.astype(jnp.float32), axis=0)
+    grad_b_in = jnp.sum(grad_pre.astype(jnp.float32), axis=0)
+    back_total = rep_spread(rep_reduce(grad_w_back, reps), reps).astype(jnp.float32)
+    in_total = rep_spread(rep_reduce(grad_w_in, reps), reps).astype(jnp.float32)
+    bias_total = rep_total(jnp.concatenate([grad_b_in, grad_b_back]).reshape(-1, LANES), reps)
+    bias_total = bias_total.reshape(-1)
+
     grad_out = cotangent.astype(jnp.float32)
-    gated_first = (gate_first[:, None] * grad_out).astype(jnp.bfloat16)
-    gated_second = (gate_second[:, None] * grad_out).astype(jnp.bfloat16)
-    grad_slots = lax.dot_general(
-        pick_first, gated_first, contract_first, preferred_element_type=jnp.float32
-    )
-    grad_slots = grad_slots + lax.dot_general(
-        pick_second, gated_second, contract_first, preferred_element_type=jnp.float32
-    )
-    grad_results = lax.all_to_all(
-        grad_slots.astype(jnp.bfloat16).reshape(experts, capacity, D),
-        "exp",
-        split_axis=0,
-        concat_axis=0,
-        tiled=True,
-    )
-    pre = jnp.einsum(
-        "scd,df->scf", received_part, w_in[0], preferred_element_type=jnp.float32
-    ) + b_in[0].astype(jnp.float32)
-    active = jax.nn.gelu(pre, approximate=False).astype(jnp.bfloat16)
-    grad_w_back = jnp.einsum(
-        "scf,scd->fd", active, grad_results, preferred_element_type=jnp.float32
-    )
-    grad_b_back = jnp.sum(grad_results.astype(jnp.float32), axis=(0, 1))
-    grad_active = jnp.einsum(
-        "scd,fd->scf", grad_results, w_back[0], preferred_element_type=jnp.float32
-    )
-    grad_pre = (grad_active * gelu_slope(pre)).astype(jnp.bfloat16)
-    grad_w_in = jnp.einsum(
-        "scd,scf->df", received_part, grad_pre, preferred_element_type=jnp.float32
-    )
-    grad_b_in = jnp.sum(grad_pre.astype(jnp.float32), axis=(0, 1))
-    expert_sums = (
-        lax.psum(grad_w_in.astype(jnp.bfloat16), "rep").astype(jnp.float32),
-        lax.psum(grad_b_in.astype(jnp.bfloat16), "rep").astype(jnp.float32),
-        lax.psum(grad_w_back.astype(jnp.bfloat16), "rep").astype(jnp.float32),
-        lax.psum(grad_b_back.astype(jnp.bfloat16), "rep").astype(jnp.float32),
-    )
-    grad_received = jnp.einsum(
-        "scf,df->scd", grad_pre, w_in[0], preferred_element_type=jnp.float32
-    ).astype(jnp.bfloat16)
-    grad_buffer = lax.all_to_all(
-        grad_received, "exp", split_axis=0, concat_axis=0, tiled=True
-    ).reshape(experts * capacity, D)
-    grad_gate_first = jnp.sum(grad_out * picked_first, axis=1)
-    grad_gate_second = jnp.sum(grad_out * picked_second, axis=1)
+    grad_gate_first = jnp.sum(pick_first.astype(jnp.float32) * grad_gate_slots, axis=1)
+    grad_gate_second = jnp.sum(pick_second.astype(jnp.float32) * grad_gate_slots, axis=1)
     grad_probs = grad_gate_first[:, None] * first_hot + grad_gate_second[:, None] * second_hot
     grad_logits = (
         probs * (grad_probs - jnp.sum(probs * grad_probs, axis=1, keepdims=True))
     ).astype(jnp.bfloat16)
-    dense_back = (
-        lax.all_gather(ln1_gain, ("exp", "rep"), axis=0, tiled=True),
-        lax.all_gather(ln1_bias, ("exp", "rep"), axis=0, tiled=True),
-        lax.all_gather(w_qkv, ("exp", "rep"), axis=0, tiled=True),
-        lax.all_gather(w_out, ("exp", "rep"), axis=0, tiled=True),
-        lax.all_gather(ln2_gain, ("exp", "rep"), axis=0, tiled=True),
-        lax.all_gather(ln2_bias, ("exp", "rep"), axis=0, tiled=True),
-        lax.all_gather(w_router, ("exp", "rep"), axis=0, tiled=True),
-    )
-    gain_one, bias_one, qkv_weight, out_weight, gain_two, bias_two, router_weight = dense_back
     grad_router = lax.dot_general(
         routed, grad_logits, contract_first, preferred_element_type=jnp.float32
     )
@@ -275,12 +561,8 @@
     grad_mixed = lax.dot_general(
         grad_attn, out_weight, contract_last, preferred_element_type=jnp.float32
     )
-    grad_mixed = grad_mixed.astype(jnp.bfloat16).reshape(ROWS_DEV, SLOTS, D)
-    grad_qkv = lax.map(
-        lambda group: attend_backward(group[0], group[1], group[2], group[3]),
-        (qkv, allowed, lse, grad_mixed),
-    )
-    grad_qkv = grad_qkv.reshape(TOK_DEV, 3 * D)
+    grad_mixed = grad_mixed.astype(jnp.bfloat16)
+    grad_qkv = attend_backward(qkv[0], allowed[0], lse, grad_mixed)
     grad_qkv_weight = lax.dot_general(
         normed_low, grad_qkv, contract_first, preferred_element_type=jnp.float32
     )
@@ -291,29 +573,44 @@
         grad_normed, normal_one, inverse_one, gain_one
     )
     grad_tokens = grad_resid + grad_norm_one
-    dense_grads = (
-        lax.psum_scatter(grad_gain_one, ("exp", "rep"), scatter_dimension=0, tiled=True),
-        lax.psum_scatter(grad_bias_one, ("exp", "rep"), scatter_dimension=0, tiled=True),
-        lax.psum_scatter(grad_qkv_weight, ("exp", "rep"), scatter_dimension=0, tiled=True),
-        lax.psum_scatter(grad_out_weight, ("exp", "rep"), scatter_dimension=0, tiled=True),
-        lax.psum_scatter(grad_gain_two, ("exp", "rep"), scatter_dimension=0, tiled=True),
-        lax.psum_scatter(grad_bias_two, ("exp", "rep"), scatter_dimension=0, tiled=True),
-        lax.psum_scatter(grad_router, ("exp", "rep"), scatter_dimension=0, tiled=True),
-    )
+
+    picked_first = jnp.dot(pick_first, returned, preferred_element_type=jnp.float32)
+    picked_second = jnp.dot(pick_second, returned, preferred_element_type=jnp.float32)
+    output = resid + gate_first[:, None] * picked_first + gate_second[:, None] * picked_second
+
+    grad_small = jnp.concatenate(
+        [
+            grad_router,
+            jnp.stack([grad_gain_one, grad_bias_one, grad_gain_two, grad_bias_two], axis=1),
+        ],
+        axis=1,
+    )
+    grad_small = jnp.pad(grad_small, ((0, 0), (0, LANES - grad_small.shape[1])))
+    sum_qkv, sum_out, sum_small = scatter_sums(
+        [
+            grad_qkv_weight.astype(jnp.bfloat16),
+            grad_out_weight.astype(jnp.bfloat16),
+            grad_small.astype(jnp.bfloat16),
+        ],
+        devices,
+        reps,
+    )
+    vector_sums = sum_small[:, experts : experts + 4]
+    hidden = b_in.shape[1]
     return (
         output.astype(jnp.bfloat16),
         grad_tokens,
-        dense_grads[0],
-        dense_grads[1],
-        dense_grads[2],
-        dense_grads[3],
-        dense_grads[4],
-        dense_grads[5],
-        dense_grads[6],
-        expert_sums[0][None],
-        expert_sums[1][None],
-        expert_sums[2][None],
-        expert_sums[3][None],
+        vector_sums[:, 0],
+        vector_sums[:, 1],
+        sum_qkv,
+        sum_out,
+        vector_sums[:, 2],
+        vector_sums[:, 3],
+        sum_small[:, :experts],
+        in_total[None],
+        bias_total[None, :hidden],
+        back_total[None],
+        bias_total[None, hidden:],
     )
 
 

time: 843 us -> 529 us (0.63)
  waiting for transfers between devices: 331 us -> 117 us
  blocking collectives: 208 us -> 0 us
  Pallas kernels: 0 us -> 90.7 us
  starting transfers between devices: 14.7 us -> 35.1 us
  other arithmetic: 85.2 us -> 65.6 us
  matrix products: 162 us -> 178 us
  local copies, waits for them, and re-layouts: 20.4 us -> 33.6 us
  between operations: 14.8 us -> 2.43 us
    reduce_scatter x2 -> x0, waiting for transfers between devices: 218 us -> none  [the longest x1 125 us: on_device(): lax.psum_scatter(grad_qkv_weight, ('exp', 'rep'), scatter_dimension=0, ti...]
    pallas_call x0 -> x2, Pallas kernels: none -> 90.7 us  [the longest x1 53.3 us: scatter_sums(): pl.pallas_call(functools.partial(scatter_kernel, devices, reps, chunks, l...]
    unnamed x2 -> x0, blocking collectives: 81.3 us -> none
    all_gather x1 -> x0, blocking collectives: 65.3 us -> none  [on_device(): lax.all_gather(w_router, ('exp', 'rep'), axis=0, tiled=True)]
    all_to_all x1 -> x0, blocking collectives: 50.3 us -> none  [on_device(): lax.all_to_all(grad_slots.astype(jnp.bfloat16).reshape(experts, capacity,...]
    ppermute x0 -> x10, waiting for transfers between devices: none -> 36.3 us  [the longest x4 36.3 us: rep_spread(): arrived = lax.ppermute(piece, 'rep', rep_pairs(reps, bit))]
    all_gather x2 -> x0, waiting for transfers between devices: 28.1 us -> none  [the longest x1 19.1 us: on_device(): lax.all_gather(w_out, ('exp', 'rep'), axis=0, tiled=True)]
    dot_general x10 -> x9, matrix products: 78.8 us -> 101 us  [the longest x1 41.5 us: on_device(): jnp.dot(received, first_weight, preferred_element_type=jnp.float32)]
  transfers between devices with their start and end apart: 8 -> 16, of which waited for: 7 -> 7; matrix products, arithmetic and copies ran while one was open for 19% -> 36% of each run, Pallas kernels for 0% -> 10%
where the time goes in v1:
time: 529 us; the launch traced here: 523 us
  matrix products  178 us (34%)
  waiting for transfers between devices  117 us (22%)
  Pallas kernels  90.7 us (17%)
  other arithmetic  65.6 us (12%)
  starting transfers between devices  35.1 us (7%)
  local copies, waits for them, and re-layouts  33.6 us (6%)
    all_to_all x6, waiting for transfers between devices, exchange(): lax.all_to_all(blocks, 'exp', split_axis=0, concat_axis=0, tiled=True)  80.6 us
    pallas_call x1, Pallas kernels, scatter_sums(): pl.pallas_call(functools.partial(scatter_kernel, devices, reps, chunks, l...  53.3 us
    dot_general x1, matrix products, on_device(): jnp.dot(received, first_weight, preferred_element_type=jnp.float32)  41.5 us
    pallas_call x1, Pallas kernels, gather_blocks(): pl.pallas_call(functools.partial(gather_kernel, devices, reps), out_shape...  37.4 us
    ppermute x4, waiting for transfers between devices, rep_spread(): arrived = lax.ppermute(piece, 'rep', rep_pairs(reps, bit))  36.3 us
    all_to_all x6, starting transfers between devices, exchange(): lax.all_to_all(blocks, 'exp', split_axis=0, concat_axis=0, tiled=True)  29.3 us
    dot_general x1, matrix products, on_device(): lax.dot_general(grad_results, second_weight, contract_last, preferred_ele...  13.6 us
    convert_element_type x1, other arithmetic, attend_backward(): grad_scores = (probs * (grad_probs - jnp.sum(probs * grad_probs, axis=-1,...  12.4 us
  transfers between devices with their start and end apart: 16, of which 7 were waited for; matrix products, arithmetic and copies ran while one was open for 36% of the time, Pallas kernels for 10%

profile of v1, /device:TPU:0, one launch (start us, length us, event | category | flops | bytes accessed | tf_op | source)
XLA Modules:
  0.0 522.6 jit_solution(6350478384972308005)
XLA Ops:
  8.4 1.6 fusion.115.own_ref
  10.0 37.4 %gather_dense.1 = bf16[32,24,3200]{2,1,0:T(8,128)(2,1)} custom-call(bf16[24,3200]{1,0:T(8,128)(2,1)} %fusion.115.own_ref), custom_call_target="tpu_custom_call" | custom-call | tf_op jit(solution)/shard_map/gather_dense/pallas_call | solution.py:226
  48.5 4.1 slice.95
  54.7 3.5 convolution_convert_fusion.5
  58.3 2.4 convolution_convert_fusion.3
  60.7 1.4 fusion.145
  62.9 1.9 copy.88
  64.8 2.6 copy.87
  67.4 7.7 %fusion.146 = (f32[12,576]{1,0:T(8,128)S(1)}, f32[12,576,576]{1,2,0:T(8,128)}) fusion(bf16[576,12,64]{0,2,1:T(8,128)(2,1)S(1)} %bitcast.121, bf16[576,12,64]{0,2,1:T(8,128)(2,1)S(1)} %bitcast.116, pred[576,576]{0,1:T(8,128)(4,1)S(1)} %fusion.78), kind=kOutput, calls=%fused_computation.222 | convolution fusion | flops 521544960 | bytes 18054144 | tf_op jit(solution)/shard_map/qhc,khc->hqk/dot_general | solution.py:65
  75.1 8.6 %fusion = f32[12,576]{1,0:T(8,128)S(1)} fusion(f32[12,576,576]{1,2,0:T(8,128)} %get-tuple-element.108, f32[12,576]{1,0:T(8,128)S(1)} %get-tuple-element.107), kind=kLoop, calls=%fused_computation.8 | loop fusion | flops 7955712 | bytes 15980544 | tf_op jit(solution)/shard_map/reduce_sum | solution.py:76
  83.7 9.3 %fusion.79 = bf16[12,64,576]{2,1,0:T(8,128)(2,1)S(1)} fusion(bf16[576,12,64]{0,2,1:T(8,128)(2,1)S(1)} %bitcast.125, f32[12,576,576]{1,2,0:T(8,128)} %get-tuple-element.108, f32[12,576]{1,0:T(8,128)S(1)} %fusion, f32[12,576]{1,0:T(8,128)S(1)} %get-tuple-element.107), kind=kOutput, calls=%fused_computation.127 | convolution fusion | flops 521994240 | bytes 17750016 | tf_op jit(solution)/shard_map/hqk,khc->qhc/dot_general | solution.py:78
  93.1 2.6 fusion.147
  97.3 3.5 convolution_convert_fusion.4
  100.8 6.3 %all-to-all-start = ((bf16[8,152,768]{2,1,0:T(8,128)(2,1)}), bf16[8,152,768]{2,1,0:T(8,128)(2,1)S(1)}, u32[]{:S(2)}, u32[]{:S(2)}) async-start(bf16[8,152,768]{2,1,0:T(8,128)(2,1)} %bitcast.135), calls=%async_computation | async-start | bytes 3735552 | tf_op jit(solution)/shard_map/all_to_all | solution.py:423
  108.4 2.5 fusion.148
  110.9 40.1 %all-to-all-done = bf16[8,152,768]{2,1,0:T(8,128)(2,1)S(1)} async-done(((bf16[8,152,768]{2,1,0:T(8,128)(2,1)}), bf16[8,152,768]{2,1,0:T(8,128)(2,1)S(1)}, u32[]{:S(2)}, u32[]{:S(2)}) %all-to-all-start) | async-done | bytes 1867808 | tf_op jit(solution)/shard_map/all_to_all | solution.py:423
  151.0 4.3 all-to-all-start.3
  155.3 41.5 %fusion.3 = (bf16[1216,3072]{1,0:T(8,128)(2,1)}, f32[1216,3072]{1,0:T(8,128)}) fusion(f32[3072]{0:T(1024)S(1)} %bitcast.147, bf16[1216,768]{1,0:T(8,128)(2,1)S(1)} %bitcast.130, bf16[1,768,3072]{2,1,0:T(8,128)(2,1)} %param.25), kind=kOutput, calls=%fused_computation.11 | convolution fusion | flops 5984354304 | bytes 29011968 | tf_op jit(solution)/shard_map/dot_general | solution.py:501
  196.8 1.5 all-to-all-done.3
  198.4 12.1 %multiply_reduce_fusion.1 = (f32[1216]{0:T(1024)S(1)}, f32[1216,768]{1,0:T(8,128)}, bf16[1216,768]{1,0:T(8,128)(2,1)}) fusion(bf16[1216,768]{1,0:T(8,128)(2,1)} %bitcast.68, f32[768]{0:T(1024)S(1)} %copy-done.57, bf16[1216,3072]{1,0:T(8,128)(2,1)} %get-tuple-element.111, bf16[1,3072,768]{2,1,0:T(8,128)(2,1)} %param.27), kind=kOutput, calls=%fused_computation.57 | convolution fusion | flops 5743410176 | bytes 19668736 | tf_op jit(solution)/shard_map/dot_general | solution.py:511
  211.2 4.4 all-to-all-start.5
  215.7 6.4 %all-to-all-done.5 = f32[8,1,152]{2,1,0:T(1,128)S(1)} async-done(((f32[8,1,152]{2,1,0:T(1,128)}), f32[8,1,152]{2,1,0:T(1,128)S(1)}, u32[]{:S(2)}, u32[]{:S(2)}) %all-to-all-start.5) | async-done | bytes 4896 | tf_op jit(solution)/shard_map/all_to_all | solution.py:423
  222.3 1.5 fusion.41
  223.9 1.6 fusion.40
  226.1 3.3 all-to-all-start.2
  229.5 6.4 %all-to-all-done.2 = f32[8,1,152]{2,1,0:T(1,128)S(1)} async-done(((f32[8,1,152]{2,1,0:T(1,128)}), f32[8,1,152]{2,1,0:T(1,128)S(1)}, u32[]{:S(2)}, u32[]{:S(2)}) %all-to-all-start.2) | async-done | bytes 4896 | tf_op jit(solution)/shard_map/all_to_all | solution.py:423
  235.9 4.7 all-to-all-start.1
  240.8 2.2 convert_reduce_fusion.1
  243.0 13.6 %convert_reduce_fusion = (f32[3072]{0:T(1024)S(1)}, bf16[1216,3072]{1,0:T(8,128)(2,1)S(1)}) fusion(f32[1216,3072]{1,0:T(8,128)} %get-tuple-element.112, f32[3072]{0:T(1024)S(1)} %bitcast.148, bf16[1216,768]{1,0:T(8,128)(2,1)S(1)} %bitcast.136, bf16[1,3072,768]{2,1,0:T(8,128)(2,1)} %param.27), kind=kOutput, calls=%fused_computation.17 | convolution fusion | flops 5786366976 | bytes 29024256 | tf_op jit(solution)/shard_map/dot_general | solution.py:506
  256.8 9.2 %convolution_convert_fusion = bf16[3072,768]{1,0:T(8,128)(2,1)S(1)} fusion(bf16[1216,3072]{1,0:T(8,128)(2,1)S(1)} %bitcast.160, f32[1216,768]{1,0:T(8,128)} %get-tuple-element.101, f32[1216]{0:T(1024)S(1)} %mul.391), kind=kOutput, calls=%fused_computation.37 | convolution fusion | flops 5742034944 | bytes 15930112 | tf_op jit(solution)/shard_map/dot_general | solution.py:526
  266.0 6.6 %convolution_convert_fusion.1 = bf16[768,3072]{1,0:T(8,128)(2,1)S(1)} fusion(bf16[1216,768]{1,0:T(8,128)(2,1)S(1)} %bitcast.131, bf16[1216,3072]{1,0:T(8,128)(2,1)S(1)} %get-tuple-element.121), kind=kOutput, calls=%fused_computation.38 | convolution fusion | flops 5740167168 | bytes 14057472 | tf_op jit(solution)/shard_map/dot_general | solution.py:529
  272.6 1.7 constant_dynamic-slice_fusion.1
  274.8 1.6 constant_dynamic-slice_fusion.3
  276.8 7.2 %fusion.33 = bf16[1216,768]{1,0:T(8,128)(2,1)} fusion(bf16[1216,3072]{1,0:T(8,128)(2,1)S(1)} %get-tuple-element.121, bf16[1,768,3072]{2,1,0:T(8,128)(2,1)S(1)} %bitcast.156), kind=kOutput, calls=%fused_computation.63 | convolution fusion | flops 5738741760 | bytes 14057472 | tf_op jit(solution)/shard_map/dot_general | solution.py:514
  284.7 6.2 %all-to-all-start.4 = ((bf16[8,152,768]{2,1,0:T(8,128)(2,1)}), bf16[8,152,768]{2,1,0:T(8,128)(2,1)}, u32[]{:S(2)}, u32[]{:S(2)}) async-start(bf16[8,152,768]{2,1,0:T(8,128)(2,1)} %bitcast.133), calls=%async_computation.4 | async-start | bytes 3735552 | tf_op jit(solution)/shard_map/all_to_all | solution.py:423
  292.4 3.0 add_convert_fusion
  295.4 1.3 constant_dynamic-slice_fusion
  296.7 1.4 collective-permute-start.7
  300.8 3.2 fusion.44
  304.0 4.2 add_convert_fusion.4
  308.2 26.1 %all-to-all-done.4 = bf16[8,152,768]{2,1,0:T(8,128)(2,1)} async-done(((bf16[8,152,768]{2,1,0:T(8,128)(2,1)}), bf16[8,152,768]{2,1,0:T(8,128)(2,1)}, u32[]{:S(2)}, u32[]{:S(2)}) %all-to-all-start.4) | async-done | bytes 1867808 | tf_op jit(solution)/shard_map/all_to_all | solution.py:423
  334.3 3.6 fusion.84
  337.9 2.2 multiply_reduce_fusion.2
  342.0 2.2 convolution_convert_fusion.7
  344.9 11.3 %multiply_reduce_fusion = (f32[12,576]{1,0:T(8,128)S(1)}, f32[12,576,576]{1,2,0:T(8,128)}) fusion(f32[12,576,576]{1,2,0:T(8,128)} %get-tuple-element.108, f32[12,576]{1,0:T(8,128)S(1)} %copy-done.30, bf16[576,12,64]{0,2,1:T(8,128)(2,1)S(1)} %bitcast.119, bf16[576,12,64]{0,2,1:T(8,128)(2,1)S(1)} %bitcast.126), kind=kOutput, calls=%fused_computation.3 | convolution fusion | flops 521544960 | bytes 33675264 | tf_op jit(solution)/shard_map/qhc,khc->hqk/dot_general | solution.py:86
  356.2 12.4 %multiply_convert_fusion = bf16[12,576,576]{1,2,0:T(8,128)(2,1)S(1)} fusion(f32[12,576,576]{1,2,0:T(8,128)} %get-tuple-element.118, f32[12,576,576]{1,2,0:T(8,128)} %get-tuple-element.108, f32[12,576]{1,0:T(8,128)S(1)} %get-tuple-element.117, f32[12,576]{1,0:T(8,128)S(1)} %copy-done.30), kind=kLoop, calls=%fused_computation.2 | loop fusion | flops 15925248 | bytes 39868416 | tf_op jit(solution)/shard_map/convert_element_type | solution.py:92
  368.6 9.9 %fusion.80 = bf16[12,64,576]{2,1,0:T(8,128)(2,1)} fusion(bf16[576,12,64]{0,2,1:T(8,128)(2,1)S(1)} %bitcast.120, f32[12,576,576]{1,2,0:T(8,128)} %get-tuple-element.108, f32[12,576]{1,0:T(8,128)S(1)} %copy-done.30), kind=kOutput, calls=%fused_computation.128 | convolution fusion | flops 518012928 | bytes 17722368 | tf_op jit(solution)/shard_map/hqk,qhc->khc/dot_general | solution.py:87
  378.5 1.8 add_convert_fusion.3
  380.3 1.4 collective-permute-start.2
  381.8 2.7 multiply_convert_fusion.3
  384.5 3.0 add_convert_fusion.2
  388.2 1.7 multiply_convert_fusion.4
  389.9 19.3 %collective-permute-done.2 = bf16[192,3072]{1,0:T(8,128)(2,1)S(1)} collective-permute-done((bf16[192,3072]{1,0:T(8,128)(2,1)S(1)}, bf16[192,3072]{1,0:T(8,128)(2,1)S(1)}, u32[]{:S(2)}, u32[]{:S(2)}) %collective-permute-start.2) | collective-permute-done | bytes 1179680 | tf_op jit(solution)/shard_map/ppermute | solution.py:406
  410.3 4.1 fusion.69
  415.4 17.0 %collective-permute-done.8 = bf16[768,768]{1,0:T(8,128)(2,1)} collective-permute-done((bf16[768,768]{1,0:T(8,128)(2,1)}, bf16[768,768]{1,0:T(8,128)(2,1)}, u32[]{:S(2)}, u32[]{:S(2)}) %collective-permute-start.8) | collective-permute-done | bytes 1179680 | tf_op jit(solution)/shard_map/ppermute | solution.py:406
  432.4 3.8 maximum_select_fusion.3
  436.3 2.1 convolution_convert_fusion.6
  438.4 7.4 %convolution_convert_fusion.2 = bf16[768,2304]{1,0:T(8,128)(2,1)} fusion(bf16[576,768]{0,1:T(8,128)(2,1)S(1)} %bitcast.139, bf16[576,768]{0,1:T(8,128)(2,1)S(1)} %bitcast.141, bf16[576,768]{0,1:T(8,128)(2,1)S(1)} %bitcast.129, bf16[576,768]{1,0:T(8,128)(2,1)S(1)} %copy-done.11, f32[768]{0:T(1024)S(1)} %copy-done.54, f32[768]{0:T(1024)S(1)} %copy-done.49, ...), kind=kOutput, calls=%fused_computation.39 | convolution fusion | flops 2050818048 | bytes 7088640 | tf_op jit(solution)/shard_map/dot_general | solution.py:566
  445.8 53.3 %scatter_dense.1 = (f32[24,2304]{1,0:T(8,128)}, f32[24,768]{1,0:T(8,128)}, f32[24,128]{1,0:T(8,128)}) custom-call(bf16[4,8,24,2304]{3,2,1,0:T(8,128)(2,1)} %bitcast.127, bf16[4,8,24,768]{3,2,1,0:T(8,128)(2,1)} %bitcast.137, bf16[4,8,24,128]{3,2,1,0:T(8,128)(2,1)} %bitcast.142), custom_call_target="tpu_custom_call" | custom-call | tf_op jit(solution)/shard_map/scatter_dense/pallas_call | solution.py:368
  499.1 1.4 copy.96
  500.5 1.6 slice_reduce_fusion
  502.1 3.8 fusion.68
  505.9 6.3 %fusion.21 = f32[1,768,3072]{2,1,0:T(8,128)} fusion(bf16[1,384,3072]{2,1,0:T(8,128)(2,1)} %bitcast.36, bf16[1,384,3072]{2,1,0:T(8,128)(2,1)S(1)} %bitcast.118, pred[]{:T(512)S(6)} %eq.133), kind=kLoop, calls=%fused_computation.41 | loop fusion | flops 23592960 | bytes 14155777 | tf_op jit(solution)/shard_map/convert_element_type | solution.py:535
  512.2 8.6 %fusion.22 = f32[1,3072,768]{2,1,0:T(8,128)} fusion(bf16[1,1536,768]{2,1,0:T(8,128)(2,1)} %bitcast.40, bf16[1,1536,768]{2,1,0:T(8,128)(2,1)} %bitcast.39, pred[]{:T(512)S(6)} %eq.133), kind=kLoop, calls=%fused_computation.43 | loop fusion | flops 23592960 | bytes 14155777 | tf_op jit(solution)/shard_map/convert_element_type | solution.py:534
  (239 shorter events, 28.5 us)
Async XLA Ops:
  4.5 92.7 %copy-start.61 = (pred[576]{0:T(1024)(128)(4,1)}, pred[576]{0:T(1024)(128)(4,1)S(1)}, u32[]{:S(2)}) copy-start(pred[576]{0:T(1024)(128)(4,1)S(1)} %get-tuple-element.102) | copy-start | bytes 1732
  48.4 5.1 copy-start.47
  48.4 5.1 copy-start.65
  48.5 6.2 %copy-start.28 = (bf16[576,768]{1,0:T(8,128)(2,1)S(1)}, bf16[576,768]{1,0:T(8,128)(2,1)}, u32[]{:S(2)}) copy-start(bf16[576,768]{1,0:T(8,128)(2,1)} %param.33) | copy-start | bytes 2654212
  53.1 5.2 copy-start.45
  53.6 43.7 %copy-start.55 = (s32[576]{0:T(1024)}, s32[576]{0:T(1024)S(1)}, u32[]{:S(2)}) copy-start(s32[576]{0:T(1024)S(1)} %get-tuple-element.96) | copy-start | bytes 6916
  54.0 43.2 %copy-start.63 = (pred[576]{0:T(1024)(128)(4,1)}, pred[576]{0:T(1024)(128)(4,1)S(1)}, u32[]{:S(2)}) copy-start(pred[576]{0:T(1024)(128)(4,1)S(1)} %compare_and_fusion) | copy-start | bytes 1732
  54.1 43.1 %copy-start.58 = (s32[576]{0:T(1024)}, s32[576]{0:T(1024)S(1)}, u32[]{:S(2)}) copy-start(s32[576]{0:T(1024)S(1)} %add_reduce_fusion) | copy-start | bytes 6916
  54.7 41.4 %copy-start.39 = (f32[768]{0:T(1024)}, f32[768]{0:T(1024)S(1)}, u32[]{:S(2)}) copy-start(f32[768]{0:T(1024)S(1)} %get-tuple-element.92) | copy-start | bytes 9220
  62.9 12.2 %copy-start.2 = (bf16[576,768]{0,1:T(8,128)(2,1)}, bf16[576,768]{0,1:T(8,128)(2,1)S(1)}, u32[]{:S(2)}) copy-start(bf16[576,768]{0,1:T(8,128)(2,1)S(1)} %copy.89) | copy-start | bytes 2654212
  64.7 10.4 %copy-start.8 = (bf16[576,768]{0,1:T(8,128)(2,1)}, bf16[576,768]{0,1:T(8,128)(2,1)S(1)}, u32[]{:S(2)}) copy-start(bf16[576,768]{0,1:T(8,128)(2,1)S(1)} %copy.88) | copy-start | bytes 2654212
  75.1 8.6 %copy-start.18 = (bf16[576,768]{0,1:T(8,128)(2,1)S(1)}, bf16[576,768]{0,1:T(8,128)(2,1)}, u32[]{:S(2)}) copy-start(bf16[576,768]{0,1:T(8,128)(2,1)} %copy.87) | copy-start | bytes 2654212
  95.7 5.1 copy-start.33
  96.1 4.8 copy-start.41
  97.3 11.1 %copy-start.12 = (bf16[576,768]{1,0:T(8,128)(2,1)}, bf16[576,768]{1,0:T(8,128)(2,1)S(1)}, u32[]{:S(2)}) copy-start(bf16[576,768]{1,0:T(8,128)(2,1)S(1)} %add_convert_fusion.5) | copy-start | bytes 2654212
  100.8 6.3 %copy-start.52 = (bf16[1,3072]{1,0:T(2,128)(2,1)S(1)}, bf16[1,3072]{1,0:T(2,128)(2,1)}, u32[]{:S(2)}) copy-start(bf16[1,3072]{1,0:T(2,128)(2,1)} %param.26) | copy-start | bytes 18436
  100.8 6.3 %copy-start.60 = (bf16[1,768]{1,0:T(2,128)(2,1)S(1)}, bf16[1,768]{1,0:T(2,128)(2,1)}, u32[]{:S(2)}) copy-start(bf16[1,768]{1,0:T(2,128)(2,1)} %param.28) | copy-start | bytes 4612
  100.8 50.1 %all-to-all-start = ((bf16[8,152,768]{2,1,0:T(8,128)(2,1)}), bf16[8,152,768]{2,1,0:T(8,128)(2,1)S(1)}, u32[]{:S(2)}, u32[]{:S(2)}) async-start(bf16[8,152,768]{2,1,0:T(8,128)(2,1)} %bitcast.135), calls=%async_computation | async-start | bytes 3735552 | tf_op jit(solution)/shard_map/all_to_all | solution.py:423
  151.0 47.4 %all-to-all-start.3 = ((bf16[8,152,768]{2,1,0:T(8,128)(2,1)}), bf16[8,152,768]{2,1,0:T(8,128)(2,1)}, u32[]{:S(2)}, u32[]{:S(2)}) async-start(bf16[8,152,768]{2,1,0:T(8,128)(2,1)} %bitcast.134), calls=%async_computation.3 | async-start | bytes 3735552 | tf_op jit(solution)/shard_map/all_to_all | solution.py:423
  155.3 43.0 %copy-start.57 = (f32[768]{0:T(1024)S(1)}, f32[768]{0:T(1024)}, u32[]{:S(2)}) copy-start(f32[768]{0:T(1024)} %convert_reduce_fusion.4) | copy-start | bytes 9220
  198.4 17.2 %copy-start.31 = (f32[576,8]{0,1:T(8,128)S(1)}, f32[576,8]{0,1:T(8,128)}, u32[]{:S(2)}) copy-start(f32[576,8]{0,1:T(8,128)} %get-tuple-element.115) | copy-start | bytes 55300
  198.4 17.2 %copy-start.36 = (f32[576]{0:T(1024)S(1)}, f32[576]{0:T(1024)}, u32[]{:S(2)}) copy-start(f32[576]{0:T(1024)} %get-tuple-element.114) | copy-start | bytes 6916
  198.4 23.9 %copy-start.56 = (s32[576]{0:T(1024)S(1)}, s32[576]{0:T(1024)}, u32[]{:S(2)}) copy-start(s32[576]{0:T(1024)} %copy-done.55) | copy-start | bytes 6916
  198.4 23.9 %copy-start.59 = (s32[576]{0:T(1024)S(1)}, s32[576]{0:T(1024)}, u32[]{:S(2)}) copy-start(s32[576]{0:T(1024)} %copy-done.58) | copy-start | bytes 6916
  198.4 23.9 %copy-start.62 = (pred[576]{0:T(1024)(128)(4,1)S(1)}, pred[576]{0:T(1024)(128)(4,1)}, u32[]{:S(2)}) copy-start(pred[576]{0:T(1024)(128)(4,1)} %copy-done.61) | copy-start | bytes 1732
  198.4 23.9 %copy-start.64 = (pred[576]{0:T(1024)(128)(4,1)S(1)}, pred[576]{0:T(1024)(128)(4,1)}, u32[]{:S(2)}) copy-start(pred[576]{0:T(1024)(128)(4,1)} %copy-done.63) | copy-start | bytes 1732
  198.4 25.4 %copy-start.38 = (s32[576]{0:T(1024)S(1)}, s32[576]{0:T(1024)}, u32[]{:S(2)}) copy-start(s32[576]{0:T(1024)} %copy-done.37) | copy-start | bytes 6916
  198.4 25.4 %copy-start.44 = (s32[576]{0:T(1024)S(1)}, s32[576]{0:T(1024)}, u32[]{:S(2)}) copy-start(s32[576]{0:T(1024)} %copy-done.43) | copy-start | bytes 6916
  211.2 10.9 %all-to-all-start.5 = ((f32[8,1,152]{2,1,0:T(1,128)}), f32[8,1,152]{2,1,0:T(1,128)S(1)}, u32[]{:S(2)}, u32[]{:S(2)}) async-start(f32[8,1,152]{2,1,0:T(1,128)} %all_to_all.30), calls=%async_computation.5 | async-start | bytes 16384 | tf_op jit(solution)/shard_map/all_to_all | solution.py:423
  226.1 9.8 %all-to-all-start.2 = ((f32[8,1,152]{2,1,0:T(1,128)}), f32[8,1,152]{2,1,0:T(1,128)S(1)}, u32[]{:S(2)}, u32[]{:S(2)}) async-start(f32[8,1,152]{2,1,0:T(1,128)} %all_to_all.26), calls=%async_computation.2 | async-start | bytes 16384 | tf_op jit(solution)/shard_map/all_to_all | solution.py:423
  235.9 48.8 %all-to-all-start.1 = ((bf16[8,152,768]{2,1,0:T(8,128)(2,1)}), bf16[8,152,768]{2,1,0:T(8,128)(2,1)}, u32[]{:S(2)}, u32[]{:S(2)}) async-start(bf16[8,152,768]{2,1,0:T(8,128)(2,1)} %bitcast.132), calls=%async_computation.1 | async-start | bytes 3735552 | tf_op jit(solution)/shard_map/all_to_all | solution.py:423
  240.8 16.0 %slice-start.4 = ((s8[7471104]{0:T(1024)(128)(4,1)}), s8[4194304]{0:T(1024)(128)(4,1)S(1)}, s32[]{:S(2)}) async-start(s8[7471104]{0:T(1024)(128)(4,1)} %bitcast.159), calls=%async_computation.10 | async-start | bytes 8388608
  240.8 36.0 %slice-start.2 = ((s8[4718592]{0:T(1024)(128)(4,1)}), s8[4194304]{0:T(1024)(128)(4,1)S(1)}, s32[]{:S(2)}) async-start(s8[4718592]{0:T(1024)(128)(4,1)} %bitcast.155), calls=%async_computation.8 | async-start | bytes 8388608
  243.0 13.8 %slice-start.5 = ((s8[7471104]{0:T(1024)(128)(4,1)}), s8[3276800]{0:T(1024)(128)(4,1)S(1)}, s32[]{:S(2)}) async-start(s8[7471104]{0:T(1024)(128)(4,1)} %bitcast.159), calls=%async_computation.11 | async-start | bytes 6553600
  243.0 33.8 %slice-start.3 = ((s8[4718592]{0:T(1024)(128)(4,1)}), s8[524288]{0:T(1024)(128)(4,1)S(1)}, s32[]{:S(2)}) async-start(s8[4718592]{0:T(1024)(128)(4,1)} %bitcast.155), calls=%async_computation.9 | async-start | bytes 1048576
  256.7 27.3 %collective-permute-start.4 = (f32[30,128]{1,0:T(8,128)S(1)}, f32[30,128]{1,0:T(8,128)S(1)}, u32[]{:S(2)}, u32[]{:S(2)}) collective-permute-start(f32[30,128]{1,0:T(8,128)S(1)} %maximum_bitcast_fusion), channel_id=1, source_target_pairs={{0,1},{1,0},{2,3},{3,2},{4,5},{5,4},{6,7},{7,6},{8,9},{9,8},{10,11... | collective-permute-start | bytes 46088 | tf_op jit(solution)/shard_map/ppermute | solution.py:417
  266.0 6.7 %copy-start.17 = (bf16[3072,768]{1,0:T(8,128)(2,1)}, bf16[3072,768]{1,0:T(8,128)(2,1)S(1)}, u32[]{:S(2)}) copy-start(bf16[3072,768]{1,0:T(8,128)(2,1)S(1)} %convolution_convert_fusion) | copy-start | bytes 14155780
  274.4 18.0 %collective-permute-start.6 = (bf16[1536,768]{1,0:T(8,128)(2,1)}, bf16[1536,768]{1,0:T(8,128)(2,1)}, u32[]{:S(2)}, u32[]{:S(2)}) collective-permute-start(bf16[1536,768]{1,0:T(8,128)(2,1)} %constant_dynamic-slice_fusion.1), channel_id=1, source_target_pairs={{0,1},{1,0},{2,3},{3,2},{4,5},{5,4},{6,7},{7,6},{8,9},{9,8},{10,11... | collective-permute-start | bytes 7077896 | tf_op jit(solution)/shard_map/ppermute | solution.py:397
  276.4 21.7 %collective-permute-start = (bf16[384,3072]{1,0:T(8,128)(2,1)}, bf16[384,3072]{1,0:T(8,128)(2,1)S(1)}, u32[]{:S(2)}, u32[]{:S(2)}) collective-permute-start(bf16[384,3072]{1,0:T(8,128)(2,1)} %constant_dynamic-slice_fusion.3), channel_id=1, source_target_pairs={{0,1},{1,0},{2,3},{3,2},{4,5},{5,4},{6,7},{7,6},{8,9},{9,8},{10,11... | collective-permute-start | bytes 7077896 | tf_op jit(solution)/shard_map/ppermute | solution.py:397
  284.0 6.9 %copy-start.13 = (bf16[576,768]{1,0:T(8,128)(2,1)S(1)}, bf16[576,768]{1,0:T(8,128)(2,1)}, u32[]{:S(2)}) copy-start(bf16[576,768]{1,0:T(8,128)(2,1)} %copy-done.12) | copy-start | bytes 2654212
  284.0 7.1 %collective-permute-start.5 = (f32[30,128]{1,0:T(8,128)S(1)}, f32[30,128]{1,0:T(8,128)S(1)}, u32[]{:S(2)}, u32[]{:S(2)}) collective-permute-start(f32[30,128]{1,0:T(8,128)S(1)} %fusion.142), channel_id=1, source_target_pairs={{0,2},{1,3},{2,0},{3,1},{4,6},{5,7},{6,4},{7,5},{8,10},{9,11},{10,... | collective-permute-start | bytes 46088 | tf_op jit(solution)/shard_map/ppermute | solution.py:417
  284.7 49.6 %all-to-all-start.4 = ((bf16[8,152,768]{2,1,0:T(8,128)(2,1)}), bf16[8,152,768]{2,1,0:T(8,128)(2,1)}, u32[]{:S(2)}, u32[]{:S(2)}) async-start(bf16[8,152,768]{2,1,0:T(8,128)(2,1)} %bitcast.133), calls=%async_computation.4 | async-start | bytes 3735552 | tf_op jit(solution)/shard_map/all_to_all | solution.py:423
  290.9 7.1 %slice-start = ((s8[4718592]{0:T(1024)(128)(4,1)}), s8[4194304]{0:T(1024)(128)(4,1)S(1)}, s32[]{:S(2)}) async-start(s8[4718592]{0:T(1024)(128)(4,1)} %bitcast.123), calls=%async_computation.6 | async-start | bytes 8388608
  292.4 5.7 %slice-start.1 = ((s8[4718592]{0:T(1024)(128)(4,1)}), s8[524288]{0:T(1024)(128)(4,1)S(1)}, s32[]{:S(2)}) async-start(s8[4718592]{0:T(1024)(128)(4,1)} %bitcast.123), calls=%async_computation.7 | async-start | bytes 1048576
  296.7 87.8 %collective-permute-start.7 = (bf16[768,768]{1,0:T(8,128)(2,1)}, bf16[768,768]{1,0:T(8,128)(2,1)}, u32[]{:S(2)}, u32[]{:S(2)}) collective-permute-start(bf16[768,768]{1,0:T(8,128)(2,1)} %constant_dynamic-slice_fusion), channel_id=1, source_target_pairs={{0,2},{1,3},{2,0},{3,1},{4,6},{5,7},{6,4},{7,5},{8,10},{9,11},{10,... | collective-permute-start | bytes 3538952 | tf_op jit(solution)/shard_map/ppermute | solution.py:397
  299.0 5.0 copy-start.6
  300.2 78.4 %collective-permute-start.1 = (bf16[192,3072]{1,0:T(8,128)(2,1)}, bf16[192,3072]{1,0:T(8,128)(2,1)}, u32[]{:S(2)}, u32[]{:S(2)}) collective-permute-start(bf16[192,3072]{1,0:T(8,128)(2,1)} %constant_dynamic-slice_fusion.2), channel_id=1, source_target_pairs={{0,2},{1,3},{2,0},{3,1},{4,6},{5,7},{6,4},{7,5},{8,10},{9,11},{10,... | collective-permute-start | bytes 3538952 | tf_op jit(solution)/shard_map/ppermute | solution.py:397
  368.6 9.9 %copy-start.7 = (bf16[384,3072]{1,0:T(8,128)(2,1)S(1)}, bf16[384,3072]{1,0:T(8,128)(2,1)}, u32[]{:S(2)}) copy-start(bf16[384,3072]{1,0:T(8,128)(2,1)} %copy-done.6) | copy-start | bytes 7077892
  380.3 28.9 %collective-permute-start.2 = (bf16[192,3072]{1,0:T(8,128)(2,1)S(1)}, bf16[192,3072]{1,0:T(8,128)(2,1)S(1)}, u32[]{:S(2)}, u32[]{:S(2)}) collective-permute-start(bf16[192,3072]{1,0:T(8,128)(2,1)S(1)} %add_convert_fusion.3), channel_id=1, source_target_pairs={{0,2},{1,3},{2,0},{3,1},{4,6},{5,7},{6,4},{7,5},{8,10},{9,11},{10,... | collective-permute-start | bytes 3538952 | tf_op jit(solution)/shard_map/ppermute | solution.py:406
  384.5 25.8 %copy-start.26 = (bf16[12,64,576]{2,1,0:T(8,128)(2,1)}, bf16[12,64,576]{2,1,0:T(8,128)(2,1)S(1)}, u32[]{:S(2)}) copy-start(bf16[12,64,576]{2,1,0:T(8,128)(2,1)S(1)} %multiply_convert_fusion.3) | copy-start | bytes 2654212
  387.5 44.9 %collective-permute-start.8 = (bf16[768,768]{1,0:T(8,128)(2,1)}, bf16[768,768]{1,0:T(8,128)(2,1)}, u32[]{:S(2)}, u32[]{:S(2)}) collective-permute-start(bf16[768,768]{1,0:T(8,128)(2,1)} %add_convert_fusion.2), channel_id=1, source_target_pairs={{0,2},{1,3},{2,0},{3,1},{4,6},{5,7},{6,4},{7,5},{8,10},{9,11},{10,... | collective-permute-start | bytes 3538952 | tf_op jit(solution)/shard_map/ppermute | solution.py:406
  388.2 22.1 %copy-start.24 = (bf16[12,64,576]{2,1,0:T(8,128)(2,1)S(1)}, bf16[12,64,576]{2,1,0:T(8,128)(2,1)}, u32[]{:S(2)}) copy-start(bf16[12,64,576]{2,1,0:T(8,128)(2,1)} %fusion.80) | copy-start | bytes 2654212
  389.8 24.6 %copy-start.22 = (bf16[12,64,576]{2,1,0:T(8,128)(2,1)}, bf16[12,64,576]{2,1,0:T(8,128)(2,1)S(1)}, u32[]{:S(2)}) copy-start(bf16[12,64,576]{2,1,0:T(8,128)(2,1)S(1)} %multiply_convert_fusion.4) | copy-start | bytes 2654212
  389.9 20.4 %copy-start.11 = (bf16[576,768]{1,0:T(8,128)(2,1)S(1)}, bf16[576,768]{1,0:T(8,128)(2,1)}, u32[]{:S(2)}) copy-start(bf16[576,768]{1,0:T(8,128)(2,1)} %param.17) | copy-start | bytes 2654212
  389.9 20.4 %copy-start.21 = (bf16[768,2304]{1,0:T(8,128)(2,1)S(1)}, bf16[768,2304]{1,0:T(8,128)(2,1)}, u32[]{:S(2)}) copy-start(bf16[768,2304]{1,0:T(8,128)(2,1)} %slice.95) | copy-start | bytes 10616836
  389.9 20.4 %copy-start.46 = (f32[576]{0:T(1024)S(1)}, f32[576]{0:T(1024)}, u32[]{:S(2)}) copy-start(f32[576]{0:T(1024)} %copy-done.45) | copy-start | bytes 6916
  389.9 20.4 %copy-start.49 = (f32[768]{0:T(1024)S(1)}, f32[768]{0:T(1024)}, u32[]{:S(2)}) copy-start(f32[768]{0:T(1024)} %copy-done.48) | copy-start | bytes 9220
  389.9 20.4 %copy-start.51 = (f32[576]{0:T(1024)S(1)}, f32[576]{0:T(1024)}, u32[]{:S(2)}) copy-start(f32[576]{0:T(1024)} %copy-done.50) | copy-start | bytes 6916
  410.1 95.8 %collective-permute-start.3 = (bf16[384,3072]{1,0:T(8,128)(2,1)S(1)}, bf16[384,3072]{1,0:T(8,128)(2,1)}, u32[]{:S(2)}, u32[]{:S(2)}) collective-permute-start(bf16[384,3072]{1,0:T(8,128)(2,1)S(1)} %maximum_select_fusion.2), channel_id=1, source_target_pairs={{0,1},{1,0},{2,3},{3,2},{4,5},{5,4},{6,7},{7,6},{8,9},{9,8},{10,11... | collective-permute-start | bytes 7077896 | tf_op jit(solution)/shard_map/ppermute | solution.py:406
  414.7 21.6 %copy-start.15 = (f32[576,768]{1,0:T(8,128)S(1)}, f32[576,768]{1,0:T(8,128)}, u32[]{:S(2)}) copy-start(f32[576,768]{1,0:T(8,128)} %copy-done.14) | copy-start | bytes 5308420
  414.7 21.6 %copy-start.68 = (bf16[12,64,576]{2,1,0:T(8,128)(2,1)S(1)}, bf16[12,64,576]{2,1,0:T(8,128)(2,1)}, u32[]{:S(2)}) copy-start(bf16[12,64,576]{2,1,0:T(8,128)(2,1)} %copy-done.67) | copy-start | bytes 2654212
  436.2 76.0 %collective-permute-start.9 = (bf16[1536,768]{1,0:T(8,128)(2,1)}, bf16[1536,768]{1,0:T(8,128)(2,1)}, u32[]{:S(2)}, u32[]{:S(2)}) collective-permute-start(bf16[1536,768]{1,0:T(8,128)(2,1)} %maximum_select_fusion.3), channel_id=1, source_target_pairs={{0,1},{1,0},{2,3},{3,2},{4,5},{5,4},{6,7},{7,6},{8,9},{9,8},{10,11... | collective-permute-start | bytes 7077896 | tf_op jit(solution)/shard_map/ppermute | solution.py:406
  512.2 8.6 %copy-start.32 = (f32[24,2304]{1,0:T(8,128)S(1)}, f32[24,2304]{1,0:T(8,128)}, u32[]{:S(2)}) copy-start(f32[24,2304]{1,0:T(8,128)} %get-tuple-element.141) | copy-start | bytes 663556
  512.2 9.3 %copy-start.35 = (f32[24,768]{1,0:T(8,128)S(1)}, f32[24,768]{1,0:T(8,128)}, u32[]{:S(2)}) copy-start(f32[24,768]{1,0:T(8,128)} %get-tuple-element.142) | copy-start | bytes 221188
  (27 other events, 79.9 us)

commit v2 on v1

--- a/solution.py
+++ b/solution.py
@@ -103,7 +103,7 @@
     return joined.astype(jnp.bfloat16)
 
 
-def dispatch_tables(routes, priority, padding, experts, capacity):
+def dispatch_tables(routes, priority, padding, experts, capacity, padded):
     labels = jnp.arange(experts, dtype=jnp.int32)
     first_hot = (routes[:, 0:1] == labels[None, :]).astype(jnp.bfloat16)
     second_hot = (routes[:, 1:2] == labels[None, :]).astype(jnp.bfloat16)
@@ -119,9 +119,9 @@
     place_second = jnp.sum(before_second * second_hot, axis=1).astype(jnp.int32)
     kept_first = (padding == 1) & (place_first < capacity)
     kept_second = (padding == 1) & (place_second < capacity)
-    slot_labels = jnp.arange(experts * capacity, dtype=jnp.int32)
-    slot_first = routes[:, 0] * capacity + place_first
-    slot_second = routes[:, 1] * capacity + place_second
+    slot_labels = jnp.arange(experts * padded, dtype=jnp.int32)
+    slot_first = routes[:, 0] * padded + place_first
+    slot_second = routes[:, 1] * padded + place_second
     pick_first = ((slot_first[:, None] == slot_labels[None, :]) & kept_first[:, None]).astype(
         jnp.bfloat16
     )
@@ -419,6 +419,377 @@
     return small
 
 
+def row_of(column, width):
+    count = column.shape[0]
+    down = lax.broadcasted_iota(jnp.int32, (count, width), 0)
+    across = lax.broadcasted_iota(jnp.int32, (count, width), 1)
+    return jnp.sum(jnp.where(down == across, column, 0.0), axis=0, keepdims=True)
+
+
+def column_of(row, count):
+    width = row.shape[1]
+    down = lax.broadcasted_iota(jnp.int32, (count, width), 0)
+    across = lax.broadcasted_iota(jnp.int32, (count, width), 1)
+    return jnp.sum(jnp.where(down == across, row, 0.0), axis=1, keepdims=True)
+
+
+def three_terms(value):
+    high = value.astype(jnp.bfloat16).astype(jnp.float32)
+    rest = value - high
+    middle = rest.astype(jnp.bfloat16).astype(jnp.float32)
+    return (high, middle, rest - middle)
+
+
+def expert_kernel(
+    experts,
+    capacity,
+    padded,
+    block,
+    send_ref,
+    grad_ref,
+    w_in_ref,
+    w_back_ref,
+    b_in_ref,
+    b_back_ref,
+    return_ref,
+    result_ref,
+    sum_back_ref,
+    sum_in_ref,
+    sum_b_in_ref,
+    sum_b_back_ref,
+    slots,
+    grads,
+    gated,
+    weight_in,
+    weight_back,
+    active,
+    grad_pre,
+    back_rows,
+    result_rows,
+    result_total,
+    back_total,
+    stage_back,
+    stage_in,
+    load_sem,
+    send_sem,
+    recv_sem,
+    return_send_sem,
+    return_recv_sem,
+    result_sem,
+    stage_sem,
+):
+    mine = lax.axis_index("exp")
+    rep = lax.axis_index("rep")
+    bits = bit_count(experts)
+    groups = experts // 2
+    hidden = weight_in.shape[1]
+    steps = hidden // block
+    lanes = 256 if capacity <= 256 else D
+    gate_row = capacity - (padded - 16)
+
+    barrier = pltpu.get_barrier_semaphore()
+
+    def greet_one(step, carry):
+        other = lax.rem(mine + step, experts)
+        pl.semaphore_signal(barrier, inc=1, device_id=(other, rep), device_id_type=MESH_ID)
+        return carry
+
+    lax.fori_loop(1, experts, greet_one, 0)
+
+    def group_of(index):
+        half = lax.div(mine, 2)
+        found = half
+        for bit in range(bits - 1):
+            found = found + lax.rem(lax.div(index, 1 << bit), 2) * (
+                (1 - 2 * lax.rem(lax.div(half, 1 << bit), 2)) * (1 << bit)
+            )
+        return found
+
+    def place(expert):
+        return pl.ds(pl.multiple_of(expert * padded, 16), padded)
+
+    def outgoing(expert):
+        return pltpu.make_async_remote_copy(
+            src_ref=send_ref.at[expert],
+            dst_ref=slots.at[place(mine)],
+            send_sem=send_sem.at[expert],
+            recv_sem=recv_sem.at[mine],
+            device_id=(expert, rep),
+            device_id_type=MESH_ID,
+        )
+
+    def incoming(expert):
+        return pltpu.make_async_remote_copy(
+            src_ref=send_ref.at[mine],
+            dst_ref=slots.at[place(expert)],
+            send_sem=send_sem.at[expert],
+            recv_sem=recv_sem.at[expert],
+            device_id=(expert, rep),
+            device_id_type=MESH_ID,
+        )
+
+    def going_back(expert):
+        return pltpu.make_async_remote_copy(
+            src_ref=back_rows.at[place(expert)],
+            dst_ref=return_ref.at[mine],
+            send_sem=return_send_sem.at[expert],
+            recv_sem=return_recv_sem.at[mine],
+            device_id=(expert, rep),
+            device_id_type=MESH_ID,
+        )
+
+    def coming_back(expert):
+        return pltpu.make_async_remote_copy(
+            src_ref=back_rows.at[place(expert)],
+            dst_ref=return_ref.at[expert],
+            send_sem=return_send_sem.at[expert],
+            recv_sem=return_recv_sem.at[expert],
+            device_id=(expert, rep),
+            device_id_type=MESH_ID,
+        )
+
+    neighbour = flip(mine, 0)
+    loads = [
+        pltpu.make_async_copy(send_ref.at[mine], slots.at[place(mine)], load_sem.at[0]),
+        pltpu.make_async_copy(grad_ref, grads, load_sem.at[1]),
+        pltpu.make_async_copy(w_in_ref, weight_in, load_sem.at[2]),
+        pltpu.make_async_copy(w_back_ref, weight_back, load_sem.at[3]),
+    ]
+    for copy in loads:
+        copy.start()
+    pl.semaphore_wait(barrier, experts - 1)
+
+    def send_group(index):
+        pair = group_of(index)
+        outgoing(2 * pair).start()
+        outgoing(2 * pair + 1).start()
+
+    outgoing(neighbour).start()
+    if groups > 2:
+        send_group(2)
+    if groups > 1:
+        send_group(1)
+    for copy in loads:
+        copy.wait()
+
+    def send_back_group(index):
+        pair = group_of(index)
+        going_back(2 * pair).start()
+        going_back(2 * pair + 1).start()
+
+    def gate_columns(expert):
+        tail = slots[pl.ds(pl.multiple_of(expert * padded + padded - 16, 16), 16), :].astype(jnp.float32)
+        row = jnp.sum(tail[gate_row : gate_row + 3, :lanes], axis=0, keepdims=True)
+        return column_of(row, padded)
+
+    def group_step(index, carry):
+        pair = group_of(index)
+
+        @pl.when(index == 0)
+        def _():
+            incoming(neighbour).wait_recv()
+
+        @pl.when(index > 0)
+        def _():
+            incoming(2 * pair).wait_recv()
+            incoming(2 * pair + 1).wait_recv()
+
+        @pl.when(jnp.logical_and(index >= 1, index + 2 < groups))
+        def _():
+            send_group(index + 2)
+
+        @pl.when(index == 1)
+        def _():
+            going_back(neighbour).start()
+
+        @pl.when(index > 1)
+        def _():
+            send_back_group(index - 1)
+
+        here = pl.ds(pl.multiple_of(pair * 2 * padded, 16), 2 * padded)
+        for side in range(2):
+            spot = place(2 * pair + side)
+            gate = gate_columns(2 * pair + side)
+            gated[spot, :] = (gate * grads[spot, :].astype(jnp.float32)).astype(jnp.bfloat16)
+
+        def hidden_step(step, inner):
+            columns = pl.ds(pl.multiple_of(step * block, block), block)
+            pre = (
+                jnp.dot(slots[here, :], weight_in[:, columns], preferred_element_type=jnp.float32)
+                + b_in_ref[:, columns]
+            )
+            grad_active = lax.dot_general(
+                gated[here, :],
+                weight_back[columns, :],
+                contract_last,
+                preferred_element_type=jnp.float32,
+            )
+            cumulative = 0.5 * (1.0 + lax.erf(pre * root_half))
+            slope = cumulative + pre * inverse_root_tau * jnp.exp(-0.5 * pre * pre)
+            active_low = (pre * cumulative).astype(jnp.bfloat16)
+            grad_low = (grad_active * slope).astype(jnp.bfloat16)
+            active[here, columns] = active_low
+            grad_pre[here, columns] = grad_low
+            result_part = jnp.dot(
+                active_low, weight_back[columns, :], preferred_element_type=jnp.float32
+            )
+            back_part = lax.dot_general(
+                grad_low, weight_in[:, columns], contract_last, preferred_element_type=jnp.float32
+            )
+
+            @pl.when(step == 0)
+            def _():
+                result_total[...] = result_part
+                back_total[...] = back_part
+
+            @pl.when(step > 0)
+            def _():
+                result_total[...] += result_part
+                back_total[...] += back_part
+
+            return inner
+
+        lax.fori_loop(0, steps, hidden_step, 0)
+        for side in range(2):
+            expert = 2 * pair + side
+            span = slice(side * padded, (side + 1) * padded)
+            spot = place(expert)
+            result_low = (result_total[span, :] + b_back_ref[...]).astype(jnp.bfloat16)
+            result_rows[spot, :] = result_low
+            grad_gate = jnp.sum(
+                grads[spot, :].astype(jnp.float32) * result_low.astype(jnp.float32),
+                axis=1,
+                keepdims=True,
+            )
+            gate_line = row_of(
+                jnp.where(
+                    lax.broadcasted_iota(jnp.int32, (padded, 1), 0) < capacity, grad_gate, 0.0
+                ),
+                lanes,
+            )
+            if lanes < D:
+                gate_line = jnp.concatenate(
+                    [gate_line, jnp.zeros((1, D - lanes), jnp.float32)], axis=1
+                )
+            high, middle, lowest = three_terms(gate_line)
+            row = lax.broadcasted_iota(jnp.int32, (padded, D), 0)
+            value = back_total[span, :]
+            value = jnp.where(row == capacity, high, value)
+            value = jnp.where(row == capacity + 1, middle, value)
+            value = jnp.where(row == capacity + 2, lowest, value)
+            back_rows[spot, :] = value.astype(jnp.bfloat16)
+        return carry
+
+    lax.fori_loop(0, groups, group_step, 0)
+    if groups > 1:
+        send_back_group(groups - 1)
+    else:
+        going_back(neighbour).start()
+    own_back = pltpu.make_async_copy(back_rows.at[place(mine)], return_ref.at[mine], load_sem.at[0])
+    own_back.start()
+    results = pltpu.make_async_copy(result_rows, result_ref, result_sem)
+    results.start()
+
+    sum_b_back_ref[...] = jnp.sum(gated[...].astype(jnp.float32), axis=0, keepdims=True)
+
+    def stages(step, slot):
+        columns = pl.ds(pl.multiple_of(step * block, block), block)
+        return (
+            pltpu.make_async_copy(stage_back.at[slot], sum_back_ref.at[columns, :], stage_sem.at[0, slot]),
+            pltpu.make_async_copy(stage_in.at[slot], sum_in_ref.at[:, columns], stage_sem.at[1, slot]),
+        )
+
+    def sum_step(step, carry):
+        columns = pl.ds(pl.multiple_of(step * block, block), block)
+        slot = lax.rem(step, 2)
+
+        @pl.when(step >= 2)
+        def _():
+            for copy in stages(step - 2, slot):
+                copy.wait()
+
+        stage_back[slot] = lax.dot_general(
+            active[:, columns], gated[...], contract_first, preferred_element_type=jnp.float32
+        ).astype(jnp.bfloat16)
+        stage_in[slot] = lax.dot_general(
+            slots[...], grad_pre[:, columns], contract_first, preferred_element_type=jnp.float32
+        ).astype(jnp.bfloat16)
+        sum_b_in_ref[:, columns] = jnp.sum(
+            grad_pre[:, columns].astype(jnp.float32), axis=0, keepdims=True
+        )
+        for copy in stages(step, slot):
+            copy.start()
+        return carry
+
+    lax.fori_loop(0, steps, sum_step, 0)
+    for step in range(max(steps - 2, 0), steps):
+        for copy in stages(step, step % 2):
+            copy.wait()
+    own_back.wait()
+    results.wait()
+
+    def finish(step, carry):
+        other = lax.rem(mine + step, experts)
+        outgoing(other).wait_send()
+        going_back(other).wait_send()
+        coming_back(other).wait_recv()
+        return carry
+
+    lax.fori_loop(1, experts, finish, 0)
+
+
+def run_experts(buffer, grads, w_in, w_back, b_in, b_back, capacity):
+    experts, padded = (buffer.shape[0], buffer.shape[1])
+    hidden = w_in.shape[1]
+    block = 512
+    rows = experts * padded
+    low = jnp.bfloat16
+    anywhere = pl.BlockSpec(memory_space=pl.ANY)
+    inside = pl.BlockSpec(memory_space=pltpu.VMEM)
+    return pl.pallas_call(
+        functools.partial(expert_kernel, experts, capacity, padded, block),
+        out_shape=[
+            jax.ShapeDtypeStruct((experts, padded, D), low),
+            jax.ShapeDtypeStruct((rows, D), low),
+            jax.ShapeDtypeStruct((hidden, D), low),
+            jax.ShapeDtypeStruct((D, hidden), low),
+            jax.ShapeDtypeStruct((1, hidden), jnp.float32),
+            jax.ShapeDtypeStruct((1, D), jnp.float32),
+        ],
+        in_specs=[anywhere, anywhere, anywhere, anywhere, inside, inside],
+        out_specs=[anywhere, anywhere, anywhere, anywhere, inside, inside],
+        scratch_shapes=[
+            pltpu.VMEM((rows, D), low),
+            pltpu.VMEM((rows, D), low),
+            pltpu.VMEM((rows, D), low),
+            pltpu.VMEM((D, hidden), low),
+            pltpu.VMEM((hidden, D), low),
+            pltpu.VMEM((rows, hidden), low),
+            pltpu.VMEM((rows, hidden), low),
+            pltpu.VMEM((rows, D), low),
+            pltpu.VMEM((rows, D), low),
+            pltpu.VMEM((2 * padded, D), jnp.float32),
+            pltpu.VMEM((2 * padded, D), jnp.float32),
+            pltpu.VMEM((2, block, D), low),
+            pltpu.VMEM((2, D, block), low),
+            pltpu.SemaphoreType.DMA((4,)),
+            pltpu.SemaphoreType.DMA((experts,)),
+            pltpu.SemaphoreType.DMA((experts,)),
+            pltpu.SemaphoreType.DMA((experts,)),
+            pltpu.SemaphoreType.DMA((experts,)),
+            pltpu.SemaphoreType.DMA,
+            pltpu.SemaphoreType.DMA((2, 2)),
+        ],
+        compiler_params=pltpu.CompilerParams(
+            collective_id=2, has_side_effects=True, vmem_limit_bytes=60 * 1024 * 1024
+        ),
+        cost_estimate=pl.CostEstimate(
+            flops=12 * rows * D * hidden, bytes_accessed=40 << 20, transcendentals=2 * rows * hidden
+        ),
+        name="experts",
+    )(buffer, grads.reshape(rows, D), w_in, w_back, b_in.astype(jnp.float32), b_back.astype(jnp.float32))
+
+
 def exchange(blocks):
     return lax.all_to_all(blocks, "exp", split_axis=0, concat_axis=0, tiled=True)
 
@@ -446,6 +817,7 @@
     reps = lax.axis_size("rep")
     devices = experts * reps
     capacity = (TOK_DEV * 210 + experts * 100 - 1) // (experts * 100)
+    padded = -(-(capacity + 3) // 16) * 16
     rows = w_qkv.shape[0]
     small = jnp.concatenate(
         [w_router, jnp.stack([ln1_gain, ln1_bias, ln2_gain, ln2_bias], axis=1)], axis=1
@@ -460,14 +832,14 @@
     gain_one, bias_one, gain_two, bias_two = (vectors[0], vectors[1], vectors[2], vectors[3])
 
     first_hot, second_hot, pick_first, pick_second = dispatch_tables(
-        routes, priority, padding, experts, capacity
+        routes, priority, padding, experts, capacity, padded
     )
     picks = pick_first + pick_second
     grad_blocks = lax.dot_general(picks, cotangent, contract_first, preferred_element_type=jnp.float32)
-    grad_blocks = grad_blocks.astype(jnp.bfloat16).reshape(experts, capacity, D)
+    grad_blocks = grad_blocks.astype(jnp.bfloat16).reshape(experts, padded, D)
     grad_blocks, gathered_done = lax.optimization_barrier((grad_blocks, qkv_weight))
     qkv_weight = gathered_done
-    grad_arrived = exchange(grad_blocks).reshape(experts * capacity, D)
+    grad_arrived = exchange(grad_blocks)
 
     inputs = tokens.astype(jnp.float32)
     normed, normal_one, inverse_one = norm_forward(inputs, gain_one, bias_one)
@@ -488,52 +860,28 @@
     gate_first = jnp.sum(probs * first_hot, axis=1)
     gate_second = jnp.sum(probs * second_hot, axis=1)
     buffer = lax.dot_general(picks, routed, contract_first, preferred_element_type=jnp.float32)
-    buffer = buffer.astype(jnp.bfloat16).reshape(experts, capacity, D)
-    received = exchange(buffer).reshape(experts * capacity, D)
+    buffer = buffer.astype(jnp.bfloat16).reshape(experts, padded, D)
     slot_gates = jnp.sum(
         pick_first.astype(jnp.float32) * gate_first[:, None]
         + pick_second.astype(jnp.float32) * gate_second[:, None],
         axis=0,
-    )
-    gates = exchange(slot_gates.reshape(experts, capacity)).reshape(experts * capacity, 1)
-
-    first_weight, second_weight = (w_in[0], w_back[0])
-    pre = jnp.dot(received, first_weight, preferred_element_type=jnp.float32) + b_in[0].astype(
-        jnp.float32
-    )
-    active = jax.nn.gelu(pre, approximate=False).astype(jnp.bfloat16)
-    grad_results = (gates * grad_arrived.astype(jnp.float32)).astype(jnp.bfloat16)
-    grad_active = lax.dot_general(
-        grad_results, second_weight, contract_last, preferred_element_type=jnp.float32
-    )
-    grad_pre = (grad_active * gelu_slope(pre)).astype(jnp.bfloat16)
-    result = (
-        jnp.dot(active, second_weight, preferred_element_type=jnp.float32)
-        + b_back[0].astype(jnp.float32)
-    ).astype(jnp.bfloat16)
-    grad_received = lax.dot_general(
-        grad_pre, first_weight, contract_last, preferred_element_type=jnp.float32
-    ).astype(jnp.bfloat16)
-    slot_grad_gates = jnp.sum(grad_arrived.astype(jnp.float32) * result.astype(jnp.float32), axis=1)
-    grad_gate_slots = exchange(slot_grad_gates.reshape(experts, capacity)).reshape(
-        1, experts * capacity
-    )
-    grad_buffer = exchange(grad_received.reshape(experts, capacity, D)).reshape(
-        experts * capacity, D
-    )
-    returned = exchange(result.reshape(experts, capacity, D)).reshape(experts * capacity, D)
-
-    grad_w_back = lax.dot_general(
-        active, grad_results, contract_first, preferred_element_type=jnp.float32
-    ).astype(jnp.bfloat16)
-    grad_w_in = lax.dot_general(
-        received, grad_pre, contract_first, preferred_element_type=jnp.float32
-    ).astype(jnp.bfloat16)
-    grad_b_back = jnp.sum(grad_results.astype(jnp.float32), axis=0)
-    grad_b_in = jnp.sum(grad_pre.astype(jnp.float32), axis=0)
+    ).reshape(experts, padded)[:, :capacity]
+    high = lax.reduce_precision(slot_gates, 8, 7)
+    middle = lax.reduce_precision(slot_gates - high, 8, 7)
+    terms = jnp.stack([high, middle, slot_gates - high - middle], axis=1).astype(jnp.bfloat16)
+    terms = jnp.pad(terms, ((0, 0), (0, padded - capacity - 3), (0, D - capacity)))
+    buffer = lax.dynamic_update_slice(buffer, terms, (0, capacity, 0))
+    grad_buffer, result, grad_w_back, grad_w_in, grad_b_in, grad_b_back = run_experts(
+        buffer, grad_arrived, w_in[0], w_back[0], b_in, b_back, capacity
+    )
+    returned = exchange(result.reshape(experts, padded, D)).reshape(experts * padded, D)
+    grad_gate_slots = jnp.sum(
+        grad_buffer[:, capacity : capacity + 3, :padded].astype(jnp.float32), axis=1
+    ).reshape(1, experts * padded)
+    grad_buffer = grad_buffer.reshape(experts * padded, D)
     back_total = rep_spread(rep_reduce(grad_w_back, reps), reps).astype(jnp.float32)
     in_total = rep_spread(rep_reduce(grad_w_in, reps), reps).astype(jnp.float32)
-    bias_total = rep_total(jnp.concatenate([grad_b_in, grad_b_back]).reshape(-1, LANES), reps)
+    bias_total = rep_total(jnp.concatenate([grad_b_in[0], grad_b_back[0]]).reshape(-1, LANES), reps)
     bias_total = bias_total.reshape(-1)
 
     grad_out = cotangent.astype(jnp.float32)

time: 529 us -> 499 us (0.943)
  Pallas kernels: 90.7 us -> 175 us
  matrix products: 178 us -> 102 us
  waiting for transfers between devices: 117 us -> 83.3 us
    dot_general x6 -> x0, matrix products: 90.3 us -> none  [the longest x1 41.5 us: on_device(): jnp.dot(received, first_weight, preferred_element_type=jnp.float32)]
    pallas_call x0 -> x1, Pallas kernels: none -> 83.7 us  [run_experts(): pl.pallas_call(functools.partial(expert_kernel, experts, capacity, padded...]
    all_to_all x6 -> x2, waiting for transfers between devices: 80.6 us -> 0.01 us  [exchange(): lax.all_to_all(blocks, 'exp', split_axis=0, concat_axis=0, tiled=True)]
    ppermute x4, waiting for transfers between devices: 0.01 us -> 40.7 us  [rep_reduce(): arrived = lax.ppermute(away, 'rep', rep_pairs(reps, bit))]
    ppermute x4, waiting for transfers between devices: 36.3 us -> 42.4 us  [rep_spread(): arrived = lax.ppermute(piece, 'rep', rep_pairs(reps, bit))]
    all_to_all x6 -> x2, starting transfers between devices: 29.3 us -> 25.6 us  [exchange(): lax.all_to_all(blocks, 'exp', split_axis=0, concat_axis=0, tiled=True)]
  transfers between devices with their start and end apart: 16 -> 12, of which waited for: 7 -> 5; matrix products, arithmetic and copies ran while one was open for 36% -> 24% of each run, Pallas kernels for 10% -> 11%
where the time goes in v2:
time: 499 us; the launch traced here: 490 us
  Pallas kernels  175 us (35%)
  matrix products  102 us (20%)
  waiting for transfers between devices  83.3 us (17%)
  other arithmetic  64.1 us (13%)
  local copies, waits for them, and re-layouts  33.8 us (7%)
  starting transfers between devices  30.2 us (6%)
    pallas_call x1, Pallas kernels, run_experts(): pl.pallas_call(functools.partial(expert_kernel, experts, capacity, padded...  83.7 us
    pallas_call x1, Pallas kernels, scatter_sums(): pl.pallas_call(functools.partial(scatter_kernel, devices, reps, chunks, l...  54.2 us
    ppermute x4, waiting for transfers between devices, rep_spread(): arrived = lax.ppermute(piece, 'rep', rep_pairs(reps, bit))  42.4 us
    ppermute x4, waiting for transfers between devices, rep_reduce(): arrived = lax.ppermute(away, 'rep', rep_pairs(reps, bit))  40.7 us
    pallas_call x1, Pallas kernels, gather_blocks(): pl.pallas_call(functools.partial(gather_kernel, devices, reps), out_shape...  37.4 us
    all_to_all x2, starting transfers between devices, exchange(): lax.all_to_all(blocks, 'exp', split_axis=0, concat_axis=0, tiled=True)  25.6 us
    dot_general x1, matrix products, attend_backward(): jnp.einsum('qhc,khc->hqk', grad_mixed, values, preferred_element_type=jnp...  16.1 us
    convert_element_type x1, other arithmetic, attend_backward(): grad_scores = (probs * (grad_probs - jnp.sum(probs * grad_probs, axis=-1,...  12.3 us
  transfers between devices with their start and end apart: 12, of which 5 were waited for; matrix products, arithmetic and copies ran while one was open for 24% of the time, Pallas kernels for 11%

profile of v2, /device:TPU:0, one launch (start us, length us, event | category | flops | bytes accessed | tf_op | source)
XLA Modules:
  0.0 490.5 jit_solution(10298729734067701370)
XLA Ops:
  2.2 1.2 fusion.68
  4.1 0.8 add_reduce_fusion.1
  4.9 1.2 fusion.65
  6.8 0.8 copy.106
  7.6 0.7 copy.107
  8.3 0.7 copy.108
  9.0 0.7 copy.109
  9.8 0.7 copy.110
  10.6 1.6 fusion.87.own_ref
  12.2 37.4 %gather_dense.1 = bf16[32,24,3200]{2,1,0:T(8,128)(2,1)} custom-call(bf16[24,3200]{1,0:T(8,128)(2,1)} %fusion.87.own_ref), custom_call_target="tpu_custom_call" | custom-call | tf_op jit(solution)/shard_map/gather_dense/pallas_call | solution.py:226
  49.6 4.1 slice.103
  53.7 3.7 convolution_convert_fusion.3
  57.5 6.0 %all-to-all-start = ((bf16[8,160,768]{2,1,0:T(8,128)(2,1)}), bf16[8,160,768]{2,1,0:T(8,128)(2,1)}, u32[]{:S(2)}, u32[]{:S(2)}) async-start(bf16[8,160,768]{2,1,0:T(8,128)(2,1)} %bitcast.100), calls=%async_computation | async-start | bytes 3932160 | tf_op jit(solution)/shard_map/all_to_all | solution.py:794
  63.5 1.0 slice.100
  65.4 4.4 convolution_convert_fusion.1
  69.8 1.1 fusion.127
  70.9 1.3 copy.112
  72.8 1.9 copy.114
  75.3 7.9 %fusion.128 = (f32[12,576]{1,0:T(8,128)S(1)}, f32[12,576,576]{1,2,0:T(8,128)}) fusion(bf16[576,12,64]{0,2,1:T(8,128)(2,1)S(1)} %bitcast.92, bf16[576,12,64]{0,2,1:T(8,128)(2,1)S(1)} %bitcast.88, pred[576,576]{0,1:T(8,128)(4,1)S(1)} %fusion.46), kind=kOutput, calls=%fused_computation.198 | convolution fusion | flops 521544960 | bytes 18054144 | tf_op jit(solution)/shard_map/qhc,khc->hqk/dot_general | solution.py:65
  83.3 8.6 %fusion = f32[12,576]{1,0:T(8,128)S(1)} fusion(f32[12,576,576]{1,2,0:T(8,128)} %get-tuple-element.131, f32[12,576]{1,0:T(8,128)S(1)} %get-tuple-element.130), kind=kLoop, calls=%fused_computation.6 | loop fusion | flops 7955712 | bytes 15980544 | tf_op jit(solution)/shard_map/reduce_sum | solution.py:76
  92.0 10.3 %fusion.47 = bf16[12,64,576]{2,1,0:T(8,128)(2,1)} fusion(bf16[576,12,64]{0,2,1:T(8,128)(2,1)S(1)} %bitcast.95, f32[12,576,576]{1,2,0:T(8,128)} %get-tuple-element.131, f32[12,576]{1,0:T(8,128)S(1)} %fusion, f32[12,576]{1,0:T(8,128)S(1)} %get-tuple-element.130), kind=kOutput, calls=%fused_computation.84 | convolution fusion | flops 521994240 | bytes 17750016 | tf_op jit(solution)/shard_map/hqk,khc->qhc/dot_general | solution.py:78
  102.3 2.8 fusion.129
  105.8 0.9 copy-done.5
  106.7 1.3 fusion.130
  108.1 1.5 fusion.9
  111.0 3.6 convolution_convert_fusion.2
  114.6 1.3 copy-done.21
  115.9 83.7 %experts.1 = (bf16[8,160,768]{2,1,0:T(8,128)(2,1)}, bf16[1280,768]{1,0:T(8,128)(2,1)}, bf16[3072,768]{1,0:T(8,128)(2,1)}, bf16[768,3072]{1,0:T(8,128)(2,1)}, f32[1,3072]{1,0:T(1,128)}, /*index=5*/f32[1,768]{1,0:T(1,128)}) custom-call(bf16[8,160,768]{2,1,0:T(8,128)(2,1)} %copy-done.21, bf16[1280,768]{1,0:T(8,128)(2,1)} %bitcast.17.grad_ref, ...), custom_call_target="tpu_custom_call" | custom-call | flops 36238786560 | bytes 41943040 | tf_op jit(solution)/shard_map/experts/pallas_call | solution.py:749
  199.6 0.8 convert_reduce_fusion.1
  200.4 4.8 fusion.52
  205.3 1.5 fusion.10
  206.8 2.8 multiply_reduce_fusion.1
  210.3 1.2 copy-done.7
  211.5 3.1 convolution_convert_fusion.5
  214.6 2.4 copy.119
  217.0 16.1 %multiply_reduce_fusion = (f32[12,576]{1,0:T(8,128)S(1)}, f32[12,576,576]{1,2,0:T(8,128)}) fusion(f32[12,576,576]{1,2,0:T(8,128)} %get-tuple-element.131, f32[12,576]{1,0:T(8,128)S(1)} %log_add_fusion, bf16[576,12,64]{0,2,1:T(8,128)(2,1)} %bitcast.90, bf16[576,12,64]{0,2,1:T(8,128)(2,1)} %bitcast.94), kind=kOutput, calls=%fused_computation.1 | convolution fusion | flops 521544960 | bytes 33675264 | tf_op jit(solution)/shard_map/qhc,khc->hqk/dot_general | solution.py:86
  233.1 12.3 %multiply_convert_fusion = bf16[12,576,576]{1,2,0:T(8,128)(2,1)S(1)} fusion(f32[12,576,576]{1,2,0:T(8,128)} %get-tuple-element.138, f32[12,576,576]{1,2,0:T(8,128)} %get-tuple-element.131, f32[12,576]{1,0:T(8,128)S(1)} %get-tuple-element.137, f32[12,576]{1,0:T(8,128)S(1)} %log_add_fusion), kind=kLoop, calls=%fused_computation | loop fusion | flops 15925248 | bytes 39868416 | tf_op jit(solution)/shard_map/convert_element_type | solution.py:92
  245.4 3.7 multiply_convert_fusion.1
  249.2 3.2 constant_dynamic-slice_fusion.3
  252.4 3.3 constant_dynamic-slice_fusion.1
  256.2 9.8 %fusion.48 = bf16[12,64,576]{2,1,0:T(8,128)(2,1)} fusion(bf16[576,12,64]{0,2,1:T(8,128)(2,1)S(1)} %bitcast.91, f32[12,576,576]{1,2,0:T(8,128)} %get-tuple-element.131, f32[12,576]{1,0:T(8,128)S(1)} %log_add_fusion), kind=kOutput, calls=%fused_computation.85 | convolution fusion | flops 518012928 | bytes 17722368 | tf_op jit(solution)/shard_map/hqk,qhc->khc/dot_general | solution.py:87
  265.9 2.6 multiply_convert_fusion.2
  268.6 19.5 %all-to-all-start.1 = ((bf16[8,160,768]{2,1,0:T(8,128)(2,1)}), bf16[8,160,768]{2,1,0:T(8,128)(2,1)}, u32[]{:S(2)}, u32[]{:S(2)}) async-start(bf16[8,160,768]{2,1,0:T(8,128)(2,1)} %bitcast.99), calls=%async_computation.1 | async-start | bytes 3932160 | tf_op jit(solution)/shard_map/all_to_all | solution.py:794
  288.2 6.0 %fusion.37 = (bf16[768]{0:T(1024)(128)(2,1)S(1)}, f32[576]{0:T(1024)S(1)}, f32[576]{0:T(1024)S(1)}, bf16[768]{0:T(1024)(128)(2,1)S(1)}, f32[576,768]{1,0:T(8,128)S(1)}) fusion(bf16[576,768]{1,0:T(8,128)(2,1)S(1)} %copy-done.4, f32[576]{0:T(1024)S(1)} %add_rsqrt_fusion.1, f32[576]{0:T(1024)S(1)} %broadcast_multiply_fusion.5, ...), kind=kOutput, calls=%fused_computation.64 | convolution fusion | flops 2050815488 | bytes 8862720 | tf_op jit(solution)/shard_map/dot_general | solution.py:917
  294.2 3.3 add_convert_fusion.1
  298.2 3.0 add_convert_fusion
  301.3 1.4 collective-permute-start.7
  302.8 23.6 %collective-permute-done.1 = bf16[192,3072]{1,0:T(8,128)(2,1)S(1)} collective-permute-done((bf16[192,3072]{1,0:T(8,128)(2,1)S(1)}, bf16[192,3072]{1,0:T(8,128)(2,1)S(1)}, u32[]{:S(2)}, u32[]{:S(2)}) %collective-permute-start.1) | collective-permute-done | bytes 1179680 | tf_op jit(solution)/shard_map/ppermute | solution.py:397
  327.6 7.1 %convolution_convert_fusion = bf16[768,2304]{1,0:T(8,128)(2,1)} fusion(bf16[576,768]{0,1:T(8,128)(2,1)S(1)} %bitcast.103, bf16[576,768]{0,1:T(8,128)(2,1)S(1)} %bitcast.105, bf16[576,768]{0,1:T(8,128)(2,1)S(1)} %bitcast.98, bf16[576,768]{1,0:T(8,128)(2,1)S(1)} %copy-done.4, f32[768]{0:T(1024)S(1)} %get-tuple-element.118, f32[768]{0:T(1024)S(1)} %get-tuple-element.119, ...), kind=kOutput, calls=%fused_computation.11 | convolution fusion | flops 2050818048 | bytes 7088640 | tf_op jit(solution)/shard_map/dot_general | solution.py:914
  334.7 17.0 %collective-permute-done.7 = bf16[768,768]{1,0:T(8,128)(2,1)S(1)} collective-permute-done((bf16[768,768]{1,0:T(8,128)(2,1)S(1)}, bf16[768,768]{1,0:T(8,128)(2,1)S(1)}, u32[]{:S(2)}, u32[]{:S(2)}) %collective-permute-start.7) | collective-permute-done | bytes 1179680 | tf_op jit(solution)/shard_map/ppermute | solution.py:397
  352.8 1.8 fusion.36
  354.6 22.4 %collective-permute-done.2 = bf16[192,3072]{1,0:T(8,128)(2,1)S(1)} collective-permute-done((bf16[192,3072]{1,0:T(8,128)(2,1)S(1)}, bf16[192,3072]{1,0:T(8,128)(2,1)S(1)}, u32[]{:S(2)}, u32[]{:S(2)}) %collective-permute-start.2) | collective-permute-done | bytes 1179680 | tf_op jit(solution)/shard_map/ppermute | solution.py:406
  377.0 1.9 maximum_select_fusion.2
  378.9 2.1 convolution_convert_fusion.4
  381.1 20.0 %collective-permute-done.8 = bf16[768,768]{1,0:T(8,128)(2,1)S(1)} collective-permute-done((bf16[768,768]{1,0:T(8,128)(2,1)S(1)}, bf16[768,768]{1,0:T(8,128)(2,1)S(1)}, u32[]{:S(2)}, u32[]{:S(2)}) %collective-permute-start.8) | collective-permute-done | bytes 1179680 | tf_op jit(solution)/shard_map/ppermute | solution.py:406
  401.0 1.8 maximum_select_fusion.3
  403.4 0.7 pad.15.clone
  404.1 54.2 %scatter_dense.1 = (f32[24,2304]{1,0:T(8,128)}, f32[24,768]{1,0:T(8,128)}, f32[24,128]{1,0:T(8,128)}) custom-call(bf16[4,8,24,2304]{3,2,1,0:T(8,128)(2,1)} %bitcast.96, bf16[4,8,24,768]{3,2,1,0:T(8,128)(2,1)} %bitcast.101, bf16[4,8,24,128]{3,2,1,0:T(8,128)(2,1)} %bitcast.106), custom_call_target="tpu_custom_call" | custom-call | tf_op jit(solution)/shard_map/scatter_dense/pallas_call | solution.py:368
  458.9 1.6 slice_reduce_fusion
  460.5 1.4 copy.124
  463.3 3.1 fusion.13
  466.4 4.2 add_convert_fusion.4
  470.6 9.4 %fusion.6 = f32[1,768,3072]{2,1,0:T(8,128)} fusion(bf16[1,384,3072]{2,1,0:T(8,128)(2,1)} %bitcast.35, bf16[1,384,3072]{2,1,0:T(8,128)(2,1)} %bitcast.34, pred[]{:T(512)S(6)} %eq.133), kind=kLoop, calls=%fused_computation.13 | loop fusion | flops 23592960 | bytes 14155777 | tf_op jit(solution)/shard_map/convert_element_type | solution.py:883
  480.1 8.7 %fusion.7 = f32[1,3072,768]{2,1,0:T(8,128)} fusion(bf16[1,1536,768]{2,1,0:T(8,128)(2,1)} %bitcast.40, bf16[1,1536,768]{2,1,0:T(8,128)(2,1)} %bitcast.39, pred[]{:T(512)S(6)} %eq.133), kind=kLoop, calls=%fused_computation.15 | loop fusion | flops 23592960 | bytes 14155777 | tf_op jit(solution)/shard_map/convert_element_type | solution.py:882
  (123 shorter events, 15.5 us)
Async XLA Ops:
  49.6 4.1 copy-start.13
  57.5 7.3 %copy-start.3 = (bf16[576,768]{1,0:T(8,128)(2,1)S(1)}, bf16[576,768]{1,0:T(8,128)(2,1)}, u32[]{:S(2)}) copy-start(bf16[576,768]{1,0:T(8,128)(2,1)} %param.17) | copy-start | bytes 2654212
  57.5 58.4 %all-to-all-start = ((bf16[8,160,768]{2,1,0:T(8,128)(2,1)}), bf16[8,160,768]{2,1,0:T(8,128)(2,1)}, u32[]{:S(2)}, u32[]{:S(2)}) async-start(bf16[8,160,768]{2,1,0:T(8,128)(2,1)} %bitcast.100), calls=%async_computation | async-start | bytes 3932160 | tf_op jit(solution)/shard_map/all_to_all | solution.py:794
  70.9 3.8 copy-start.22
  72.8 10.5 %copy-start.1 = (bf16[576,768]{0,1:T(8,128)(2,1)}, bf16[576,768]{0,1:T(8,128)(2,1)S(1)}, u32[]{:S(2)}) copy-start(bf16[576,768]{0,1:T(8,128)(2,1)S(1)} %copy.113) | copy-start | bytes 2654212
  83.3 8.6 %copy-start.9 = (bf16[576,768]{0,1:T(8,128)(2,1)S(1)}, bf16[576,768]{0,1:T(8,128)(2,1)}, u32[]{:S(2)}) copy-start(bf16[576,768]{0,1:T(8,128)(2,1)} %copy.112) | copy-start | bytes 2654212
  105.4 4.3 copy-start.18
  105.5 4.9 %copy-start.19 = (bf16[1,768]{1,0:T(2,128)(2,1)S(1)}, bf16[1,768]{1,0:T(2,128)(2,1)}, u32[]{:S(2)}) copy-start(bf16[1,768]{1,0:T(2,128)(2,1)} %param.28) | copy-start | bytes 4612
  105.8 0.9 copy-start.5
  114.6 1.3 copy-start.21
  206.8 2.8 copy-start.14
  210.3 1.2 copy-start.7
  233.1 12.3 %copy-start.2 = (bf16[576,768]{0,1:T(8,128)(2,1)S(1)}, bf16[576,768]{0,1:T(8,128)(2,1)}, u32[]{:S(2)}) copy-start(bf16[576,768]{0,1:T(8,128)(2,1)} %copy-done.1) | copy-start | bytes 2654212
  252.4 41.8 %collective-permute-start = (bf16[384,3072]{1,0:T(8,128)(2,1)}, bf16[384,3072]{1,0:T(8,128)(2,1)}, u32[]{:S(2)}, u32[]{:S(2)}) collective-permute-start(bf16[384,3072]{1,0:T(8,128)(2,1)} %constant_dynamic-slice_fusion.3), channel_id=1, source_target_pairs={{0,1},{1,0},{2,3},{3,2},{4,5},{5,4},{6,7},{7,6},{8,9},{9,8},{10,11... | collective-permute-start | bytes 7077896 | tf_op jit(solution)/shard_map/ppermute | solution.py:397
  252.4 3.8 copy-start
  255.7 42.6 %collective-permute-start.6 = (bf16[1536,768]{1,0:T(8,128)(2,1)}, bf16[1536,768]{1,0:T(8,128)(2,1)}, u32[]{:S(2)}, u32[]{:S(2)}) collective-permute-start(bf16[1536,768]{1,0:T(8,128)(2,1)} %constant_dynamic-slice_fusion.1), channel_id=1, source_target_pairs={{0,1},{1,0},{2,3},{3,2},{4,5},{5,4},{6,7},{7,6},{8,9},{9,8},{10,11... | collective-permute-start | bytes 7077896 | tf_op jit(solution)/shard_map/ppermute | solution.py:397
  268.6 19.6 %copy-start.20 = (f32[1,768]{1,0:T(1,128)S(1)}, f32[1,768]{1,0:T(1,128)}, u32[]{:S(2)}) copy-start(f32[1,768]{1,0:T(1,128)} %get-tuple-element.33) | copy-start | bytes 9220
  268.6 19.6 %copy-start.4 = (bf16[576,768]{1,0:T(8,128)(2,1)S(1)}, bf16[576,768]{1,0:T(8,128)(2,1)}, u32[]{:S(2)}) copy-start(bf16[576,768]{1,0:T(8,128)(2,1)} %param.17) | copy-start | bytes 2654212
  268.6 194.7 %all-to-all-start.1 = ((bf16[8,160,768]{2,1,0:T(8,128)(2,1)}), bf16[8,160,768]{2,1,0:T(8,128)(2,1)}, u32[]{:S(2)}, u32[]{:S(2)}) async-start(bf16[8,160,768]{2,1,0:T(8,128)(2,1)} %bitcast.99), calls=%async_computation.1 | async-start | bytes 3932160 | tf_op jit(solution)/shard_map/all_to_all | solution.py:794
  297.5 28.9 %collective-permute-start.1 = (bf16[192,3072]{1,0:T(8,128)(2,1)S(1)}, bf16[192,3072]{1,0:T(8,128)(2,1)S(1)}, u32[]{:S(2)}, u32[]{:S(2)}) collective-permute-start(bf16[192,3072]{1,0:T(8,128)(2,1)S(1)} %constant_dynamic-slice_fusion.2), channel_id=1, source_target_pairs={{0,2},{1,3},{2,0},{3,1},{4,6},{5,7},{6,4},{7,5},{8,10},{9,11},{10,... | collective-permute-start | bytes 3538952 | tf_op jit(solution)/shard_map/ppermute | solution.py:397
  301.3 26.2 %copy-start.10 = (bf16[12,64,576]{2,1,0:T(8,128)(2,1)S(1)}, bf16[12,64,576]{2,1,0:T(8,128)(2,1)}, u32[]{:S(2)}) copy-start(bf16[12,64,576]{2,1,0:T(8,128)(2,1)} %multiply_convert_fusion.2) | copy-start | bytes 2654212
  301.3 26.2 %copy-start.11 = (bf16[12,64,576]{2,1,0:T(8,128)(2,1)S(1)}, bf16[12,64,576]{2,1,0:T(8,128)(2,1)}, u32[]{:S(2)}) copy-start(bf16[12,64,576]{2,1,0:T(8,128)(2,1)} %fusion.48) | copy-start | bytes 2654212
  301.3 26.2 %copy-start.12 = (bf16[12,64,576]{2,1,0:T(8,128)(2,1)S(1)}, bf16[12,64,576]{2,1,0:T(8,128)(2,1)}, u32[]{:S(2)}) copy-start(bf16[12,64,576]{2,1,0:T(8,128)(2,1)} %multiply_convert_fusion.1) | copy-start | bytes 2654212
  301.3 50.4 %collective-permute-start.7 = (bf16[768,768]{1,0:T(8,128)(2,1)S(1)}, bf16[768,768]{1,0:T(8,128)(2,1)S(1)}, u32[]{:S(2)}, u32[]{:S(2)}) collective-permute-start(bf16[768,768]{1,0:T(8,128)(2,1)S(1)} %constant_dynamic-slice_fusion), channel_id=1, source_target_pairs={{0,2},{1,3},{2,0},{3,1},{4,6},{5,7},{6,4},{7,5},{8,10},{9,11},{10,... | collective-permute-start | bytes 3538952 | tf_op jit(solution)/shard_map/ppermute | solution.py:397
  326.8 50.1 %collective-permute-start.2 = (bf16[192,3072]{1,0:T(8,128)(2,1)S(1)}, bf16[192,3072]{1,0:T(8,128)(2,1)S(1)}, u32[]{:S(2)}, u32[]{:S(2)}) collective-permute-start(bf16[192,3072]{1,0:T(8,128)(2,1)S(1)} %add_convert_fusion.3), channel_id=1, source_target_pairs={{0,2},{1,3},{2,0},{3,1},{4,6},{5,7},{6,4},{7,5},{8,10},{9,11},{10,... | collective-permute-start | bytes 3538952 | tf_op jit(solution)/shard_map/ppermute | solution.py:406
  334.7 18.1 %copy-start.16 = (f32[1,3072]{1,0:T(1,128)S(1)}, f32[1,3072]{1,0:T(1,128)}, u32[]{:S(2)}) copy-start(f32[1,3072]{1,0:T(1,128)} %get-tuple-element.32) | copy-start | bytes 36868
  334.7 18.1 %copy-start.8 = (f32[576,768]{1,0:T(8,128)S(1)}, f32[576,768]{1,0:T(8,128)}, u32[]{:S(2)}) copy-start(f32[576,768]{1,0:T(8,128)} %copy-done.7) | copy-start | bytes 5308420
  352.0 49.0 %collective-permute-start.8 = (bf16[768,768]{1,0:T(8,128)(2,1)S(1)}, bf16[768,768]{1,0:T(8,128)(2,1)S(1)}, u32[]{:S(2)}, u32[]{:S(2)}) collective-permute-start(bf16[768,768]{1,0:T(8,128)(2,1)S(1)} %add_convert_fusion.2), channel_id=1, source_target_pairs={{0,2},{1,3},{2,0},{3,1},{4,6},{5,7},{6,4},{7,5},{8,10},{9,11},{10,... | collective-permute-start | bytes 3538952 | tf_op jit(solution)/shard_map/ppermute | solution.py:406
  352.8 105.5 %collective-permute-start.4 = (f32[30,128]{1,0:T(8,128)S(1)}, f32[30,128]{1,0:T(8,128)S(1)}, u32[]{:S(2)}, u32[]{:S(2)}) collective-permute-start(f32[30,128]{1,0:T(8,128)S(1)} %maximum_bitcast_fusion), channel_id=1, source_target_pairs={{0,1},{1,0},{2,3},{3,2},{4,5},{5,4},{6,7},{7,6},{8,9},{9,8},{10,11... | collective-permute-start | bytes 46088 | tf_op jit(solution)/shard_map/ppermute | solution.py:417
  354.6 24.3 %copy-start.23 = (bf16[12,64,576]{2,1,0:T(8,128)(2,1)S(1)}, bf16[12,64,576]{2,1,0:T(8,128)(2,1)}, u32[]{:S(2)}) copy-start(bf16[12,64,576]{2,1,0:T(8,128)(2,1)} %fusion.47) | copy-start | bytes 2654212
  378.9 91.7 %collective-permute-start.3 = (bf16[384,3072]{1,0:T(8,128)(2,1)}, bf16[384,3072]{1,0:T(8,128)(2,1)}, u32[]{:S(2)}, u32[]{:S(2)}) collective-permute-start(bf16[384,3072]{1,0:T(8,128)(2,1)} %maximum_select_fusion.2), channel_id=1, source_target_pairs={{0,1},{1,0},{2,3},{3,2},{4,5},{5,4},{6,7},{7,6},{8,9},{9,8},{10,11... | collective-permute-start | bytes 7077896 | tf_op jit(solution)/shard_map/ppermute | solution.py:406
  381.1 21.8 %copy-start.6 = (bf16[576,768]{1,0:T(8,128)(2,1)S(1)}, bf16[576,768]{1,0:T(8,128)(2,1)}, u32[]{:S(2)}) copy-start(bf16[576,768]{1,0:T(8,128)(2,1)} %copy-done.5) | copy-start | bytes 2654212
  402.9 77.2 %collective-permute-start.9 = (bf16[1536,768]{1,0:T(8,128)(2,1)}, bf16[1536,768]{1,0:T(8,128)(2,1)}, u32[]{:S(2)}, u32[]{:S(2)}) collective-permute-start(bf16[1536,768]{1,0:T(8,128)(2,1)} %maximum_select_fusion.3), channel_id=1, source_target_pairs={{0,1},{1,0},{2,3},{3,2},{4,5},{5,4},{6,7},{7,6},{8,9},{9,8},{10,11... | collective-permute-start | bytes 7077896 | tf_op jit(solution)/shard_map/ppermute | solution.py:406
  458.3 3.8 collective-permute-start.5
  480.1 8.7 %copy-start.15 = (f32[24,2304]{1,0:T(8,128)S(1)}, f32[24,2304]{1,0:T(8,128)}, u32[]{:S(2)}) copy-start(f32[24,2304]{1,0:T(8,128)} %get-tuple-element.159) | copy-start | bytes 663556
  480.1 9.4 %copy-start.17 = (f32[24,768]{1,0:T(8,128)S(1)}, f32[24,768]{1,0:T(8,128)}, u32[]{:S(2)}) copy-start(f32[24,768]{1,0:T(8,128)} %get-tuple-element.160) | copy-start | bytes 221188

commit v3 on v2

--- a/solution.py
+++ b/solution.py
@@ -26,81 +26,6 @@
     inverse = lax.rsqrt(jnp.mean(center * center, axis=-1, keepdims=True) + 1e-06)
     normal = center * inverse
     return (normal * gain.astype(jnp.float32) + offset.astype(jnp.float32), normal, inverse)
-
-
-def norm_backward(grad, normal, inverse, gain):
-    scaled = grad * gain.astype(jnp.float32)
-    grad_in = inverse * (
-        scaled
-        - jnp.mean(scaled, axis=-1, keepdims=True)
-        - normal * jnp.mean(scaled * normal, axis=-1, keepdims=True)
-    )
-    return (grad_in, jnp.sum(grad * normal, axis=0), jnp.sum(grad, axis=0))
-
-
-def gelu_slope(pre):
-    return 0.5 * (1.0 + lax.erf(pre * root_half)) + pre * inverse_root_tau * jnp.exp(
-        -0.5 * pre * pre
-    )
-
-
-def row_masks(lengths, padding):
-    bounds = jnp.cumsum(lengths, axis=1)
-    places = jnp.arange(SLOTS, dtype=jnp.int32)
-    segments = jnp.sum((places[None, :, None] >= bounds[:, None, :]).astype(jnp.int32), axis=2)
-    live = padding.reshape(ROWS_DEV, SLOTS) == 1
-    same = segments[:, :, None] == segments[:, None, :]
-    diagonal = places[:, None] == places[None, :]
-    return same & (live[:, None, :] | diagonal[None])
-
-
-def split_heads(qkv_row):
-    query = qkv_row[:, :D].reshape(SLOTS, HEADS, HEAD)
-    keys = qkv_row[:, D : 2 * D].reshape(SLOTS, HEADS, HEAD)
-    values = qkv_row[:, 2 * D :].reshape(SLOTS, HEADS, HEAD)
-    return (query, keys, values)
-
-
-def masked_scores(query, keys, allowed_row):
-    scores = jnp.einsum("qhc,khc->hqk", query, keys, preferred_element_type=jnp.float32) * HEAD ** (
-        -0.5
-    )
-    return jnp.where(allowed_row[None], scores, -1e30)
-
-
-def attend_forward(qkv_row, allowed_row):
-    query, keys, values = split_heads(qkv_row)
-    scores = masked_scores(query, keys, allowed_row)
-    top = jnp.max(scores, axis=-1, keepdims=True)
-    expo = jnp.exp(scores - top)
-    total = jnp.sum(expo, axis=-1, keepdims=True)
-    probs = (expo / total).astype(jnp.bfloat16)
-    mixed = jnp.einsum("hqk,khc->qhc", probs, values, preferred_element_type=jnp.float32)
-    return (mixed.reshape(SLOTS, D), top + jnp.log(total))
-
-
-def attend_backward(qkv_row, allowed_row, lse_row, grad_row):
-    query, keys, values = split_heads(qkv_row)
-    probs = jnp.exp(masked_scores(query, keys, allowed_row) - lse_row)
-    grad_mixed = grad_row.reshape(SLOTS, HEADS, HEAD)
-    grad_probs = jnp.einsum("qhc,khc->hqk", grad_mixed, values, preferred_element_type=jnp.float32)
-    grad_values = jnp.einsum(
-        "hqk,qhc->khc", probs.astype(jnp.bfloat16), grad_mixed, preferred_element_type=jnp.float32
-    )
-    grad_scores = (
-        probs * (grad_probs - jnp.sum(probs * grad_probs, axis=-1, keepdims=True))
-    ).astype(jnp.bfloat16)
-    grad_query = jnp.einsum(
-        "hqk,khc->qhc", grad_scores, keys, preferred_element_type=jnp.float32
-    ) * HEAD ** (-0.5)
-    grad_keys = jnp.einsum(
-        "hqk,qhc->khc", grad_scores, query, preferred_element_type=jnp.float32
-    ) * HEAD ** (-0.5)
-    joined = jnp.concatenate(
-        [grad_query.reshape(SLOTS, D), grad_keys.reshape(SLOTS, D), grad_values.reshape(SLOTS, D)],
-        axis=1,
-    )
-    return joined.astype(jnp.bfloat16)
 
 
 def dispatch_tables(routes, priority, padding, experts, capacity, padded):
@@ -238,187 +163,6 @@
     )(block)
 
 
-def scatter_plan(devices, reps):
-    bits = bit_count(devices)
-    low = min(bit_count(reps) + 1, bits)
-    return (bits, low, list(range(low)) + list(range(bits - 1, low - 1, -1)))
-
-
-def reverse_bits(number, width):
-    return sum((number >> bit & 1) << (width - 1 - bit) for bit in range(width))
-
-
-def scatter_kernel(devices, reps, chunks, arrays, *refs):
-    bits, low, plan = scatter_plan(devices, reps)
-    ins, outs, refs = (refs[:arrays], refs[arrays : 2 * arrays], refs[2 * arrays :])
-    count = len(chunks)
-    owns, refs = (refs[:count], refs[count:])
-    recvs, refs = ([refs[c * bits : (c + 1) * bits] for c in range(count)], refs[count * bits :])
-    send_sem, recv_sem, local_sem = refs
-    me = lax.axis_index("exp") * reps + lax.axis_index("rep")
-    greet(bits, me, reps)
-    high = devices >> low
-    rows = owns[0].shape[1]
-    my_bit = [lax.rem(lax.div(me, 1 << bit), 2) for bit in range(bits)]
-    firsts = 1 << (low - 1)
-    stride = firsts + bits - 1
-
-    def first_copies(c):
-        array, start, width = chunks[c]
-        columns = pl.ds(start, width)
-        copies, local = ([], [])
-        for rest in range(firsts):
-            place = reverse_bits(rest, low - 1) * high
-            index = c * stride + rest
-            copies.append(
-                pltpu.make_async_remote_copy(
-                    src_ref=ins[array].at[:, 2 * rest + 1 - my_bit[0], :, columns],
-                    dst_ref=recvs[c][0].at[pl.ds(place, high)],
-                    send_sem=send_sem.at[index],
-                    recv_sem=recv_sem.at[index],
-                    device_id=coordinates(flip(me, plan[0]), reps),
-                    device_id_type=MESH_ID,
-                )
-            )
-            local.append(
-                pltpu.make_async_copy(
-                    ins[array].at[:, 2 * rest + my_bit[0], :, columns],
-                    owns[c].at[pl.ds(place, high)],
-                    local_sem.at[c * firsts + rest],
-                )
-            )
-        return (copies, local)
-
-    def later_copy(c, phase):
-        half = devices >> (phase + 1)
-        index = c * stride + firsts + phase - 1
-        return pltpu.make_async_remote_copy(
-            src_ref=recvs[c][phase - 1].at[pl.ds((1 - my_bit[plan[phase]]) * half, half)],
-            dst_ref=recvs[c][phase],
-            send_sem=send_sem.at[index],
-            recv_sem=recv_sem.at[index],
-            device_id=coordinates(flip(me, plan[phase]), reps),
-            device_id_type=MESH_ID,
-        )
-
-    started = [first_copies(c) for c in range(count)]
-    for copies, local in started:
-        for copy in copies + local:
-            copy.start()
-    current = [None] * count
-    sent = []
-
-    def absorb(c, phase):
-        half = devices >> (phase + 1)
-        if phase == 0:
-            for copy in started[c][0]:
-                copy.wait_recv()
-            for copy in started[c][1]:
-                copy.wait()
-            held, base = (owns[c], 0)
-        else:
-            current[c].wait_recv()
-            held, base = (recvs[c][phase - 1], my_bit[plan[phase]] * half)
-        into = recvs[c][phase]
-        if phase == bits - 1:
-            array, start, width = chunks[c]
-            outs[array][:, pl.ds(start, width)] = into[0].astype(jnp.float32) + held[base].astype(
-                jnp.float32
-            )
-            return
-
-        def one(i, carry):
-            total = into[i].astype(jnp.float32) + held[base + i].astype(jnp.float32)
-            into[i] = total.astype(into.dtype)
-            return carry
-
-        lax.fori_loop(0, half, one, 0)
-        copy = later_copy(c, phase + 1)
-        copy.start()
-        sent.append(copy)
-        current[c] = copy
-
-    for step in range(bits + count - 1):
-        for c in range(count):
-            phase = step - c
-            if 0 <= phase < bits:
-                absorb(c, phase)
-    for copies, local in started:
-        for copy in copies:
-            copy.wait_send()
-    for copy in sent:
-        copy.wait_send()
-
-
-def scatter_sums(parts, devices, reps):
-    bits, low, plan = scatter_plan(devices, reps)
-    high = devices >> low
-    rows = parts[0].shape[0] // devices
-    chunks = []
-    for array, part in enumerate(parts):
-        width = part.shape[1] if part.shape[1] < D else D
-        for start in range(0, part.shape[1], width):
-            chunks.append((array, start, width))
-    scratch = [pltpu.VMEM((devices // 2, rows, width), jnp.bfloat16) for _, _, width in chunks]
-    for _, _, width in chunks:
-        for phase in range(bits):
-            scratch.append(pltpu.VMEM((devices >> (phase + 1), rows, width), jnp.bfloat16))
-    firsts = 1 << (low - 1)
-    total = len(chunks) * (firsts + bits - 1)
-    return pl.pallas_call(
-        functools.partial(scatter_kernel, devices, reps, chunks, len(parts)),
-        out_shape=[jax.ShapeDtypeStruct((rows, part.shape[1]), jnp.float32) for part in parts],
-        in_specs=[pl.BlockSpec(memory_space=pl.ANY)] * len(parts),
-        out_specs=[pl.BlockSpec(memory_space=pltpu.VMEM)] * len(parts),
-        scratch_shapes=scratch
-        + [
-            pltpu.SemaphoreType.DMA((total,)),
-            pltpu.SemaphoreType.DMA((total,)),
-            pltpu.SemaphoreType.DMA((len(chunks) * firsts,)),
-        ],
-        compiler_params=pltpu.CompilerParams(
-            collective_id=1, has_side_effects=True, vmem_limit_bytes=60 * 1024 * 1024
-        ),
-        name="scatter_dense",
-    )(*[part.reshape(high, 1 << low, rows, part.shape[1]) for part in parts])
-
-
-def rep_pairs(reps, bit):
-    return [(source, source ^ (1 << bit)) for source in range(reps)]
-
-
-def rep_reduce(partial, reps):
-    mine = lax.axis_index("rep")
-    for bit in range(bit_count(reps)):
-        half = partial.shape[0] // 2
-        mine_bit = lax.rem(lax.div(mine, 1 << bit), 2)
-        away = lax.dynamic_slice_in_dim(partial, (1 - mine_bit) * half, half, 0)
-        kept = lax.dynamic_slice_in_dim(partial, mine_bit * half, half, 0)
-        arrived = lax.ppermute(away, "rep", rep_pairs(reps, bit))
-        partial = (kept.astype(jnp.float32) + arrived.astype(jnp.float32)).astype(jnp.bfloat16)
-    return partial
-
-
-def rep_spread(piece, reps):
-    mine = lax.axis_index("rep")
-    for bit in reversed(range(bit_count(reps))):
-        mine_bit = lax.rem(lax.div(mine, 1 << bit), 2)
-        arrived = lax.ppermute(piece, "rep", rep_pairs(reps, bit))
-        piece = jnp.where(
-            mine_bit == 0,
-            jnp.concatenate([piece, arrived], axis=0),
-            jnp.concatenate([arrived, piece], axis=0),
-        )
-    return piece
-
-
-def rep_total(small, reps):
-    for bit in range(bit_count(reps)):
-        arrived = lax.ppermute(small, "rep", rep_pairs(reps, bit))
-        small = small + arrived
-    return small
-
-
 def row_of(column, width):
     count = column.shape[0]
     down = lax.broadcasted_iota(jnp.int32, (count, width), 0)
@@ -453,10 +197,8 @@
     b_back_ref,
     return_ref,
     result_ref,
-    sum_back_ref,
-    sum_in_ref,
-    sum_b_in_ref,
-    sum_b_back_ref,
+    half_back_ref,
+    half_in_ref,
     slots,
     grads,
     gated,
@@ -468,14 +210,18 @@
     result_rows,
     result_total,
     back_total,
-    stage_back,
-    stage_in,
+    away_back,
+    away_in,
+    other_back,
+    other_in,
     load_sem,
     send_sem,
     recv_sem,
     return_send_sem,
     return_recv_sem,
     result_sem,
+    core_send,
+    core_recv,
     stage_sem,
 ):
     mine = lax.axis_index("exp")
@@ -495,6 +241,9 @@
         return carry
 
     lax.fori_loop(1, experts, greet_one, 0)
+    core = lax.rem(rep, 2)
+    partner = (mine, flip(rep, 0))
+    pl.semaphore_signal(barrier, inc=1, device_id=partner, device_id_type=MESH_ID)
 
     def group_of(index):
         half = lax.div(mine, 2)
@@ -557,7 +306,7 @@
     ]
     for copy in loads:
         copy.start()
-    pl.semaphore_wait(barrier, experts - 1)
+    pl.semaphore_wait(barrier, experts)
 
     def send_group(index):
         pair = group_of(index)
@@ -690,41 +439,77 @@
     results = pltpu.make_async_copy(result_rows, result_ref, result_sem)
     results.start()
 
-    sum_b_back_ref[...] = jnp.sum(gated[...].astype(jnp.float32), axis=0, keepdims=True)
-
-    def stages(step, slot):
-        columns = pl.ds(pl.multiple_of(step * block, block), block)
-        return (
-            pltpu.make_async_copy(stage_back.at[slot], sum_back_ref.at[columns, :], stage_sem.at[0, slot]),
-            pltpu.make_async_copy(stage_in.at[slot], sum_in_ref.at[:, columns], stage_sem.at[1, slot]),
-        )
-
-    def sum_step(step, carry):
-        columns = pl.ds(pl.multiple_of(step * block, block), block)
-        slot = lax.rem(step, 2)
-
-        @pl.when(step >= 2)
-        def _():
-            for copy in stages(step - 2, slot):
-                copy.wait()
-
-        stage_back[slot] = lax.dot_general(
+    piece = away_in.shape[2]
+    half = away_in.shape[0]
+    bias_back = jnp.sum(gated[...].astype(jnp.float32), axis=0, keepdims=True)
+
+    def sums_of(number):
+        columns = pl.ds(pl.multiple_of(number * piece, LANES), piece)
+        back = lax.dot_general(
             active[:, columns], gated[...], contract_first, preferred_element_type=jnp.float32
-        ).astype(jnp.bfloat16)
-        stage_in[slot] = lax.dot_general(
+        )
+        inward = lax.dot_general(
             slots[...], grad_pre[:, columns], contract_first, preferred_element_type=jnp.float32
-        ).astype(jnp.bfloat16)
-        sum_b_in_ref[:, columns] = jnp.sum(
-            grad_pre[:, columns].astype(jnp.float32), axis=0, keepdims=True
-        )
-        for copy in stages(step, slot):
+        )
+        bias_in = jnp.sum(grad_pre[:, columns].astype(jnp.float32), axis=0, keepdims=True)
+        if piece < D:
+            bias_in = jnp.concatenate([bias_in, jnp.zeros((1, D - piece), jnp.float32)], axis=1)
+        row = lax.broadcasted_iota(jnp.int32, (16, D), 0)
+        extra = jnp.where(row == 0, bias_in, jnp.where(row == 1, bias_back, 0.0))
+        return (back, inward, extra)
+
+    def core_copies(index):
+        return [
+            pltpu.make_async_remote_copy(
+                src_ref=source.at[index],
+                dst_ref=target.at[index],
+                send_sem=core_send.at[kind, index],
+                recv_sem=core_recv.at[kind, index],
+                device_id=partner,
+                device_id_type=MESH_ID,
+            )
+            for kind, (source, target) in enumerate(
+                ((away_back, other_back), (away_in, other_in))
+            )
+        ]
+
+    def away_step(index, carry):
+        back, inward, extra = sums_of(2 * index + 1 - core)
+        away_back[index, :piece, :] = back.astype(jnp.bfloat16)
+        away_back[index, piece:, :] = extra.astype(jnp.bfloat16)
+        away_in[index] = inward.astype(jnp.bfloat16)
+        for copy in core_copies(index):
             copy.start()
         return carry
 
-    lax.fori_loop(0, steps, sum_step, 0)
-    for step in range(max(steps - 2, 0), steps):
-        for copy in stages(step, step % 2):
+    def kept_copies(index):
+        return (
+            pltpu.make_async_copy(other_back.at[index], half_back_ref.at[index], stage_sem.at[0, index]),
+            pltpu.make_async_copy(other_in.at[index], half_in_ref.at[index], stage_sem.at[1, index]),
+        )
+
+    def kept_step(index, carry):
+        back, inward, extra = sums_of(2 * index + core)
+        for copy in core_copies(index):
+            copy.wait_recv()
+        other_back[index, :piece, :] = (
+            back + other_back[index, :piece, :].astype(jnp.float32)
+        ).astype(jnp.bfloat16)
+        other_back[index, piece:, :] = (
+            extra + other_back[index, piece:, :].astype(jnp.float32)
+        ).astype(jnp.bfloat16)
+        other_in[index] = (inward + other_in[index].astype(jnp.float32)).astype(jnp.bfloat16)
+        for copy in kept_copies(index):
+            copy.start()
+        return carry
+
+    lax.fori_loop(0, half, away_step, 0)
+    lax.fori_loop(0, half, kept_step, 0)
+    for index in range(half):
+        for copy in kept_copies(index):
             copy.wait()
+        for copy in core_copies(index):
+            copy.wait_send()
     own_back.wait()
     results.wait()
 
@@ -738,11 +523,13 @@
     lax.fori_loop(1, experts, finish, 0)
 
 
-def run_experts(buffer, grads, w_in, w_back, b_in, b_back, capacity):
+def run_experts(buffer, grads, w_in, w_back, b_in, b_back, capacity, reps):
     experts, padded = (buffer.shape[0], buffer.shape[1])
     hidden = w_in.shape[1]
     block = 512
     rows = experts * padded
+    half = reps // 2
+    piece = hidden // reps
     low = jnp.bfloat16
     anywhere = pl.BlockSpec(memory_space=pl.ANY)
     inside = pl.BlockSpec(memory_space=pltpu.VMEM)
@@ -751,13 +538,11 @@
         out_shape=[
             jax.ShapeDtypeStruct((experts, padded, D), low),
             jax.ShapeDtypeStruct((rows, D), low),
-            jax.ShapeDtypeStruct((hidden, D), low),
-            jax.ShapeDtypeStruct((D, hidden), low),
-            jax.ShapeDtypeStruct((1, hidden), jnp.float32),
-            jax.ShapeDtypeStruct((1, D), jnp.float32),
+            jax.ShapeDtypeStruct((half, piece + 16, D), low),
+            jax.ShapeDtypeStruct((half, D, piece), low),
         ],
         in_specs=[anywhere, anywhere, anywhere, anywhere, inside, inside],
-        out_specs=[anywhere, anywhere, anywhere, anywhere, inside, inside],
+        out_specs=[anywhere, anywhere, anywhere, anywhere],
         scratch_shapes=[
             pltpu.VMEM((rows, D), low),
             pltpu.VMEM((rows, D), low),
@@ -770,15 +555,19 @@
             pltpu.VMEM((rows, D), low),
             pltpu.VMEM((2 * padded, D), jnp.float32),
             pltpu.VMEM((2 * padded, D), jnp.float32),
-            pltpu.VMEM((2, block, D), low),
-            pltpu.VMEM((2, D, block), low),
+            pltpu.VMEM((half, piece + 16, D), low),
+            pltpu.VMEM((half, D, piece), low),
+            pltpu.VMEM((half, piece + 16, D), low),
+            pltpu.VMEM((half, D, piece), low),
             pltpu.SemaphoreType.DMA((4,)),
             pltpu.SemaphoreType.DMA((experts,)),
             pltpu.SemaphoreType.DMA((experts,)),
             pltpu.SemaphoreType.DMA((experts,)),
             pltpu.SemaphoreType.DMA((experts,)),
             pltpu.SemaphoreType.DMA,
-            pltpu.SemaphoreType.DMA((2, 2)),
+            pltpu.SemaphoreType.DMA((2, half)),
+            pltpu.SemaphoreType.DMA((2, half)),
+            pltpu.SemaphoreType.DMA((2, half)),
         ],
         compiler_params=pltpu.CompilerParams(
             collective_id=2, has_side_effects=True, vmem_limit_bytes=60 * 1024 * 1024
@@ -788,6 +577,753 @@
         ),
         name="experts",
     )(buffer, grads.reshape(rows, D), w_in, w_back, b_in.astype(jnp.float32), b_back.astype(jnp.float32))
+
+
+def attend_kernel(segment_col, segment_row, live_row, query_ref, keys_ref, values_ref, mixed_ref, bias):
+    @pl.when(pl.program_id(0) == 0)
+    def _():
+        row = lax.broadcasted_iota(jnp.int32, (SLOTS, SLOTS), 0)
+        column = lax.broadcasted_iota(jnp.int32, (SLOTS, SLOTS), 1)
+        seen = (segment_col[...] == segment_row[...]) & ((live_row[...] == 1) | (row == column))
+        bias[...] = jnp.where(seen, 0.0, -1e30)
+
+    for side in range(2):
+        lanes = slice(side * HEAD, (side + 1) * HEAD)
+        scores = lax.dot_general(
+            query_ref[:, lanes], keys_ref[:, lanes], contract_last, preferred_element_type=jnp.float32
+        )
+        scores = scores * HEAD ** (-0.5) + bias[...]
+        expo = jnp.exp(scores - jnp.max(scores, axis=1, keepdims=True))
+        total = jnp.sum(expo, axis=1, keepdims=True)
+        probs = (expo * (1.0 / total)).astype(jnp.bfloat16)
+        mixed = jnp.dot(probs, values_ref[:, lanes], preferred_element_type=jnp.float32)
+        mixed_ref[:, lanes] = mixed.astype(jnp.bfloat16)
+
+
+def attend(qkv, segments, live):
+    pairs = HEADS // 2
+    return pl.pallas_call(
+        attend_kernel,
+        grid=(pairs,),
+        out_shape=jax.ShapeDtypeStruct((SLOTS, D), jnp.bfloat16),
+        in_specs=[
+            pl.BlockSpec((SLOTS, 1), lambda i: (0, 0)),
+            pl.BlockSpec((1, SLOTS), lambda i: (0, 0)),
+            pl.BlockSpec((1, SLOTS), lambda i: (0, 0)),
+            pl.BlockSpec((SLOTS, 2 * HEAD), lambda i: (0, i)),
+            pl.BlockSpec((SLOTS, 2 * HEAD), lambda i: (0, pairs + i)),
+            pl.BlockSpec((SLOTS, 2 * HEAD), lambda i: (0, 2 * pairs + i)),
+        ],
+        out_specs=pl.BlockSpec((SLOTS, 2 * HEAD), lambda i: (0, i)),
+        scratch_shapes=[pltpu.VMEM((SLOTS, SLOTS), jnp.float32)],
+        cost_estimate=pl.CostEstimate(
+            flops=16 * HEADS * SLOTS * SLOTS * HEAD, bytes_accessed=4 << 20, transcendentals=HEADS * SLOTS * SLOTS
+        ),
+        name="attend",
+    )(segments.reshape(SLOTS, 1), segments.reshape(1, SLOTS), live.reshape(1, SLOTS), qkv, qkv, qkv)
+
+
+BAND = 48
+
+
+def fold_rows(values):
+    return jnp.sum(values.reshape(BAND // 8, 8, values.shape[1]), axis=0)
+
+
+def backward_kernel(
+    experts,
+    reps,
+    chunks,
+    summed,
+    back_ref,
+    result_ref,
+    first_ref,
+    second_ref,
+    terms_ref,
+    probs_ref,
+    routes_ref,
+    cotangent_ref,
+    resid_ref,
+    tokens_ref,
+    normed_ref,
+    routed_ref,
+    qkv_ref,
+    mixed_ref,
+    weights_ref,
+    vectors_ref,
+    segment_col,
+    segment_row,
+    live_col,
+    half_back_ref,
+    half_in_ref,
+    output_ref,
+    grad_tokens_ref,
+    sum_qkv_ref,
+    sum_out_ref,
+    sum_small_ref,
+    total_back_ref,
+    total_in_ref,
+    all_back_ref,
+    all_in_ref,
+    *refs,
+):
+    devices = experts * reps
+    bits = bit_count(devices)
+    half = reps // 2
+    mine = lax.axis_index("exp")
+    rep = lax.axis_index("rep")
+    me = mine * reps + rep
+    core = lax.rem(rep, 2)
+    along = lax.div(rep, 2)
+    (
+        back,
+        first,
+        second,
+        cotangent,
+        resid,
+        tokens,
+        normed,
+        routed,
+        qkv,
+        mixed,
+        weights,
+        returned,
+        bias,
+        wide,
+        tall,
+        grad_resid,
+        grad_attn,
+        grad_mixed,
+        grad_qkv,
+        grad_logits,
+        own_back,
+        own_in,
+        other_back,
+        other_in,
+        cast_back,
+        cast_in,
+        full_back,
+        full_in,
+    ) = refs[:28]
+    refs = refs[28:]
+    count = len(chunks) if summed else 0
+    parts, refs = (refs[:count], refs[count:])
+    recvs, refs = ([refs[c * bits : (c + 1) * bits] for c in range(count)], refs[count * bits :])
+    (
+        load_sem,
+        result_send,
+        result_recv,
+        dense_send,
+        dense_recv,
+        half_send,
+        half_recv,
+        all_send,
+        all_recv,
+        cast_sem,
+    ) = refs
+    padded = result_ref.shape[0] // experts
+    piece = half_in_ref.shape[2]
+
+    barrier = pltpu.get_barrier_semaphore()
+
+    def greet_expert(step, carry):
+        other = lax.rem(mine + step, experts)
+        pl.semaphore_signal(barrier, inc=1, device_id=(other, rep), device_id_type=MESH_ID)
+        return carry
+
+    def greet_rep(step, carry):
+        other = lax.rem(rep + step, reps)
+        pl.semaphore_signal(barrier, inc=1, device_id=(mine, other), device_id_type=MESH_ID)
+        return carry
+
+    lax.fori_loop(1, experts, greet_expert, 0)
+    lax.fori_loop(1, reps, greet_rep, 0)
+
+    sources = [
+        (back_ref, back),
+        (first_ref, first),
+        (second_ref, second),
+        (routed_ref, routed),
+        (weights_ref, weights),
+        (resid_ref, resid),
+        (cotangent_ref, cotangent),
+        (mixed_ref, mixed),
+        (qkv_ref, qkv),
+        (normed_ref, normed),
+        (tokens_ref, tokens),
+        (half_back_ref.at[along], own_back),
+        (half_in_ref.at[along], own_in),
+    ]
+    loads = [
+        pltpu.make_async_copy(source, target, load_sem.at[i])
+        for i, (source, target) in enumerate(sources)
+    ]
+    for copy in loads:
+        copy.start()
+    pl.semaphore_wait(barrier, experts - 1 + reps - 1)
+
+    def half_copies(step):
+        other = lax.rem(along + step, half)
+        came = lax.rem(along + half - step, half)
+        device = (mine, 2 * other + core)
+        return [
+            pltpu.make_async_remote_copy(
+                src_ref=source.at[other],
+                dst_ref=target.at[step - 1],
+                send_sem=half_send.at[kind, step - 1],
+                recv_sem=half_recv.at[kind, step - 1],
+                device_id=device,
+                device_id_type=MESH_ID,
+            )
+            for kind, (source, target) in enumerate(
+                ((half_back_ref, other_back), (half_in_ref, other_in))
+            )
+        ]
+
+    half_moves = [half_copies(step) for step in range(1, half)]
+    for kind in range(2):
+        for moves in half_moves:
+            moves[kind].start()
+
+    def place(expert):
+        return pl.ds(pl.multiple_of(expert * padded, 16), padded)
+
+    def result_copy(step):
+        other = lax.rem(mine + step, experts)
+        came = lax.rem(mine + experts - step, experts)
+        return pltpu.make_async_remote_copy(
+            src_ref=result_ref.at[place(other)],
+            dst_ref=returned.at[place(mine)],
+            send_sem=result_send.at[step],
+            recv_sem=result_recv.at[step],
+            device_id=(other, rep),
+            device_id_type=MESH_ID,
+        )
+
+    def start_result(step, carry):
+        result_copy(step).start()
+        return carry
+
+    own_result = pltpu.make_async_copy(
+        result_ref.at[place(mine)], returned.at[place(mine)], result_send.at[0]
+    )
+    own_result.start()
+    lax.fori_loop(1, experts, start_result, 0)
+
+    row = lax.broadcasted_iota(jnp.int32, (SLOTS, SLOTS), 0)
+    column = lax.broadcasted_iota(jnp.int32, (SLOTS, SLOTS), 1)
+    seen = (segment_col[...] == segment_row[...]) & ((live_col[...] == 1) | (row == column))
+    bias[...] = jnp.where(seen, 0.0, -1e30)
+
+    for copy in loads[:5]:
+        copy.wait()
+    tall[...] = jnp.dot(first[...] + second[...], back[...], preferred_element_type=jnp.float32)
+    gates_back = [
+        jnp.sum(
+            lax.dot_general(
+                pick[...], terms_ref[...], contract_last, preferred_element_type=jnp.float32
+            ),
+            axis=1,
+            keepdims=True,
+        )
+        for pick in (first, second)
+    ]
+    lane = lax.broadcasted_iota(jnp.int32, (SLOTS, LANES), 1)
+    hots = [(lane == routes_ref[:, k : k + 1]).astype(jnp.float32) for k in range(2)]
+    grad_probs = gates_back[0] * hots[0] + gates_back[1] * hots[1]
+    probs = probs_ref[...]
+    grad_logits[...] = (
+        probs * (grad_probs - jnp.sum(probs * grad_probs, axis=1, keepdims=True))
+    ).astype(jnp.bfloat16)
+    tall[...] += lax.dot_general(
+        grad_logits[...], weights[:, 4 * D :], contract_last, preferred_element_type=jnp.float32
+    )
+    for copy in loads[5:]:
+        copy.wait()
+
+    def band(step):
+        return pl.ds(pl.multiple_of(step * BAND, 16), BAND)
+
+    def norm_back(inputs, grad, gain):
+        center = inputs - jnp.mean(inputs, axis=1, keepdims=True)
+        inverse = lax.rsqrt(jnp.mean(center * center, axis=1, keepdims=True) + 1e-06)
+        normal = center * inverse
+        scaled = grad * gain
+        grad_in = inverse * (
+            scaled
+            - jnp.mean(scaled, axis=1, keepdims=True)
+            - normal * jnp.mean(scaled * normal, axis=1, keepdims=True)
+        )
+        return (grad_in, fold_rows(grad * normal), fold_rows(grad))
+
+    zero = jnp.zeros((8, D), jnp.float32)
+
+    def second_norm(step, carry):
+        here = band(step)
+        grad_in, grad_gain, grad_bias = norm_back(
+            resid[here, :], tall[here, :], vectors_ref[2:3, :]
+        )
+        total = cotangent[here, :].astype(jnp.float32) + grad_in
+        grad_resid[here, :] = total
+        grad_attn[here, :] = total.astype(jnp.bfloat16)
+        return (carry[0] + grad_gain, carry[1] + grad_bias)
+
+    gain_two, bias_two = lax.fori_loop(0, SLOTS // BAND, second_norm, (zero, zero))
+
+    plan = [0] + [bit_count(reps)] + list(range(bits - 1, bit_count(reps), -1))
+    plan = plan + list(range(bit_count(reps) - 1, 0, -1))
+    my_bit = [lax.rem(lax.div(me, 1 << bit), 2) for bit in range(bits)]
+    rows = parts[0].shape[3] if summed else 0
+    stride = experts + bits - 1
+    outs = (sum_qkv_ref, sum_out_ref, sum_small_ref)
+
+    def fill(c):
+        width = chunks[c][2]
+
+        def one(block, carry):
+            owner = lax.div(block, reps)
+            inner = lax.rem(block, reps)
+            parts[c][owner, lax.div(inner, 2), lax.rem(inner, 2)] = wide[
+                pl.ds(pl.multiple_of(block * rows, rows), rows), :width
+            ].astype(jnp.bfloat16)
+            return carry
+
+        lax.fori_loop(0, devices, one, 0)
+
+    def first_copy(c, expert):
+        spot = lax.rem(expert, 2) * (devices // 4) + lax.div(expert, 2) * half
+        return pltpu.make_async_remote_copy(
+            src_ref=parts[c].at[expert, :, 1 - core],
+            dst_ref=recvs[c][0].at[pl.ds(spot, half)],
+            send_sem=dense_send.at[c * stride + expert],
+            recv_sem=dense_recv.at[c * stride + expert],
+            device_id=(mine, flip(rep, 0)),
+            device_id_type=MESH_ID,
+        )
+
+    def later_copy(c, phase):
+        size = devices >> (phase + 1)
+        index = c * stride + experts + phase - 1
+        return pltpu.make_async_remote_copy(
+            src_ref=recvs[c][phase - 1].at[pl.ds((1 - my_bit[plan[phase]]) * size, size)],
+            dst_ref=recvs[c][phase],
+            send_sem=dense_send.at[index],
+            recv_sem=dense_recv.at[index],
+            device_id=coordinates(flip(me, plan[phase]), reps),
+            device_id_type=MESH_ID,
+        )
+
+    def send_chunk(c):
+        if not summed:
+            array, start, width = chunks[c]
+            pltpu.sync_copy(wide.at[:, :width], outs[array].at[:, pl.ds(start, width)])
+            return
+        fill(c)
+
+        def one(expert, carry):
+            first_copy(c, expert).start()
+            return carry
+
+        lax.fori_loop(0, experts, one, 0)
+
+    def absorb(c, phase):
+        if not summed:
+            return
+        size = devices >> (phase + 1)
+        into = recvs[c][phase]
+        if phase == 0:
+
+            def arrived(expert, carry):
+                first_copy(c, expert).wait_recv()
+                return carry
+
+            lax.fori_loop(0, experts, arrived, 0)
+
+            def held(i):
+                side = lax.div(i, devices // 4)
+                rest = lax.rem(i, devices // 4)
+                return parts[c][2 * lax.div(rest, half) + side, lax.rem(rest, half), core]
+        else:
+            later_copy(c, phase).wait_recv()
+            base = my_bit[plan[phase]] * size
+
+            def held(i):
+                return recvs[c][phase - 1][base + i]
+
+        if phase == bits - 1:
+            array, start, width = chunks[c]
+            outs[array][:, pl.ds(start, width)] = into[0].astype(jnp.float32) + held(0).astype(
+                jnp.float32
+            )
+            return
+
+        def one(i, carry):
+            into[i] = (into[i].astype(jnp.float32) + held(i).astype(jnp.float32)).astype(
+                jnp.bfloat16
+            )
+            return carry
+
+        lax.fori_loop(0, size, one, 0)
+        later_copy(c, phase + 1).start()
+
+    out_chunk = [c for c in range(len(chunks)) if chunks[c][0] == 1][0]
+    small_chunk = [c for c in range(len(chunks)) if chunks[c][0] == 2][0]
+    qkv_chunks = [c for c in range(len(chunks)) if chunks[c][0] == 0]
+    wide[...] = lax.dot_general(
+        mixed[...], grad_attn[...], contract_first, preferred_element_type=jnp.float32
+    )
+    send_chunk(out_chunk)
+    grad_mixed[...] = lax.dot_general(
+        grad_attn[...], weights[:, 3 * D : 4 * D], contract_last, preferred_element_type=jnp.float32
+    ).astype(jnp.bfloat16)
+
+    def attend_back(pair, carry):
+        base = pl.multiple_of(pair * 2 * HEAD, 2 * HEAD)
+        queries = qkv[:, pl.ds(base, 2 * HEAD)]
+        keys = qkv[:, pl.ds(base + D, 2 * HEAD)]
+        values = qkv[:, pl.ds(base + 2 * D, 2 * HEAD)]
+        grads = grad_mixed[:, pl.ds(base, 2 * HEAD)]
+        done = []
+        for side in range(2):
+            lanes = slice(side * HEAD, (side + 1) * HEAD)
+            query, key, value, grad = (
+                queries[:, lanes],
+                keys[:, lanes],
+                values[:, lanes],
+                grads[:, lanes],
+            )
+            scores = lax.dot_general(key, query, contract_last, preferred_element_type=jnp.float32)
+            scores = scores * HEAD ** (-0.5) + bias[...]
+            expo = jnp.exp(scores - jnp.max(scores, axis=0, keepdims=True))
+            weight = expo * (1.0 / jnp.sum(expo, axis=0, keepdims=True))
+            grad_weight = lax.dot_general(
+                value, grad, contract_last, preferred_element_type=jnp.float32
+            )
+            product = weight * grad_weight
+            delta = jnp.sum(product, axis=0, keepdims=True)
+            grad_scores = (product - weight * delta).astype(jnp.bfloat16)
+            grad_value = jnp.dot(
+                weight.astype(jnp.bfloat16), grad, preferred_element_type=jnp.float32
+            )
+            grad_key = jnp.dot(grad_scores, query, preferred_element_type=jnp.float32)
+            grad_query = lax.dot_general(
+                grad_scores, key, contract_first, preferred_element_type=jnp.float32
+            )
+            done.append(
+                (grad_query * HEAD ** (-0.5), grad_key * HEAD ** (-0.5), grad_value)
+            )
+        for kind in range(3):
+            grad_qkv[:, pl.ds(base + kind * D, 2 * HEAD)] = jnp.concatenate(
+                [done[0][kind], done[1][kind]], axis=1
+            ).astype(jnp.bfloat16)
+        return carry
+
+    lax.fori_loop(0, HEADS // 2, attend_back, 0)
+
+    arrays = ((own_back, other_back, all_back_ref), (own_in, other_in, all_in_ref))
+
+    def complete(kind):
+        own, others, everywhere = arrays[kind]
+        for step in range(1, half):
+            half_moves[step - 1][kind].wait_recv()
+        size = 16
+        steps = own.shape[0] // size
+
+        def one(step, carry):
+            here = pl.ds(pl.multiple_of(step * size, 16), size)
+            total = own[here, :].astype(jnp.float32)
+            for step in range(1, half):
+                total = total + others[step - 1, here, :].astype(jnp.float32)
+            own[here, :] = total.astype(jnp.bfloat16)
+            return carry
+
+        lax.fori_loop(0, steps, one, 0)
+        local = pltpu.make_async_copy(own, everywhere.at[rep], cast_sem.at[4 + kind])
+        local.start()
+        moves = []
+        for step in range(1, half):
+            other = lax.rem(along + step, half)
+            moves.append(spread(kind, own, rep, (mine, 2 * other + core), step))
+        moves.append(spread(kind, own, rep, (mine, flip(rep, 0)), 0))
+        for move in moves:
+            move.start()
+        return (local, moves)
+
+    def spread(kind, source, owner, device, step):
+        return pltpu.make_async_remote_copy(
+            src_ref=source,
+            dst_ref=arrays[kind][2].at[owner],
+            send_sem=all_send.at[kind, step],
+            recv_sem=all_recv.at[kind, step],
+            device_id=device,
+            device_id_type=MESH_ID,
+        )
+
+    finals = [complete(0)]
+    for c in qkv_chunks:
+        start = chunks[c][1]
+        wide[...] = lax.dot_general(
+            normed[...], grad_qkv[:, start : start + D], contract_first, preferred_element_type=jnp.float32
+        )
+        send_chunk(c)
+    absorb(out_chunk, 0)
+    finals.append(complete(1))
+    tall[...] = lax.dot_general(
+        grad_qkv[...], weights[:, : 3 * D], contract_last, preferred_element_type=jnp.float32
+    )
+
+    def first_norm(step, carry):
+        here = band(step)
+        grad_in, grad_gain, grad_bias = norm_back(
+            tokens[here, :].astype(jnp.float32), tall[here, :], vectors_ref[0:1, :]
+        )
+        grad_tokens_ref[here, :] = grad_resid[here, :] + grad_in
+        return (carry[0] + grad_gain, carry[1] + grad_bias)
+
+    gain_one, bias_one = lax.fori_loop(0, SLOTS // BAND, first_norm, (zero, zero))
+    wide[:, :LANES] = lax.dot_general(
+        routed[...], grad_logits[...], contract_first, preferred_element_type=jnp.float32
+    )
+    lines = [jnp.sum(v, axis=0, keepdims=True) for v in (gain_one, bias_one, gain_two, bias_two)]
+    lane = lax.broadcasted_iota(jnp.int32, (LANES, LANES), 1)
+    for part in range(D // LANES):
+        span = slice(part * LANES, (part + 1) * LANES)
+        block = wide[span, :LANES]
+        for k in range(4):
+            block = jnp.where(lane == experts + k, column_of(lines[k][:, span], LANES), block)
+        wide[span, :LANES] = block
+    send_chunk(small_chunk)
+
+    order = [out_chunk] + qkv_chunks + [small_chunk]
+    for step in range(bits + len(order) - 1):
+        for position, c in enumerate(order):
+            phase = step - position
+            if 0 <= phase < bits and not (c == out_chunk and phase == 0):
+                absorb(c, phase)
+
+    own_result.wait()
+
+    def result_arrived(step, carry):
+        result_copy(step).wait_recv()
+        result_copy(step).wait_send()
+        return carry
+
+    lax.fori_loop(1, experts, result_arrived, 0)
+    lane = lax.broadcasted_iota(jnp.int32, (SLOTS, LANES), 1)
+    probs = probs_ref[...]
+    gates = [
+        jnp.sum(jnp.where(lane == routes_ref[:, k : k + 1], probs, 0.0), axis=1, keepdims=True)
+        for k in range(2)
+    ]
+    tall[...] = resid[...] + gates[0] * jnp.dot(
+        first[...], returned[...], preferred_element_type=jnp.float32
+    )
+    output_ref[...] = (
+        tall[...]
+        + gates[1] * jnp.dot(second[...], returned[...], preferred_element_type=jnp.float32)
+    ).astype(jnp.bfloat16)
+
+    forwards = []
+    pending = [None, None]
+
+    def convert(owner, first_wait):
+        for kind in range(2):
+            staged, full = ((cast_back, full_back), (cast_in, full_in))[kind]
+            size = staged.shape[0]
+            whole = (piece, D)[kind]
+            for block in range(whole // size):
+                span = pl.ds(block * size, size)
+                load = pltpu.make_async_copy(
+                    arrays[kind][2].at[owner, span, :], staged, cast_sem.at[kind]
+                )
+                load.start()
+                load.wait()
+                if pending[kind] is not None:
+                    pending[kind].wait()
+
+                def one(step, carry):
+                    here = pl.ds(pl.multiple_of(step * 48, 16), 48)
+                    full[here, :] = staged[here, :].astype(jnp.float32)
+                    return carry
+
+                lax.fori_loop(0, size // 48, one, 0)
+                if kind == 0:
+                    target = total_back_ref.at[
+                        pl.ds(pl.multiple_of(owner * piece + block * size, 16), size), :
+                    ]
+                else:
+                    target = total_in_ref.at[span, pl.ds(pl.multiple_of(owner * piece, LANES), piece)]
+                store = pltpu.make_async_copy(full, target, cast_sem.at[2 + kind])
+                store.start()
+                pending[kind] = store
+
+    for local, _ in finals:
+        local.wait()
+    convert(rep, True)
+    partner = flip(rep, 0)
+    for kind in range(2):
+        spread(kind, arrays[kind][2].at[partner], partner, (mine, partner), 0).wait_recv()
+    convert(partner, True)
+    for step in range(1, half):
+        came = lax.rem(along + half - step, half)
+        owner = 2 * came + core
+        for kind in range(2):
+            spread(kind, arrays[kind][2].at[owner], owner, (mine, owner), step).wait_recv()
+            forward = spread(
+                kind, arrays[kind][2].at[owner], owner, (mine, partner), half + step - 1
+            )
+            forward.start()
+            forwards.append(forward)
+        convert(owner, True)
+    for step in range(1, half):
+        came = lax.rem(along + half - step, half)
+        owner = 2 * came + 1 - core
+        for kind in range(2):
+            spread(
+                kind, arrays[kind][2].at[owner], owner, (mine, partner), half + step - 1
+            ).wait_recv()
+        convert(owner, True)
+    for copy in pending:
+        copy.wait()
+    for copy in forwards:
+        copy.wait_send()
+    for _, moves in finals:
+        for move in moves:
+            move.wait_send()
+    for moves in half_moves:
+        for move in moves:
+            move.wait_send()
+
+    def dense_sent(c):
+        def one(expert, carry):
+            first_copy(c, expert).wait_send()
+            return carry
+
+        lax.fori_loop(0, experts, one, 0)
+        for phase in range(1, bits):
+            later_copy(c, phase).wait_send()
+
+    for c in range(count):
+        dense_sent(c)
+
+
+def run_backward(operands, experts, reps, rows):
+    devices = experts * reps
+    bits = bit_count(devices)
+    half = reps // 2
+    (
+        back,
+        result,
+        first,
+        second,
+        terms,
+        probs,
+        routes,
+        cotangent,
+        resid,
+        tokens,
+        normed,
+        routed,
+        qkv,
+        mixed,
+        weights,
+        vectors,
+        segment_col,
+        segment_row,
+        live_col,
+        half_back,
+        half_in,
+    ) = operands
+    low = jnp.bfloat16
+    full = jnp.float32
+    piece = half_in.shape[2]
+    tail_rows = half_back.shape[1]
+    chunks = [(0, k * D, D) for k in range(3)] + [(1, 0, D), (2, 0, LANES)]
+    anywhere = pl.BlockSpec(memory_space=pl.ANY)
+    inside = pl.BlockSpec(memory_space=pltpu.VMEM)
+    slots = result.shape[0]
+    scratch = [
+        pltpu.VMEM((slots, D), low),
+        pltpu.VMEM((SLOTS, slots), low),
+        pltpu.VMEM((SLOTS, slots), low),
+        pltpu.VMEM((SLOTS, D), low),
+        pltpu.VMEM((SLOTS, D), full),
+        pltpu.VMEM((SLOTS, D), low),
+        pltpu.VMEM((SLOTS, D), low),
+        pltpu.VMEM((SLOTS, D), low),
+        pltpu.VMEM((SLOTS, 3 * D), low),
+        pltpu.VMEM((SLOTS, D), low),
+        pltpu.VMEM(weights.shape, low),
+        pltpu.VMEM((slots, D), low),
+        pltpu.VMEM((SLOTS, SLOTS), full),
+        pltpu.VMEM((D, D), full),
+        pltpu.VMEM((SLOTS, D), full),
+        pltpu.VMEM((SLOTS, D), full),
+        pltpu.VMEM((SLOTS, D), low),
+        pltpu.VMEM((SLOTS, D), low),
+        pltpu.VMEM((SLOTS, 3 * D), low),
+        pltpu.VMEM((SLOTS, LANES), low),
+        pltpu.VMEM((tail_rows, D), low),
+        pltpu.VMEM((D, piece), low),
+        pltpu.VMEM((half - 1, tail_rows, D), low),
+        pltpu.VMEM((half - 1, D, piece), low),
+        pltpu.VMEM((piece // 2, D), low),
+        pltpu.VMEM((D // 2, piece), low),
+        pltpu.VMEM((piece // 2, D), full),
+        pltpu.VMEM((D // 2, piece), full),
+    ]
+    summed = rows % 8 == 0
+    for _, _, width in chunks if summed else ():
+        scratch.append(pltpu.VMEM((experts, half, 2, rows, width), low))
+    for _, _, width in chunks if summed else ():
+        for phase in range(bits):
+            scratch.append(pltpu.VMEM((devices >> (phase + 1), rows, width), low))
+    dense = len(chunks) * (experts + bits - 1)
+    scratch = scratch + [
+        pltpu.SemaphoreType.DMA((13,)),
+        pltpu.SemaphoreType.DMA((experts,)),
+        pltpu.SemaphoreType.DMA((experts,)),
+        pltpu.SemaphoreType.DMA((dense,)),
+        pltpu.SemaphoreType.DMA((dense,)),
+        pltpu.SemaphoreType.DMA((2, half - 1)),
+        pltpu.SemaphoreType.DMA((2, half - 1)),
+        pltpu.SemaphoreType.DMA((2, reps)),
+        pltpu.SemaphoreType.DMA((2, reps)),
+        pltpu.SemaphoreType.DMA((6,)),
+    ]
+    hidden = piece * reps
+    call = pl.pallas_call(
+        functools.partial(backward_kernel, experts, reps, chunks, summed),
+        out_shape=[
+            jax.ShapeDtypeStruct((SLOTS, D), low),
+            jax.ShapeDtypeStruct((SLOTS, D), full),
+            jax.ShapeDtypeStruct((rows if summed else D, 3 * D), full),
+            jax.ShapeDtypeStruct((rows if summed else D, D), full),
+            jax.ShapeDtypeStruct((rows if summed else D, LANES), full),
+            jax.ShapeDtypeStruct((hidden, D), full),
+            jax.ShapeDtypeStruct((D, hidden), full),
+            jax.ShapeDtypeStruct((reps, tail_rows, D), low),
+            jax.ShapeDtypeStruct((reps, D, piece), low),
+        ],
+        in_specs=[anywhere] * 4
+        + [inside] * 3
+        + [anywhere] * 8
+        + [inside] * 4
+        + [anywhere] * 2,
+        out_specs=[inside] * 2 + [inside if summed else anywhere] * 3 + [anywhere] * 4,
+        scratch_shapes=scratch,
+        compiler_params=pltpu.CompilerParams(
+            collective_id=1, has_side_effects=True, vmem_limit_bytes=63 * 1024 * 1024
+        ),
+        name="backward",
+    )
+    gradients = list(call(*operands))
+    if not summed:
+        for index in (2, 3, 4):
+            gradients[index] = lax.psum_scatter(
+                gradients[index], ("exp", "rep"), scatter_dimension=0, tiled=True
+            )
+    return gradients
 
 
 def exchange(blocks):
@@ -849,9 +1385,11 @@
         .astype(jnp.bfloat16)
         .reshape(ROWS_DEV, SLOTS, 3 * D)
     )
-    allowed = row_masks(lengths, padding)
-    mixed, lse = attend_forward(qkv[0], allowed[0])
-    mixed_low = mixed.astype(jnp.bfloat16)
+    bounds = jnp.cumsum(lengths[0])
+    segments = jnp.sum(
+        (jnp.arange(SLOTS, dtype=jnp.int32)[:, None] >= bounds[None, :]).astype(jnp.int32), axis=1
+    )
+    mixed_low = attend(qkv[0], segments, padding)
     resid = inputs + jnp.dot(mixed_low, out_weight, preferred_element_type=jnp.float32)
     routed_float, normal_two, inverse_two = norm_forward(resid, gain_two, bias_two)
     routed = routed_float.astype(jnp.bfloat16)
@@ -871,82 +1409,54 @@
     terms = jnp.stack([high, middle, slot_gates - high - middle], axis=1).astype(jnp.bfloat16)
     terms = jnp.pad(terms, ((0, 0), (0, padded - capacity - 3), (0, D - capacity)))
     buffer = lax.dynamic_update_slice(buffer, terms, (0, capacity, 0))
-    grad_buffer, result, grad_w_back, grad_w_in, grad_b_in, grad_b_back = run_experts(
-        buffer, grad_arrived, w_in[0], w_back[0], b_in, b_back, capacity
-    )
-    returned = exchange(result.reshape(experts, padded, D)).reshape(experts * padded, D)
-    grad_gate_slots = jnp.sum(
-        grad_buffer[:, capacity : capacity + 3, :padded].astype(jnp.float32), axis=1
-    ).reshape(1, experts * padded)
-    grad_buffer = grad_buffer.reshape(experts * padded, D)
-    back_total = rep_spread(rep_reduce(grad_w_back, reps), reps).astype(jnp.float32)
-    in_total = rep_spread(rep_reduce(grad_w_in, reps), reps).astype(jnp.float32)
-    bias_total = rep_total(jnp.concatenate([grad_b_in[0], grad_b_back[0]]).reshape(-1, LANES), reps)
-    bias_total = bias_total.reshape(-1)
-
-    grad_out = cotangent.astype(jnp.float32)
-    grad_gate_first = jnp.sum(pick_first.astype(jnp.float32) * grad_gate_slots, axis=1)
-    grad_gate_second = jnp.sum(pick_second.astype(jnp.float32) * grad_gate_slots, axis=1)
-    grad_probs = grad_gate_first[:, None] * first_hot + grad_gate_second[:, None] * second_hot
-    grad_logits = (
-        probs * (grad_probs - jnp.sum(probs * grad_probs, axis=1, keepdims=True))
-    ).astype(jnp.bfloat16)
-    grad_router = lax.dot_general(
-        routed, grad_logits, contract_first, preferred_element_type=jnp.float32
-    )
-    grad_routed = jnp.dot(picks, grad_buffer, preferred_element_type=jnp.float32)
-    grad_routed = grad_routed + lax.dot_general(
-        grad_logits, router_weight, contract_last, preferred_element_type=jnp.float32
-    )
-    grad_norm_two, grad_gain_two, grad_bias_two = norm_backward(
-        grad_routed, normal_two, inverse_two, gain_two
-    )
-    grad_resid = grad_out + grad_norm_two
-    grad_attn = grad_resid.astype(jnp.bfloat16)
-    grad_out_weight = lax.dot_general(
-        mixed_low, grad_attn, contract_first, preferred_element_type=jnp.float32
-    )
-    grad_mixed = lax.dot_general(
-        grad_attn, out_weight, contract_last, preferred_element_type=jnp.float32
-    )
-    grad_mixed = grad_mixed.astype(jnp.bfloat16)
-    grad_qkv = attend_backward(qkv[0], allowed[0], lse, grad_mixed)
-    grad_qkv_weight = lax.dot_general(
-        normed_low, grad_qkv, contract_first, preferred_element_type=jnp.float32
-    )
-    grad_normed = lax.dot_general(
-        grad_qkv, qkv_weight, contract_last, preferred_element_type=jnp.float32
-    )
-    grad_norm_one, grad_gain_one, grad_bias_one = norm_backward(
-        grad_normed, normal_one, inverse_one, gain_one
-    )
-    grad_tokens = grad_resid + grad_norm_one
-
-    picked_first = jnp.dot(pick_first, returned, preferred_element_type=jnp.float32)
-    picked_second = jnp.dot(pick_second, returned, preferred_element_type=jnp.float32)
-    output = resid + gate_first[:, None] * picked_first + gate_second[:, None] * picked_second
-
-    grad_small = jnp.concatenate(
-        [
-            grad_router,
-            jnp.stack([grad_gain_one, grad_bias_one, grad_gain_two, grad_bias_two], axis=1),
-        ],
-        axis=1,
-    )
-    grad_small = jnp.pad(grad_small, ((0, 0), (0, LANES - grad_small.shape[1])))
-    sum_qkv, sum_out, sum_small = scatter_sums(
-        [
-            grad_qkv_weight.astype(jnp.bfloat16),
-            grad_out_weight.astype(jnp.bfloat16),
-            grad_small.astype(jnp.bfloat16),
-        ],
-        devices,
+    grad_buffer, result, half_back, half_in = run_experts(
+        buffer, grad_arrived, w_in[0], w_back[0], b_in, b_back, capacity, reps
+    )
+    terms = grad_buffer[:, capacity : capacity + 3, :padded].transpose(1, 0, 2)
+    terms = jnp.pad(terms.reshape(3, experts * padded), ((0, 13), (0, 0)))
+    (
+        output,
+        grad_tokens,
+        sum_qkv,
+        sum_out,
+        sum_small,
+        back_total,
+        in_total,
+        all_back,
+        all_in,
+    ) = run_backward(
+        (
+            grad_buffer.reshape(experts * padded, D),
+            result,
+            pick_first,
+            pick_second,
+            terms,
+            jnp.pad(probs, ((0, 0), (0, LANES - experts))),
+            routes,
+            cotangent,
+            resid,
+            tokens,
+            normed_low,
+            routed,
+            qkv[0],
+            mixed_low,
+            gathered,
+            vectors.astype(jnp.float32),
+            segments.reshape(SLOTS, 1),
+            segments.reshape(1, SLOTS),
+            padding.reshape(SLOTS, 1),
+            half_back,
+            half_in,
+        ),
+        experts,
         reps,
+        rows,
     )
     vector_sums = sum_small[:, experts : experts + 4]
     hidden = b_in.shape[1]
+    piece = hidden // reps
     return (
-        output.astype(jnp.bfloat16),
+        output,
         grad_tokens,
         vector_sums[:, 0],
         vector_sums[:, 1],
@@ -956,9 +1466,9 @@
         vector_sums[:, 3],
         sum_small[:, :experts],
         in_total[None],
-        bias_total[None, :hidden],
+        all_back[:, piece, :piece].astype(jnp.float32).reshape(1, hidden),
         back_total[None],
-        bias_total[None, hidden:],
+        all_back[:1, piece + 1, :].astype(jnp.float32),
     )
 
 

time: 499 us -> 393 us (0.79)
  Pallas kernels: 175 us -> 308 us
  matrix products: 102 us -> 19 us
  waiting for transfers between devices: 83.3 us -> 4.22 us
  other arithmetic: 64.1 us -> 13.8 us
  starting transfers between devices: 30.2 us -> 6.25 us
    pallas_call x1 -> x2, Pallas kernels: 54.2 us -> 189 us  [the longest x1 175 us: run_backward(): gradients = list(call(*operands))]
    dot_general x15 -> x0, matrix products: 83.9 us -> none  [the longest x1 16.1 us: attend_backward(): jnp.einsum('qhc,khc->hqk', grad_mixed, values, preferred_element_type=jnp...]
    ppermute x10 -> x0, waiting for transfers between devices: 83.3 us -> none  [the longest x4 42.4 us: rep_spread(): arrived = lax.ppermute(piece, 'rep', rep_pairs(reps, bit))]
    convert_element_type x8 -> x5, other arithmetic: 37.4 us -> 5.37 us  [the longest x1 2.31 us: dispatch_tables(): ((slot_first[:, None] == slot_labels[None, :]) & kept_first[:, None]).ast...]
    all_to_all x2 -> x1, starting transfers between devices: 25.6 us -> 6.25 us  [exchange(): lax.all_to_all(blocks, 'exp', split_axis=0, concat_axis=0, tiled=True)]
    unnamed x56 -> x58, local copies, waits for them, and re-layouts: 7.79 us -> 19.9 us
    reduce_sum x5 -> x1, other arithmetic: 11 us -> 0.08 us  [on_device(): jnp.sum((jnp.arange(SLOTS, dtype=jnp.int32)[:, None] >= bounds[None, :])....]
    dynamic_slice x4 -> x0, local copies, waits for them, and re-layouts: 6.67 us -> none  [rep_reduce(): away = lax.dynamic_slice_in_dim(partial, (1 - mine_bit) * half, half, 0)]
  transfers between devices with their start and end apart: 12 -> 1, of which waited for: 5 -> 1; matrix products, arithmetic and copies ran while one was open for 24% -> 7% of each run, Pallas kernels for 11% -> 4%
where the time goes in v3:
time: 393 us; the launch traced here: 387 us
  Pallas kernels  308 us (78%)
  local copies, waits for them, and re-layouts  34 us (9%)
  matrix products  19 us (5%)
  other arithmetic  13.8 us (4%)
  starting transfers between devices  6.25 us (2%)
  waiting for transfers between devices  4.22 us (1%)
    pallas_call x1, Pallas kernels, run_backward(): gradients = list(call(*operands))  175 us
    pallas_call x1, Pallas kernels, run_experts(): pl.pallas_call(functools.partial(expert_kernel, experts, capacity, padded...  81.5 us
    pallas_call x1, Pallas kernels, gather_blocks(): pl.pallas_call(functools.partial(gather_kernel, devices, reps), out_shape...  37.4 us
    unnamed x58, local copies, waits for them, and re-layouts  19.9 us
    pallas_call x1, Pallas kernels, attend(): pl.pallas_call(attend_kernel, grid=(pairs,), out_shape=jax.ShapeDtypeStru...  14.4 us
  transfers between devices with their start and end apart: 1, of which 1 were waited for; matrix products, arithmetic and copies ran while one was open for 7% of the time, Pallas kernels for 4%

profile of v3, /device:TPU:0, one launch (start us, length us, event | category | flops | bytes accessed | tf_op | source)
XLA Modules:
  0.0 387.2 jit_solution(16281662217915127025)
XLA Ops:
  0.7 0.8 convert_element_type.134
  1.5 0.7 slice_reduce_fusion.5
  2.2 0.2 convert_reduce_fusion.1
  2.4 1.4 fusion.27
  3.8 0.7 compare_and_fusion.1
  4.5 0.8 add_reduce_fusion.2
  5.3 1.4 fusion.24
  6.8 0.1 copy.100
  6.9 0.1 copy.101
  7.0 0.1 copy.102
  7.1 0.1 copy.103
  7.2 0.1 copy.99
  7.3 0.1 concatenate.6
  7.4 0.7 fusion.55.own_ref
  8.1 37.4 %gather_dense.1 = bf16[32,24,3200]{2,1,0:T(8,128)(2,1)} custom-call(bf16[24,3200]{1,0:T(8,128)(2,1)} %fusion.55.own_ref), custom_call_target="tpu_custom_call" | custom-call | tf_op jit(solution)/shard_map/gather_dense/pallas_call | solution.py:151
  45.4 4.1 %slice.86 = bf16[768,2304]{1,0:T(8,128)(2,1)} slice(bf16[768,3200]{1,0:T(8,128)(2,1)} %bitcast.37), slice={[0:768], [0:2304]} | slice | bytes 7077888 | tf_op jit(solution)/shard_map/slice | solution.py:1364
  49.5 3.7 convolution_convert_fusion.2
  53.2 6.2 %all-to-all-start = ((bf16[8,160,768]{2,1,0:T(8,128)(2,1)}), bf16[8,160,768]{2,1,0:T(8,128)(2,1)}, u32[]{:S(2)}, u32[]{:S(2)}) async-start(bf16[8,160,768]{2,1,0:T(8,128)(2,1)} %bitcast.8), calls=%async_computation | async-start | bytes 3932160 | tf_op jit(solution)/shard_map/all_to_all | solution.py:1330
  59.5 0.6 reshape.165.live_row
  60.1 0.2 reduce-window.8
  60.3 0.1 convert_reduce_fusion.2
  60.3 0.6 reshape.164.segment_row
  60.9 0.9 reshape.179.segment_col
  61.8 1.0 slice.83
  62.9 0.2 convert_reduce_fusion
  63.1 0.4 fusion.10
  63.5 0.1 copy.117
  63.7 0.4 fusion.13.normed_ref
  64.1 6.1 %convolution_convert_fusion.query_ref.keys_ref.values_ref.qkv_ref = bf16[576,2304]{1,0:T(8,128)(2,1)} fusion(bf16[576,768]{1,0:T(8,128)(2,1)S(1)} %fusion.13.normed_ref, bf16[768,2304]{1,0:T(8,128)(2,1)} %slice.86), kind=kOutput, calls=%fused_computation | convolution fusion | flops 2039758848 | bytes 7077888 | tf_op jit(solution)/shard_map/dot_general | solution.py:1384
  70.2 14.4 %attend.1.mixed_ref = bf16[576,768]{1,0:T(8,128)(2,1)} custom-call(s32[576,1]{1,0:T(8,128)} %reshape.179.segment_col, s32[1,576]{1,0:T(1,128)} %reshape.164.segment_row, s32[1,576]{1,0:T(1,128)} %reshape.165.live_row, bf16[576,2304]{1,0:T(8,128)(2,1)} %convolution_convert_fusion.query_ref.keys_ref.values_ref.qkv_ref, ...), custom_call_target="tpu_custom_call" | custom-call | flops 4076863488 | bytes 4194304 | tf_op jit(solution)/shard_map/attend/pallas_call | solution.py:605
  84.5 2.5 fusion.80
  87.0 1.0 copy.111.routes_ref
  88.1 0.9 broadcast_in_dim.9.live_col
  88.9 0.6 convert_element_type.156.b_back_ref
  89.5 0.6 convert_element_type.155.b_in_ref
  90.1 0.3 multiply_reduce_fusion
  90.5 0.4 add_convert_fusion.routed_ref
  90.9 1.5 fusion.81
  92.4 0.1 copy.106
  92.6 0.3 fusion.47
  92.8 0.6 fusion.40
  93.4 1.5 add_reduce_fusion
  94.9 0.1 reshape.169
  95.1 0.8 pad.19.probs_ref
  95.8 2.4 convolution_convert_fusion.1
  98.4 0.6 bitcast_convert_fusion.1.vectors_ref
  99.0 2.3 fusion.1
  101.3 4.2 %all-to-all-done = bf16[8,160,768]{2,1,0:T(8,128)(2,1)} async-done(((bf16[8,160,768]{2,1,0:T(8,128)(2,1)}), bf16[8,160,768]{2,1,0:T(8,128)(2,1)}, u32[]{:S(2)}, u32[]{:S(2)}) %all-to-all-start) | async-done | bytes 1966112 | tf_op jit(solution)/shard_map/all_to_all | solution.py:1330
  105.5 81.5 %experts.1 = (bf16[8,160,768]{2,1,0:T(8,128)(2,1)}, bf16[1280,768]{1,0:T(8,128)(2,1)}, bf16[2,784,768]{2,1,0:T(8,128)(2,1)}, bf16[2,768,768]{2,1,0:T(8,128)(2,1)}) custom-call(bf16[8,160,768]{2,1,0:T(8,128)(2,1)} %copy-done.19, bf16[1280,768]{1,0:T(8,128)(2,1)} %bitcast.13.grad_ref, bf16[768,3072]{1,0:T(8,128)(2,1)} %bitcast.55, bf16[3072,768]{1,0:T(8,128)(2,1)} %bitcast.56, ...), custom_call_target="tpu_custom_call" | custom-call | flops 36238786560 | bytes 41943040 | tf_op jit(solution)/shard_map/experts/pallas_call | solution.py:536
  187.1 0.8 slice_bitcast_fusion
  187.9 0.1 reshape.172
  188.0 0.6 pad.18.terms_ref
  188.6 175.1 %backward.1 = (bf16[576,768]{1,0:T(8,128)(2,1)}, f32[576,768]{1,0:T(8,128)}, f32[24,2304]{1,0:T(8,128)}, f32[24,768]{1,0:T(8,128)}, f32[24,128]{1,0:T(8,128)}, /...) custom-call(bf16[1280,768]{1,0:T(8,128)(2,1)} %bitcast.46, ...), custom_call_target="tpu_custom_call" | custom-call | tf_op jit(solution)/shard_map/backward/pallas_call | solution.py:1320
  363.7 1.4 bitcast_convert_fusion
  365.1 0.8 slice.81
  365.9 1.6 slice_reduce_fusion
  367.5 0.6 convert.21
  368.2 1.4 copy.114
  369.5 2.1 copy.125
  371.7 1.2 copy.126
  372.9 0.7 copy.127
  373.6 0.6 copy.128
  374.2 8.8 %copy.129 = f32[1,768,3072]{2,1,0:T(8,128)} copy(f32[1,768,3072]{2,1,0:T(8,128)} %bitcast.45) | data formatting | bytes 18874368
  383.0 3.7 copy.130
  (64 shorter events, 0.3 us)
Async XLA Ops:
  0.6 6.1 %copy-start.10 = (s32[576,2]{0,1:T(2,128)S(1)}, s32[576,2]{0,1:T(2,128)}, u32[]{:S(2)}) copy-start(s32[576,2]{0,1:T(2,128)} %param.30) | copy-start | bytes 13828
  0.7 6.1 %copy-start.15 = (bf16[24]{0:T(256)(128)(2,1)S(1)}, bf16[24]{0:T(256)(128)(2,1)}, u32[]{:S(2)}) copy-start(bf16[24]{0:T(256)(128)(2,1)} %param.18) | copy-start | bytes 148
  0.7 6.2 %copy-start.16 = (bf16[24]{0:T(256)(128)(2,1)S(1)}, bf16[24]{0:T(256)(128)(2,1)}, u32[]{:S(2)}) copy-start(bf16[24]{0:T(256)(128)(2,1)} %param.19) | copy-start | bytes 148
  0.7 6.3 %copy-start.17 = (bf16[24]{0:T(256)(128)(2,1)S(1)}, bf16[24]{0:T(256)(128)(2,1)}, u32[]{:S(2)}) copy-start(bf16[24]{0:T(256)(128)(2,1)} %param.22) | copy-start | bytes 148
  0.7 6.4 %copy-start.18 = (bf16[24]{0:T(256)(128)(2,1)S(1)}, bf16[24]{0:T(256)(128)(2,1)}, u32[]{:S(2)}) copy-start(bf16[24]{0:T(256)(128)(2,1)} %param.23) | copy-start | bytes 148
  0.7 6.5 %copy-start.14 = (bf16[24,8]{0,1:T(8,128)(2,1)S(1)}, bf16[24,8]{0,1:T(8,128)(2,1)}, u32[]{:S(2)}) copy-start(bf16[24,8]{0,1:T(8,128)(2,1)} %param.24) | copy-start | bytes 1156
  0.7 6.7 %copy-start.11 = (bf16[24,768]{1,0:T(8,128)(2,1)S(1)}, bf16[24,768]{1,0:T(8,128)(2,1)}, u32[]{:S(2)}) copy-start(bf16[24,768]{1,0:T(8,128)(2,1)} %param.21) | copy-start | bytes 110596
  0.7 6.7 %copy-start.7 = (bf16[24,2304]{1,0:T(8,128)(2,1)S(1)}, bf16[24,2304]{1,0:T(8,128)(2,1)}, u32[]{:S(2)}) copy-start(bf16[24,2304]{1,0:T(8,128)(2,1)} %param.20) | copy-start | bytes 331780
  45.4 4.1 %copy-start.5 = (bf16[576,768]{1,0:T(8,128)(2,1)S(1)}, bf16[576,768]{1,0:T(8,128)(2,1)}, u32[]{:S(2)}) copy-start(bf16[576,768]{1,0:T(8,128)(2,1)} %cotangent_ref.1) | copy-start | bytes 2654212
  53.2 6.3 %copy-start.9 = (s32[576]{0:T(1024)S(1)}, s32[576]{0:T(1024)}, u32[]{:S(2)}) copy-start(s32[576]{0:T(1024)} %param.32) | copy-start | bytes 6916
  53.2 6.9 %copy-start.20 = (s32[1,3]{1,0:T(1,128)S(1)}, s32[1,3]{1,0:T(1,128)}, u32[]{:S(2)}) copy-start(s32[1,3]{1,0:T(1,128)} %param.29) | copy-start | bytes 40
  53.2 9.6 %copy-start.1 = (bf16[576,768]{1,0:T(8,128)(2,1)S(1)}, bf16[576,768]{1,0:T(8,128)(2,1)}, u32[]{:S(2)}) copy-start(bf16[576,768]{1,0:T(8,128)(2,1)} %tokens_ref.1) | copy-start | bytes 2654212
  53.2 52.3 %all-to-all-start = ((bf16[8,160,768]{2,1,0:T(8,128)(2,1)}), bf16[8,160,768]{2,1,0:T(8,128)(2,1)}, u32[]{:S(2)}, u32[]{:S(2)}) async-start(bf16[8,160,768]{2,1,0:T(8,128)(2,1)} %bitcast.8), calls=%async_computation | async-start | bytes 3932160 | tf_op jit(solution)/shard_map/all_to_all | solution.py:1330
  64.1 6.1 %copy-start.3 = (bf16[576,768]{1,0:T(8,128)(2,1)}, bf16[576,768]{1,0:T(8,128)(2,1)S(1)}, u32[]{:S(2)}) copy-start(bf16[576,768]{1,0:T(8,128)(2,1)S(1)} %fusion.13.normed_ref) | copy-start | bytes 2654212
  84.5 4.4 %copy-start.13 = (bf16[1,768]{1,0:T(2,128)(2,1)S(1)}, bf16[1,768]{1,0:T(2,128)(2,1)}, u32[]{:S(2)}) copy-start(bf16[1,768]{1,0:T(2,128)(2,1)} %param.28) | copy-start | bytes 4612
  84.5 5.0 %copy-start.12 = (bf16[1,3072]{1,0:T(2,128)(2,1)S(1)}, bf16[1,3072]{1,0:T(2,128)(2,1)}, u32[]{:S(2)}) copy-start(bf16[1,3072]{1,0:T(2,128)(2,1)} %param.26) | copy-start | bytes 18436
  87.0 3.8 copy-start
  90.9 7.4 %copy-start.2 = (bf16[576,768]{1,0:T(8,128)(2,1)}, bf16[576,768]{1,0:T(8,128)(2,1)S(1)}, u32[]{:S(2)}) copy-start(bf16[576,768]{1,0:T(8,128)(2,1)S(1)} %add_convert_fusion.routed_ref) | copy-start | bytes 2654212
  98.3 7.2 %copy-start.19 = (bf16[8,160,768]{2,1,0:T(8,128)(2,1)}, bf16[8,160,768]{2,1,0:T(8,128)(2,1)S(1)}, u32[]{:S(2)}) copy-start(bf16[8,160,768]{2,1,0:T(8,128)(2,1)S(1)} %fusion.64.send_ref) | copy-start | bytes 5898244
  363.7 8.0 %copy-start.4 = (f32[576,768]{1,0:T(8,128)S(1)}, f32[576,768]{1,0:T(8,128)}, u32[]{:S(2)}) copy-start(f32[576,768]{1,0:T(8,128)} %get-tuple-element.144) | copy-start | bytes 5308420
  371.7 1.2 copy-start.6
  371.7 1.9 copy-start.8
  372.9 10.1 %slice-start = ((s8[9437184]{0:T(1024)(128)(4,1)}), s8[4194304]{0:T(1024)(128)(4,1)S(1)}, s32[]{:S(2)}) async-start(s8[9437184]{0:T(1024)(128)(4,1)} %bitcast.42), calls=%async_computation.1 | async-start | bytes 8388608
  374.2 8.8 %slice-start.1 = ((s8[9437184]{0:T(1024)(128)(4,1)}), s8[4194304]{0:T(1024)(128)(4,1)S(1)}, s32[]{:S(2)}) async-start(s8[9437184]{0:T(1024)(128)(4,1)} %bitcast.42), calls=%async_computation.2 | async-start | bytes 8388608
  374.2 8.8 %slice-start.2 = ((s8[9437184]{0:T(1024)(128)(4,1)}), s8[1048576]{0:T(1024)(128)(4,1)S(1)}, s32[]{:S(2)}) async-start(s8[9437184]{0:T(1024)(128)(4,1)} %bitcast.42), calls=%async_computation.3 | async-start | bytes 2097152

commit v4 on v3

--- a/solution.py
+++ b/solution.py
@@ -661,10 +661,9 @@
     sum_qkv_ref,
     sum_out_ref,
     sum_small_ref,
-    total_back_ref,
-    total_in_ref,
     all_back_ref,
     all_in_ref,
+    all_tail_ref,
     *refs,
 ):
     devices = experts * reps
@@ -700,12 +699,8 @@
         own_in,
         other_back,
         other_in,
-        cast_back,
-        cast_in,
-        full_back,
-        full_in,
-    ) = refs[:28]
-    refs = refs[28:]
+    ) = refs[:24]
+    refs = refs[24:]
     count = len(chunks) if summed else 0
     parts, refs = (refs[:count], refs[count:])
     recvs, refs = ([refs[c * bits : (c + 1) * bits] for c in range(count)], refs[count * bits :])
@@ -719,7 +714,7 @@
         half_recv,
         all_send,
         all_recv,
-        cast_sem,
+        own_sem,
     ) = refs
     padded = result_ref.shape[0] // experts
     piece = half_in_ref.shape[2]
@@ -977,7 +972,69 @@
         grad_attn[...], weights[:, 3 * D : 4 * D], contract_last, preferred_element_type=jnp.float32
     ).astype(jnp.bfloat16)
 
+    sums = ((own_back, other_back), (own_in, other_in))
+    kinds = ((0, 2), (1,))
+
+    def own_part(kind):
+        return (own_back.at[pl.ds(0, piece), :], own_in, own_back.at[pl.ds(piece, 16), :])[kind]
+
+    def landing(kind, owner):
+        if kind == 0:
+            return all_back_ref.at[pl.ds(pl.multiple_of(owner * piece, 16), piece), :]
+        if kind == 1:
+            return all_in_ref.at[:, pl.ds(pl.multiple_of(owner * piece, LANES), piece)]
+        return all_tail_ref.at[owner]
+
+    def spread(kind, source, owner, device, step):
+        return pltpu.make_async_remote_copy(
+            src_ref=source,
+            dst_ref=landing(kind, owner),
+            send_sem=all_send.at[kind, step],
+            recv_sem=all_recv.at[kind, step],
+            device_id=device,
+            device_id_type=MESH_ID,
+        )
+
+    def own_moves(kind):
+        moves = [pltpu.make_async_copy(own_part(kind), landing(kind, rep), own_sem.at[kind])]
+        for step in range(1, half):
+            other = lax.rem(along + step, half)
+            moves.append(spread(kind, own_part(kind), rep, (mine, 2 * other + core), step))
+        moves.append(spread(kind, own_part(kind), rep, (mine, flip(rep, 0)), 0))
+        return moves
+
+    def complete(number):
+        own, others = sums[number]
+        for step in range(1, half):
+            half_moves[step - 1][number].wait_recv()
+        size = 16
+        steps = own.shape[0] // size
+
+        def one(step, carry):
+            here = pl.ds(pl.multiple_of(step * size, 16), size)
+            total = own[here, :].astype(jnp.float32)
+            for step in range(1, half):
+                total = total + others[step - 1, here, :].astype(jnp.float32)
+            own[here, :] = total.astype(jnp.bfloat16)
+            return carry
+
+        lax.fori_loop(0, steps, one, 0)
+        for kind in kinds[number]:
+            for move in own_moves(kind):
+                move.start()
+
+    complete(0)
+    absorb(out_chunk, 0)
+
     def attend_back(pair, carry):
+        @pl.when(pair == 1)
+        def _():
+            absorb(out_chunk, 1)
+
+        @pl.when(pair == 3)
+        def _():
+            complete(1)
+
         base = pl.multiple_of(pair * 2 * HEAD, 2 * HEAD)
         queries = qkv[:, pl.ds(base, 2 * HEAD)]
         keys = qkv[:, pl.ds(base + D, 2 * HEAD)]
@@ -1020,57 +1077,20 @@
 
     lax.fori_loop(0, HEADS // 2, attend_back, 0)
 
-    arrays = ((own_back, other_back, all_back_ref), (own_in, other_in, all_in_ref))
-
-    def complete(kind):
-        own, others, everywhere = arrays[kind]
-        for step in range(1, half):
-            half_moves[step - 1][kind].wait_recv()
-        size = 16
-        steps = own.shape[0] // size
-
-        def one(step, carry):
-            here = pl.ds(pl.multiple_of(step * size, 16), size)
-            total = own[here, :].astype(jnp.float32)
-            for step in range(1, half):
-                total = total + others[step - 1, here, :].astype(jnp.float32)
-            own[here, :] = total.astype(jnp.bfloat16)
-            return carry
-
-        lax.fori_loop(0, steps, one, 0)
-        local = pltpu.make_async_copy(own, everywhere.at[rep], cast_sem.at[4 + kind])
-        local.start()
-        moves = []
-        for step in range(1, half):
-            other = lax.rem(along + step, half)
-            moves.append(spread(kind, own, rep, (mine, 2 * other + core), step))
-        moves.append(spread(kind, own, rep, (mine, flip(rep, 0)), 0))
-        for move in moves:
-            move.start()
-        return (local, moves)
-
-    def spread(kind, source, owner, device, step):
-        return pltpu.make_async_remote_copy(
-            src_ref=source,
-            dst_ref=arrays[kind][2].at[owner],
-            send_sem=all_send.at[kind, step],
-            recv_sem=all_recv.at[kind, step],
-            device_id=device,
-            device_id_type=MESH_ID,
-        )
-
-    finals = [complete(0)]
-    for c in qkv_chunks:
+    for position, c in enumerate(qkv_chunks):
         start = chunks[c][1]
         wide[...] = lax.dot_general(
             normed[...], grad_qkv[:, start : start + D], contract_first, preferred_element_type=jnp.float32
         )
         send_chunk(c)
-    absorb(out_chunk, 0)
-    finals.append(complete(1))
+        if position > 0:
+            absorb(qkv_chunks[position - 1], 0)
+    absorb(out_chunk, 2)
     tall[...] = lax.dot_general(
         grad_qkv[...], weights[:, : 3 * D], contract_last, preferred_element_type=jnp.float32
     )
+    absorb(qkv_chunks[2], 0)
+    absorb(qkv_chunks[0], 1)
 
     def first_norm(step, carry):
         here = band(step)
@@ -1094,12 +1114,8 @@
         wide[span, :LANES] = block
     send_chunk(small_chunk)
 
-    order = [out_chunk] + qkv_chunks + [small_chunk]
-    for step in range(bits + len(order) - 1):
-        for position, c in enumerate(order):
-            phase = step - position
-            if 0 <= phase < bits and not (c == out_chunk and phase == 0):
-                absorb(c, phase)
+    absorb(qkv_chunks[1], 1)
+    absorb(out_chunk, 3)
 
     own_result.wait()
 
@@ -1123,73 +1139,38 @@
         + gates[1] * jnp.dot(second[...], returned[...], preferred_element_type=jnp.float32)
     ).astype(jnp.bfloat16)
 
-    forwards = []
-    pending = [None, None]
-
-    def convert(owner, first_wait):
-        for kind in range(2):
-            staged, full = ((cast_back, full_back), (cast_in, full_in))[kind]
-            size = staged.shape[0]
-            whole = (piece, D)[kind]
-            for block in range(whole // size):
-                span = pl.ds(block * size, size)
-                load = pltpu.make_async_copy(
-                    arrays[kind][2].at[owner, span, :], staged, cast_sem.at[kind]
-                )
-                load.start()
-                load.wait()
-                if pending[kind] is not None:
-                    pending[kind].wait()
-
-                def one(step, carry):
-                    here = pl.ds(pl.multiple_of(step * 48, 16), 48)
-                    full[here, :] = staged[here, :].astype(jnp.float32)
-                    return carry
-
-                lax.fori_loop(0, size // 48, one, 0)
-                if kind == 0:
-                    target = total_back_ref.at[
-                        pl.ds(pl.multiple_of(owner * piece + block * size, 16), size), :
-                    ]
-                else:
-                    target = total_in_ref.at[span, pl.ds(pl.multiple_of(owner * piece, LANES), piece)]
-                store = pltpu.make_async_copy(full, target, cast_sem.at[2 + kind])
-                store.start()
-                pending[kind] = store
-
-    for local, _ in finals:
-        local.wait()
-    convert(rep, True)
+    order = [out_chunk] + qkv_chunks + [small_chunk]
+    done = {out_chunk: 4, qkv_chunks[0]: 2, qkv_chunks[1]: 2, qkv_chunks[2]: 1, small_chunk: 0}
+    for step in range(bits + len(order) - 1):
+        for position, c in enumerate(order):
+            phase = step - position
+            if done[c] <= phase < bits:
+                absorb(c, phase)
+
     partner = flip(rep, 0)
-    for kind in range(2):
-        spread(kind, arrays[kind][2].at[partner], partner, (mine, partner), 0).wait_recv()
-    convert(partner, True)
-    for step in range(1, half):
-        came = lax.rem(along + half - step, half)
-        owner = 2 * came + core
-        for kind in range(2):
-            spread(kind, arrays[kind][2].at[owner], owner, (mine, owner), step).wait_recv()
-            forward = spread(
-                kind, arrays[kind][2].at[owner], owner, (mine, partner), half + step - 1
-            )
-            forward.start()
-            forwards.append(forward)
-        convert(owner, True)
-    for step in range(1, half):
-        came = lax.rem(along + half - step, half)
-        owner = 2 * came + 1 - core
-        for kind in range(2):
+
+    def passed_on(kind, step):
+        owner = 2 * lax.rem(along + half - step, half) + core
+        return spread(kind, landing(kind, owner), owner, (mine, partner), half + step - 1)
+
+    for kind in (0, 2, 1):
+        for step in range(1, half):
+            owner = 2 * lax.rem(along + half - step, half) + core
+            spread(kind, landing(kind, owner), owner, (mine, owner), step).wait_recv()
+            passed_on(kind, step).start()
+    for kind in (0, 2, 1):
+        spread(kind, landing(kind, partner), partner, (mine, partner), 0).wait_recv()
+        for step in range(1, half):
+            owner = 2 * lax.rem(along + half - step, half) + 1 - core
             spread(
-                kind, arrays[kind][2].at[owner], owner, (mine, partner), half + step - 1
+                kind, landing(kind, owner), owner, (mine, partner), half + step - 1
             ).wait_recv()
-        convert(owner, True)
-    for copy in pending:
-        copy.wait()
-    for copy in forwards:
-        copy.wait_send()
-    for _, moves in finals:
-        for move in moves:
+        moves = own_moves(kind)
+        moves[0].wait()
+        for move in moves[1:]:
             move.wait_send()
+        for step in range(1, half):
+            passed_on(kind, step).wait_send()
     for moves in half_moves:
         for move in moves:
             move.wait_send()
@@ -1267,10 +1248,6 @@
         pltpu.VMEM((D, piece), low),
         pltpu.VMEM((half - 1, tail_rows, D), low),
         pltpu.VMEM((half - 1, D, piece), low),
-        pltpu.VMEM((piece // 2, D), low),
-        pltpu.VMEM((D // 2, piece), low),
-        pltpu.VMEM((piece // 2, D), full),
-        pltpu.VMEM((D // 2, piece), full),
     ]
     summed = rows % 8 == 0
     for _, _, width in chunks if summed else ():
@@ -1287,11 +1264,10 @@
         pltpu.SemaphoreType.DMA((dense,)),
         pltpu.SemaphoreType.DMA((2, half - 1)),
         pltpu.SemaphoreType.DMA((2, half - 1)),
-        pltpu.SemaphoreType.DMA((2, reps)),
-        pltpu.SemaphoreType.DMA((2, reps)),
-        pltpu.SemaphoreType.DMA((6,)),
+        pltpu.SemaphoreType.DMA((3, reps)),
+        pltpu.SemaphoreType.DMA((3, reps)),
+        pltpu.SemaphoreType.DMA((3,)),
     ]
-    hidden = piece * reps
     call = pl.pallas_call(
         functools.partial(backward_kernel, experts, reps, chunks, summed),
         out_shape=[
@@ -1300,17 +1276,16 @@
             jax.ShapeDtypeStruct((rows if summed else D, 3 * D), full),
             jax.ShapeDtypeStruct((rows if summed else D, D), full),
             jax.ShapeDtypeStruct((rows if summed else D, LANES), full),
-            jax.ShapeDtypeStruct((hidden, D), full),
-            jax.ShapeDtypeStruct((D, hidden), full),
-            jax.ShapeDtypeStruct((reps, tail_rows, D), low),
-            jax.ShapeDtypeStruct((reps, D, piece), low),
+            jax.ShapeDtypeStruct((reps * piece, D), low),
+            jax.ShapeDtypeStruct((D, reps * piece), low),
+            jax.ShapeDtypeStruct((reps, tail_rows - piece, D), low),
         ],
         in_specs=[anywhere] * 4
         + [inside] * 3
         + [anywhere] * 8
         + [inside] * 4
         + [anywhere] * 2,
-        out_specs=[inside] * 2 + [inside if summed else anywhere] * 3 + [anywhere] * 4,
+        out_specs=[inside] * 2 + [inside if summed else anywhere] * 3 + [anywhere] * 3,
         scratch_shapes=scratch,
         compiler_params=pltpu.CompilerParams(
             collective_id=1, has_side_effects=True, vmem_limit_bytes=63 * 1024 * 1024
@@ -1420,10 +1395,9 @@
         sum_qkv,
         sum_out,
         sum_small,
-        back_total,
-        in_total,
         all_back,
         all_in,
+        all_tail,
     ) = run_backward(
         (
             grad_buffer.reshape(experts * padded, D),
@@ -1465,10 +1439,10 @@
         vector_sums[:, 2],
         vector_sums[:, 3],
         sum_small[:, :experts],
-        in_total[None],
-        all_back[:, piece, :piece].astype(jnp.float32).reshape(1, hidden),
-        back_total[None],
-        all_back[:1, piece + 1, :].astype(jnp.float32),
+        all_in[None].astype(jnp.float32),
+        all_tail[:, 0, :piece].astype(jnp.float32).reshape(1, hidden),
+        all_back[None].astype(jnp.float32),
+        all_tail[:1, 1, :].astype(jnp.float32),
     )
 
 

time: 393 us -> 367 us (0.934)
  Pallas kernels: 308 us -> 284 us
  local copies, waits for them, and re-layouts: 34 us -> 21.8 us
  other arithmetic: 13.8 us -> 25.8 us
    pallas_call x1, Pallas kernels: 175 us -> 151 us  [run_backward(): gradients = list(call(*operands))]
    unnamed x58 -> x54, local copies, waits for them, and re-layouts: 19.9 us -> 7.7 us
    convert_element_type x2 -> x4, other arithmetic: 2.03 us -> 13.9 us  [the longest x1 7.52 us: on_device(): all_in[None].astype(jnp.float32)]
  transfers between devices with their start and end apart: 1 -> 1, of which waited for: 1 -> 1; matrix products, arithmetic and copies ran while one was open for 7% -> 8% of each run, Pallas kernels for 4% -> 4%
where the time goes in v4:
time: 367 us; the launch traced here: 362 us
  Pallas kernels  284 us (77%)
  other arithmetic  25.8 us (7%)
  local copies, waits for them, and re-layouts  21.8 us (6%)
  matrix products  19 us (5%)
  starting transfers between devices  6.24 us (2%)
    pallas_call x1, Pallas kernels, run_backward(): gradients = list(call(*operands))  151 us
    pallas_call x1, Pallas kernels, run_experts(): pl.pallas_call(functools.partial(expert_kernel, experts, capacity, padded...  81.6 us
    pallas_call x1, Pallas kernels, gather_blocks(): pl.pallas_call(functools.partial(gather_kernel, devices, reps), out_shape...  37.4 us
    pallas_call x1, Pallas kernels, attend(): pl.pallas_call(attend_kernel, grid=(pairs,), out_shape=jax.ShapeDtypeStru...  14.3 us
    unnamed x54, local copies, waits for them, and re-layouts  7.7 us
    convert_element_type x1, other arithmetic, on_device(): all_in[None].astype(jnp.float32)  7.52 us
  transfers between devices with their start and end apart: 1, of which 1 were waited for; matrix products, arithmetic and copies ran while one was open for 8% of the time, Pallas kernels for 4%

profile of v4, /device:TPU:0, one launch (start us, length us, event | category | flops | bytes accessed | tf_op | source)
XLA Modules:
  0.0 362.3 jit_solution(4938932769528915084)
XLA Ops:
  0.7 0.8 convert_element_type.146
  1.5 0.7 slice_reduce_fusion.5
  2.2 0.2 convert_reduce_fusion.1
  2.4 1.4 fusion.27
  3.8 0.7 compare_and_fusion.1
  4.5 0.8 add_reduce_fusion.2
  5.3 1.4 fusion.24
  6.8 0.1 copy.100
  6.9 0.1 copy.101
  7.0 0.1 copy.102
  7.1 0.1 copy.103
  7.2 0.1 copy.99
  7.3 0.1 concatenate.6
  7.4 0.7 fusion.55.own_ref
  8.1 37.4 %gather_dense.1 = bf16[32,24,3200]{2,1,0:T(8,128)(2,1)} custom-call(bf16[24,3200]{1,0:T(8,128)(2,1)} %fusion.55.own_ref), custom_call_target="tpu_custom_call" | custom-call | tf_op jit(solution)/shard_map/gather_dense/pallas_call | solution.py:151
  45.4 4.1 %slice.86 = bf16[768,2304]{1,0:T(8,128)(2,1)} slice(bf16[768,3200]{1,0:T(8,128)(2,1)} %bitcast.41), slice={[0:768], [0:2304]} | slice | bytes 7077888 | tf_op jit(solution)/shard_map/slice | solution.py:1339
  49.5 3.8 %convolution_convert_fusion.2 = bf16[1280,768]{1,0:T(8,128)(2,1)} fusion(bf16[576,768]{1,0:T(8,128)(2,1)S(1)} %copy-done.7, pred[576]{0:T(1024)(128)(4,1)S(1)} %compare_and_fusion, s32[576]{0:T(1024)S(1)} %add_reduce_fusion.1, s32[576]{0:T(1024)S(1)} %get-tuple-element.116, pred[576]{0:T(1024)(128)(4,1)S(1)} %get-tuple-element.119), kind=kOutput, calls=%fused_computation.4 | convolution fusion | flops 1140817920 | bytes 2856576 | tf_op jit(solution)/shard_map/dot_general | solution.py:1349
  53.3 6.2 %all-to-all-start = ((bf16[8,160,768]{2,1,0:T(8,128)(2,1)}), bf16[8,160,768]{2,1,0:T(8,128)(2,1)}, u32[]{:S(2)}, u32[]{:S(2)}) async-start(bf16[8,160,768]{2,1,0:T(8,128)(2,1)} %bitcast.8), calls=%async_computation | async-start | bytes 3932160 | tf_op jit(solution)/shard_map/all_to_all | solution.py:1305
  59.6 0.6 reshape.169.live_row
  60.2 0.2 reduce-window.8
  60.4 0.6 reshape.168.segment_row
  61.0 0.9 reshape.185.segment_col
  61.9 1.0 slice.83
  62.9 0.2 convert_reduce_fusion
  63.1 0.4 fusion.10
  63.5 0.1 copy.117
  63.7 0.4 fusion.13.normed_ref
  64.1 6.1 %convolution_convert_fusion.query_ref.keys_ref.values_ref.qkv_ref = bf16[576,2304]{1,0:T(8,128)(2,1)} fusion(bf16[576,768]{1,0:T(8,128)(2,1)S(1)} %fusion.13.normed_ref, bf16[768,2304]{1,0:T(8,128)(2,1)} %slice.86), kind=kOutput, calls=%fused_computation.2 | convolution fusion | flops 2039758848 | bytes 7077888 | tf_op jit(solution)/shard_map/dot_general | solution.py:1359
  70.2 14.3 %attend.1.mixed_ref = bf16[576,768]{1,0:T(8,128)(2,1)} custom-call(s32[576,1]{1,0:T(8,128)} %reshape.185.segment_col, s32[1,576]{1,0:T(1,128)} %reshape.168.segment_row, s32[1,576]{1,0:T(1,128)} %reshape.169.live_row, bf16[576,2304]{1,0:T(8,128)(2,1)} %convolution_convert_fusion.query_ref.keys_ref.values_ref.qkv_ref, ...), custom_call_target="tpu_custom_call" | custom-call | flops 4076863488 | bytes 4194304 | tf_op jit(solution)/shard_map/attend/pallas_call | solution.py:605
  84.5 2.5 fusion.80
  87.1 1.1 copy.111.routes_ref
  88.2 0.8 broadcast_in_dim.3.live_col
  89.0 0.6 convert_element_type.168.b_back_ref
  89.6 0.6 convert_element_type.167.b_in_ref
  90.2 0.3 multiply_reduce_fusion
  90.6 0.4 add_convert_fusion.routed_ref
  90.9 1.5 fusion.81
  92.5 0.1 copy.106
  92.6 0.3 fusion.47
  92.9 0.6 fusion.40
  93.5 1.5 add_reduce_fusion
  95.1 0.7 pad.19.probs_ref
  95.8 2.4 convolution_convert_fusion.1
  98.3 0.6 bitcast_convert_fusion.3.vectors_ref
  99.0 0.6 copy-done.21
  99.6 2.4 fusion.1
  102.0 3.6 all-to-all-done
  105.6 81.6 %experts.1 = (bf16[8,160,768]{2,1,0:T(8,128)(2,1)}, bf16[1280,768]{1,0:T(8,128)(2,1)}, bf16[2,784,768]{2,1,0:T(8,128)(2,1)}, bf16[2,768,768]{2,1,0:T(8,128)(2,1)}) custom-call(bf16[8,160,768]{2,1,0:T(8,128)(2,1)} %copy-done.21, bf16[1280,768]{1,0:T(8,128)(2,1)} %bitcast.13.grad_ref, bf16[768,3072]{1,0:T(8,128)(2,1)} %bitcast.55, bf16[3072,768]{1,0:T(8,128)(2,1)} %bitcast.56, ...), custom_call_target="tpu_custom_call" | custom-call | flops 36238786560 | bytes 41943040 | tf_op jit(solution)/shard_map/experts/pallas_call | solution.py:536
  187.2 0.8 slice_bitcast_fusion
  187.9 0.1 reshape.176
  188.0 0.6 pad.18.terms_ref
  188.7 151.2 %backward.1 = (bf16[576,768]{1,0:T(8,128)(2,1)}, f32[576,768]{1,0:T(8,128)}, f32[24,2304]{1,0:T(8,128)}, f32[24,768]{1,0:T(8,128)}, f32[24,128]{1,0:T(8,128)}, /...) custom-call(bf16[1280,768]{1,0:T(8,128)(2,1)} %bitcast.46, ...), custom_call_target="tpu_custom_call" | custom-call | tf_op jit(solution)/shard_map/backward/pallas_call | solution.py:1295
  339.8 1.3 bitcast_convert_fusion.2
  341.1 0.8 slice.81
  341.9 1.6 slice_reduce_fusion
  343.5 0.6 convert.24
  344.1 1.4 copy.114
  345.5 7.5 %bitcast_convert_fusion.1 = f32[1,768,3072]{2,1,0:T(8,128)} fusion(bf16[768,3072]{1,0:T(8,128)(2,1)} %get-tuple-element.38), kind=kLoop, calls=%fused_computation.1 | loop fusion | flops 2359296 | bytes 14155776 | tf_op jit(solution)/shard_map/convert_element_type | solution.py:1442
  353.0 4.5 %bitcast_convert_fusion = f32[1,3072,768]{2,1,0:T(8,128)} fusion(bf16[3072,768]{1,0:T(8,128)(2,1)S(1)} %copy-done.3), kind=kLoop, calls=%fused_computation | loop fusion | flops 2359296 | bytes 14155776 | tf_op jit(solution)/shard_map/convert_element_type | solution.py:1444
  357.5 0.9 copy.123
  358.4 0.9 copy-done.5
  359.3 1.2 copy.124
  360.5 0.7 copy.125
  361.2 0.6 copy.126
  (61 shorter events, 0.5 us)
Async XLA Ops:
  0.6 6.1 %copy-start.12 = (s32[576,2]{0,1:T(2,128)S(1)}, s32[576,2]{0,1:T(2,128)}, u32[]{:S(2)}) copy-start(s32[576,2]{0,1:T(2,128)} %param.30) | copy-start | bytes 13828
  0.7 6.1 %copy-start.17 = (bf16[24]{0:T(256)(128)(2,1)S(1)}, bf16[24]{0:T(256)(128)(2,1)}, u32[]{:S(2)}) copy-start(bf16[24]{0:T(256)(128)(2,1)} %param.18) | copy-start | bytes 148
  0.7 6.2 %copy-start.18 = (bf16[24]{0:T(256)(128)(2,1)S(1)}, bf16[24]{0:T(256)(128)(2,1)}, u32[]{:S(2)}) copy-start(bf16[24]{0:T(256)(128)(2,1)} %param.19) | copy-start | bytes 148
  0.7 6.3 %copy-start.19 = (bf16[24]{0:T(256)(128)(2,1)S(1)}, bf16[24]{0:T(256)(128)(2,1)}, u32[]{:S(2)}) copy-start(bf16[24]{0:T(256)(128)(2,1)} %param.22) | copy-start | bytes 148
  0.7 6.4 %copy-start.20 = (bf16[24]{0:T(256)(128)(2,1)S(1)}, bf16[24]{0:T(256)(128)(2,1)}, u32[]{:S(2)}) copy-start(bf16[24]{0:T(256)(128)(2,1)} %param.23) | copy-start | bytes 148
  0.7 6.5 %copy-start.16 = (bf16[24,8]{0,1:T(8,128)(2,1)S(1)}, bf16[24,8]{0,1:T(8,128)(2,1)}, u32[]{:S(2)}) copy-start(bf16[24,8]{0,1:T(8,128)(2,1)} %param.24) | copy-start | bytes 1156
  0.7 6.7 %copy-start.13 = (bf16[24,768]{1,0:T(8,128)(2,1)S(1)}, bf16[24,768]{1,0:T(8,128)(2,1)}, u32[]{:S(2)}) copy-start(bf16[24,768]{1,0:T(8,128)(2,1)} %param.21) | copy-start | bytes 110596
  0.7 6.7 %copy-start.9 = (bf16[24,2304]{1,0:T(8,128)(2,1)S(1)}, bf16[24,2304]{1,0:T(8,128)(2,1)}, u32[]{:S(2)}) copy-start(bf16[24,2304]{1,0:T(8,128)(2,1)} %param.20) | copy-start | bytes 331780
  45.4 4.1 %copy-start.7 = (bf16[576,768]{1,0:T(8,128)(2,1)S(1)}, bf16[576,768]{1,0:T(8,128)(2,1)}, u32[]{:S(2)}) copy-start(bf16[576,768]{1,0:T(8,128)(2,1)} %cotangent_ref.1) | copy-start | bytes 2654212
  53.3 6.3 %copy-start.11 = (s32[576]{0:T(1024)S(1)}, s32[576]{0:T(1024)}, u32[]{:S(2)}) copy-start(s32[576]{0:T(1024)} %param.32) | copy-start | bytes 6916
  53.3 6.8 %copy-start.22 = (s32[1,3]{1,0:T(1,128)S(1)}, s32[1,3]{1,0:T(1,128)}, u32[]{:S(2)}) copy-start(s32[1,3]{1,0:T(1,128)} %param.29) | copy-start | bytes 40
  53.3 9.6 %copy-start.1 = (bf16[576,768]{1,0:T(8,128)(2,1)S(1)}, bf16[576,768]{1,0:T(8,128)(2,1)}, u32[]{:S(2)}) copy-start(bf16[576,768]{1,0:T(8,128)(2,1)} %tokens_ref.1) | copy-start | bytes 2654212
  53.3 52.3 %all-to-all-start = ((bf16[8,160,768]{2,1,0:T(8,128)(2,1)}), bf16[8,160,768]{2,1,0:T(8,128)(2,1)}, u32[]{:S(2)}, u32[]{:S(2)}) async-start(bf16[8,160,768]{2,1,0:T(8,128)(2,1)} %bitcast.8), calls=%async_computation | async-start | bytes 3932160 | tf_op jit(solution)/shard_map/all_to_all | solution.py:1305
  64.1 6.1 %copy-start.4 = (bf16[576,768]{1,0:T(8,128)(2,1)}, bf16[576,768]{1,0:T(8,128)(2,1)S(1)}, u32[]{:S(2)}) copy-start(bf16[576,768]{1,0:T(8,128)(2,1)S(1)} %fusion.13.normed_ref) | copy-start | bytes 2654212
  84.5 4.5 %copy-start.15 = (bf16[1,768]{1,0:T(2,128)(2,1)S(1)}, bf16[1,768]{1,0:T(2,128)(2,1)}, u32[]{:S(2)}) copy-start(bf16[1,768]{1,0:T(2,128)(2,1)} %param.28) | copy-start | bytes 4612
  84.5 5.1 %copy-start.14 = (bf16[1,3072]{1,0:T(2,128)(2,1)S(1)}, bf16[1,3072]{1,0:T(2,128)(2,1)}, u32[]{:S(2)}) copy-start(bf16[1,3072]{1,0:T(2,128)(2,1)} %param.26) | copy-start | bytes 18436
  87.1 3.9 %copy-start = (f32[576,768]{1,0:T(8,128)}, f32[576,768]{1,0:T(8,128)S(1)}, u32[]{:S(2)}) copy-start(f32[576,768]{1,0:T(8,128)S(1)} %get-tuple-element.125.resid_ref) | copy-start | bytes 5308420
  90.9 7.3 %copy-start.2 = (bf16[576,768]{1,0:T(8,128)(2,1)}, bf16[576,768]{1,0:T(8,128)(2,1)S(1)}, u32[]{:S(2)}) copy-start(bf16[576,768]{1,0:T(8,128)(2,1)S(1)} %add_convert_fusion.routed_ref) | copy-start | bytes 2654212
  98.3 1.3 copy-start.21
  345.5 7.5 %copy-start.3 = (bf16[3072,768]{1,0:T(8,128)(2,1)S(1)}, bf16[3072,768]{1,0:T(8,128)(2,1)}, u32[]{:S(2)}) copy-start(bf16[3072,768]{1,0:T(8,128)(2,1)} %get-tuple-element.40) | copy-start | bytes 14155780
  353.0 4.5 %copy-start.6 = (bf16[576,768]{1,0:T(8,128)(2,1)S(1)}, bf16[576,768]{1,0:T(8,128)(2,1)}, u32[]{:S(2)}) copy-start(bf16[576,768]{1,0:T(8,128)(2,1)} %get-tuple-element.143) | copy-start | bytes 2654212
  357.5 1.8 copy-start.5
  359.3 1.2 copy-start.8
  359.3 1.9 copy-start.10

commit v5 on v4

--- a/solution.py
+++ b/solution.py
@@ -214,6 +214,7 @@
     away_in,
     other_back,
     other_in,
+    came_back,
     load_sem,
     send_sem,
     recv_sem,
@@ -222,6 +223,8 @@
     result_sem,
     core_send,
     core_recv,
+    along_send,
+    along_recv,
     stage_sem,
 ):
     mine = lax.axis_index("exp")
@@ -244,6 +247,15 @@
     core = lax.rem(rep, 2)
     partner = (mine, flip(rep, 0))
     pl.semaphore_signal(barrier, inc=1, device_id=partner, device_id_type=MESH_ID)
+    half = away_in.shape[0]
+    along = lax.div(rep, 2)
+
+    def greet_along(step, carry):
+        other = 2 * lax.rem(along + step, half) + core
+        pl.semaphore_signal(barrier, inc=1, device_id=(mine, other), device_id_type=MESH_ID)
+        return carry
+
+    lax.fori_loop(1, half, greet_along, 0)
 
     def group_of(index):
         half = lax.div(mine, 2)
@@ -298,6 +310,7 @@
         )
 
     neighbour = flip(mine, 0)
+    side = lax.rem(mine, 2)
     loads = [
         pltpu.make_async_copy(send_ref.at[mine], slots.at[place(mine)], load_sem.at[0]),
         pltpu.make_async_copy(grad_ref, grads, load_sem.at[1]),
@@ -306,25 +319,39 @@
     ]
     for copy in loads:
         copy.start()
-    pl.semaphore_wait(barrier, experts)
+    pl.semaphore_wait(barrier, experts + half - 1)
 
     def send_group(index):
         pair = group_of(index)
-        outgoing(2 * pair).start()
-        outgoing(2 * pair + 1).start()
+        outgoing(2 * pair + side).start()
+        outgoing(2 * pair + 1 - side).start()
+
+    half_pair = lax.div(mine, 2)
+    inner = lax.rem(lax.rem(half_pair, 2) + lax.div(half_pair, 2), 2)
+
+    def turn(index):
+        if groups != 4:
+            return index
+        high, low = (lax.div(index, 2), lax.rem(index, 2))
+        return inner * (2 * high + lax.rem(low + high, 2)) + (1 - inner) * (2 * low + high)
 
     outgoing(neighbour).start()
-    if groups > 2:
-        send_group(2)
-    if groups > 1:
-        send_group(1)
+
+    def send_step(step, carry):
+        if groups == 4:
+            send_group(inner * (lax.rem(step + 1, 3) + 1) + (1 - inner) * (step + 1))
+        else:
+            send_group(step + 1)
+        return carry
+
+    lax.fori_loop(0, groups - 1, send_step, 0)
     for copy in loads:
         copy.wait()
 
     def send_back_group(index):
         pair = group_of(index)
-        going_back(2 * pair).start()
-        going_back(2 * pair + 1).start()
+        going_back(2 * pair + side).start()
+        going_back(2 * pair + 1 - side).start()
 
     def gate_columns(expert):
         tail = slots[pl.ds(pl.multiple_of(expert * padded + padded - 16, 16), 16), :].astype(jnp.float32)
@@ -332,7 +359,7 @@
         return column_of(row, padded)
 
     def group_step(index, carry):
-        pair = group_of(index)
+        pair = group_of(turn(index))
 
         @pl.when(index == 0)
         def _():
@@ -343,22 +370,18 @@
             incoming(2 * pair).wait_recv()
             incoming(2 * pair + 1).wait_recv()
 
-        @pl.when(jnp.logical_and(index >= 1, index + 2 < groups))
-        def _():
-            send_group(index + 2)
-
         @pl.when(index == 1)
         def _():
             going_back(neighbour).start()
 
         @pl.when(index > 1)
         def _():
-            send_back_group(index - 1)
+            send_back_group(turn(index - 1))
 
         here = pl.ds(pl.multiple_of(pair * 2 * padded, 16), 2 * padded)
-        for side in range(2):
-            spot = place(2 * pair + side)
-            gate = gate_columns(2 * pair + side)
+        for member in range(2):
+            spot = place(2 * pair + member)
+            gate = gate_columns(2 * pair + member)
             gated[spot, :] = (gate * grads[spot, :].astype(jnp.float32)).astype(jnp.bfloat16)
 
         def hidden_step(step, inner):
@@ -399,9 +422,9 @@
             return inner
 
         lax.fori_loop(0, steps, hidden_step, 0)
-        for side in range(2):
-            expert = 2 * pair + side
-            span = slice(side * padded, (side + 1) * padded)
+        for member in range(2):
+            expert = 2 * pair + member
+            span = slice(member * padded, (member + 1) * padded)
             spot = place(expert)
             result_low = (result_total[span, :] + b_back_ref[...]).astype(jnp.bfloat16)
             result_rows[spot, :] = result_low
@@ -430,86 +453,128 @@
         return carry
 
     lax.fori_loop(0, groups, group_step, 0)
-    if groups > 1:
-        send_back_group(groups - 1)
-    else:
-        going_back(neighbour).start()
     own_back = pltpu.make_async_copy(back_rows.at[place(mine)], return_ref.at[mine], load_sem.at[0])
     own_back.start()
     results = pltpu.make_async_copy(result_rows, result_ref, result_sem)
     results.start()
 
     piece = away_in.shape[2]
-    half = away_in.shape[0]
     bias_back = jnp.sum(gated[...].astype(jnp.float32), axis=0, keepdims=True)
 
-    def sums_of(number):
-        columns = pl.ds(pl.multiple_of(number * piece, LANES), piece)
+    def columns_of(number):
+        return pl.ds(pl.multiple_of(number * piece, LANES), piece)
+
+    def back_sums(number):
+        columns = columns_of(number)
         back = lax.dot_general(
             active[:, columns], gated[...], contract_first, preferred_element_type=jnp.float32
-        )
-        inward = lax.dot_general(
-            slots[...], grad_pre[:, columns], contract_first, preferred_element_type=jnp.float32
         )
         bias_in = jnp.sum(grad_pre[:, columns].astype(jnp.float32), axis=0, keepdims=True)
         if piece < D:
             bias_in = jnp.concatenate([bias_in, jnp.zeros((1, D - piece), jnp.float32)], axis=1)
         row = lax.broadcasted_iota(jnp.int32, (16, D), 0)
         extra = jnp.where(row == 0, bias_in, jnp.where(row == 1, bias_back, 0.0))
-        return (back, inward, extra)
-
-    def core_copies(index):
-        return [
-            pltpu.make_async_remote_copy(
-                src_ref=source.at[index],
-                dst_ref=target.at[index],
-                send_sem=core_send.at[kind, index],
-                recv_sem=core_recv.at[kind, index],
-                device_id=partner,
-                device_id_type=MESH_ID,
-            )
-            for kind, (source, target) in enumerate(
-                ((away_back, other_back), (away_in, other_in))
-            )
-        ]
-
-    def away_step(index, carry):
-        back, inward, extra = sums_of(2 * index + 1 - core)
+        return (back, extra)
+
+    def in_sums(number):
+        return lax.dot_general(
+            slots[...],
+            grad_pre[:, columns_of(number)],
+            contract_first,
+            preferred_element_type=jnp.float32,
+        )
+
+    def core_copy(kind, index):
+        source, target = ((away_back, other_back), (away_in, other_in))[kind]
+        return pltpu.make_async_remote_copy(
+            src_ref=source.at[index],
+            dst_ref=target.at[index],
+            send_sem=core_send.at[kind, index],
+            recv_sem=core_recv.at[kind, index],
+            device_id=partner,
+            device_id_type=MESH_ID,
+        )
+
+    def along_copy(step):
+        other = lax.rem(along + step, half)
+        return pltpu.make_async_remote_copy(
+            src_ref=other_back.at[other],
+            dst_ref=came_back.at[step - 1],
+            send_sem=along_send.at[step - 1],
+            recv_sem=along_recv.at[step - 1],
+            device_id=(mine, 2 * other + core),
+            device_id_type=MESH_ID,
+        )
+
+    def away_back_step(step, carry):
+        index = lax.rem(along + step, half)
+        back, extra = back_sums(2 * index + 1 - core)
         away_back[index, :piece, :] = back.astype(jnp.bfloat16)
         away_back[index, piece:, :] = extra.astype(jnp.bfloat16)
-        away_in[index] = inward.astype(jnp.bfloat16)
-        for copy in core_copies(index):
-            copy.start()
+        core_copy(0, index).start()
         return carry
 
-    def kept_copies(index):
-        return (
-            pltpu.make_async_copy(other_back.at[index], half_back_ref.at[index], stage_sem.at[0, index]),
-            pltpu.make_async_copy(other_in.at[index], half_in_ref.at[index], stage_sem.at[1, index]),
-        )
-
-    def kept_step(index, carry):
-        back, inward, extra = sums_of(2 * index + core)
-        for copy in core_copies(index):
-            copy.wait_recv()
+    def kept_back_step(step, carry):
+        index = lax.rem(along + step, half)
+        back, extra = back_sums(2 * index + core)
+        core_copy(0, index).wait_recv()
         other_back[index, :piece, :] = (
             back + other_back[index, :piece, :].astype(jnp.float32)
         ).astype(jnp.bfloat16)
         other_back[index, piece:, :] = (
             extra + other_back[index, piece:, :].astype(jnp.float32)
         ).astype(jnp.bfloat16)
+
+        @pl.when(step < half)
+        def _():
+            along_copy(step).start()
+
+        return carry
+
+    def away_in_step(index, carry):
+        away_in[index] = in_sums(2 * index + 1 - core).astype(jnp.bfloat16)
+        core_copy(1, index).start()
+        return carry
+
+    def kept_in_copy(index):
+        return pltpu.make_async_copy(other_in.at[index], half_in_ref.at[index], stage_sem.at[index])
+
+    def kept_in_step(index, carry):
+        inward = in_sums(2 * index + core)
+        core_copy(1, index).wait_recv()
         other_in[index] = (inward + other_in[index].astype(jnp.float32)).astype(jnp.bfloat16)
-        for copy in kept_copies(index):
-            copy.start()
+        kept_in_copy(index).start()
         return carry
 
-    lax.fori_loop(0, half, away_step, 0)
-    lax.fori_loop(0, half, kept_step, 0)
+    lax.fori_loop(1, half + 1, away_back_step, 0)
+    if groups > 1:
+        send_back_group(turn(groups - 1))
+    else:
+        going_back(neighbour).start()
+    lax.fori_loop(1, half + 1, kept_back_step, 0)
+    lax.fori_loop(0, half, away_in_step, 0)
+    lax.fori_loop(0, half, kept_in_step, 0)
+    for step in range(1, half):
+        along_copy(step).wait_recv()
+
+    def along_sum(step, carry):
+        here = pl.ds(pl.multiple_of(step * 16, 16), 16)
+        total = other_back[along, here, :].astype(jnp.float32)
+        for came in range(half - 1):
+            total = total + came_back[came, here, :].astype(jnp.float32)
+        other_back[along, here, :] = total.astype(jnp.bfloat16)
+        return carry
+
+    lax.fori_loop(0, (piece + 16) // 16, along_sum, 0)
+    sum_back = pltpu.make_async_copy(other_back.at[along], half_back_ref, stage_sem.at[half])
+    sum_back.start()
+    sum_back.wait()
+    for step in range(1, half):
+        along_copy(step).wait_send()
     for index in range(half):
-        for copy in kept_copies(index):
-            copy.wait()
-        for copy in core_copies(index):
-            copy.wait_send()
+        kept_in_copy(index).wait()
+        for kind in range(2):
+            core_copy(kind, index).wait_send()
     own_back.wait()
     results.wait()
 
@@ -538,7 +603,7 @@
         out_shape=[
             jax.ShapeDtypeStruct((experts, padded, D), low),
             jax.ShapeDtypeStruct((rows, D), low),
-            jax.ShapeDtypeStruct((half, piece + 16, D), low),
+            jax.ShapeDtypeStruct((piece + 16, D), low),
             jax.ShapeDtypeStruct((half, D, piece), low),
         ],
         in_specs=[anywhere, anywhere, anywhere, anywhere, inside, inside],
@@ -559,6 +624,7 @@
             pltpu.VMEM((half, D, piece), low),
             pltpu.VMEM((half, piece + 16, D), low),
             pltpu.VMEM((half, D, piece), low),
+            pltpu.VMEM((half - 1, piece + 16, D), low),
             pltpu.SemaphoreType.DMA((4,)),
             pltpu.SemaphoreType.DMA((experts,)),
             pltpu.SemaphoreType.DMA((experts,)),
@@ -567,10 +633,12 @@
             pltpu.SemaphoreType.DMA,
             pltpu.SemaphoreType.DMA((2, half)),
             pltpu.SemaphoreType.DMA((2, half)),
-            pltpu.SemaphoreType.DMA((2, half)),
+            pltpu.SemaphoreType.DMA((half - 1,)),
+            pltpu.SemaphoreType.DMA((half - 1,)),
+            pltpu.SemaphoreType.DMA((half + 1,)),
         ],
         compiler_params=pltpu.CompilerParams(
-            collective_id=2, has_side_effects=True, vmem_limit_bytes=60 * 1024 * 1024
+            collective_id=2, has_side_effects=True, vmem_limit_bytes=63 * 1024 * 1024
         ),
         cost_estimate=pl.CostEstimate(
             flops=12 * rows * D * hidden, bytes_accessed=40 << 20, transcendentals=2 * rows * hidden
@@ -695,12 +763,11 @@
         grad_mixed,
         grad_qkv,
         grad_logits,
-        own_back,
         own_in,
-        other_back,
         other_in,
-    ) = refs[:24]
-    refs = refs[24:]
+    ) = refs[:22]
+    refs = refs[22:]
+    lines, refs = (refs[0], refs[1:])
     count = len(chunks) if summed else 0
     parts, refs = (refs[:count], refs[count:])
     recvs, refs = ([refs[c * bits : (c + 1) * bits] for c in range(count)], refs[count * bits :])
@@ -746,7 +813,6 @@
         (qkv_ref, qkv),
         (normed_ref, normed),
         (tokens_ref, tokens),
-        (half_back_ref.at[along], own_back),
         (half_in_ref.at[along], own_in),
     ]
     loads = [
@@ -757,28 +823,52 @@
         copy.start()
     pl.semaphore_wait(barrier, experts - 1 + reps - 1)
 
-    def half_copies(step):
+    def half_copy(step):
         other = lax.rem(along + step, half)
-        came = lax.rem(along + half - step, half)
-        device = (mine, 2 * other + core)
-        return [
-            pltpu.make_async_remote_copy(
-                src_ref=source.at[other],
-                dst_ref=target.at[step - 1],
-                send_sem=half_send.at[kind, step - 1],
-                recv_sem=half_recv.at[kind, step - 1],
-                device_id=device,
-                device_id_type=MESH_ID,
-            )
-            for kind, (source, target) in enumerate(
-                ((half_back_ref, other_back), (half_in_ref, other_in))
-            )
-        ]
-
-    half_moves = [half_copies(step) for step in range(1, half)]
-    for kind in range(2):
-        for moves in half_moves:
-            moves[kind].start()
+        return pltpu.make_async_remote_copy(
+            src_ref=half_in_ref.at[other],
+            dst_ref=other_in.at[step - 1],
+            send_sem=half_send.at[step - 1],
+            recv_sem=half_recv.at[step - 1],
+            device_id=(mine, 2 * other + core),
+            device_id_type=MESH_ID,
+        )
+
+    half_moves = [half_copy(step) for step in range(1, half)]
+    for move in half_moves:
+        move.start()
+
+    def own_part(kind):
+        return (half_back_ref.at[pl.ds(0, piece), :], own_in, half_back_ref.at[pl.ds(piece, 16), :])[kind]
+
+    def landing(kind, owner):
+        if kind == 0:
+            return all_back_ref.at[pl.ds(pl.multiple_of(owner * piece, 16), piece), :]
+        if kind == 1:
+            return all_in_ref.at[:, pl.ds(pl.multiple_of(owner * piece, LANES), piece)]
+        return all_tail_ref.at[owner]
+
+    def spread(kind, source, owner, device, step):
+        return pltpu.make_async_remote_copy(
+            src_ref=source,
+            dst_ref=landing(kind, owner),
+            send_sem=all_send.at[kind, step],
+            recv_sem=all_recv.at[kind, step],
+            device_id=device,
+            device_id_type=MESH_ID,
+        )
+
+    def own_moves(kind):
+        moves = [pltpu.make_async_copy(own_part(kind), landing(kind, rep), own_sem.at[kind])]
+        for step in range(1, half):
+            other = lax.rem(along + step, half)
+            moves.append(spread(kind, own_part(kind), rep, (mine, 2 * other + core), step))
+        moves.append(spread(kind, own_part(kind), rep, (mine, flip(rep, 0)), 0))
+        return moves
+
+    for kind in (0, 2):
+        for move in own_moves(kind):
+            move.start()
 
     def place(expert):
         return pl.ds(pl.multiple_of(expert * padded, 16), padded)
@@ -865,71 +955,90 @@
 
     gain_two, bias_two = lax.fori_loop(0, SLOTS // BAND, second_norm, (zero, zero))
 
-    plan = [0] + [bit_count(reps)] + list(range(bits - 1, bit_count(reps), -1))
-    plan = plan + list(range(bit_count(reps) - 1, 0, -1))
+    lines[16:24, :] = gain_two
+    lines[24:32, :] = bias_two
+
+    own_bits = bit_count(reps)
+    plan = [0] + list(range(own_bits, bits)) + list(range(own_bits - 1, 0, -1))
     my_bit = [lax.rem(lax.div(me, 1 << bit), 2) for bit in range(bits)]
-    rows = parts[0].shape[3] if summed else 0
+    rows = parts[0].shape[4] if summed else 0
     stride = experts + bits - 1
-    outs = (sum_qkv_ref, sum_out_ref, sum_small_ref)
-
-    def fill(c):
-        width = chunks[c][2]
+    first_of = [sum(number for number, _ in chunks[:family]) for family in range(len(chunks))]
+
+    def turned(number):
+        length = bits - own_bits - 1
+        found = 0
+        for bit in range(length):
+            found = found + lax.rem(lax.div(number, 1 << bit), 2) * (1 << (length - 1 - bit))
+        return found
+
+    def fill(family, c):
+        width = chunks[family][1]
 
         def one(block, carry):
             owner = lax.div(block, reps)
             inner = lax.rem(block, reps)
-            parts[c][owner, lax.div(inner, 2), lax.rem(inner, 2)] = wide[
+            parts[family][c, owner, lax.div(inner, 2), lax.rem(inner, 2)] = wide[
                 pl.ds(pl.multiple_of(block * rows, rows), rows), :width
             ].astype(jnp.bfloat16)
             return carry
 
         lax.fori_loop(0, devices, one, 0)
 
-    def first_copy(c, expert):
-        spot = lax.rem(expert, 2) * (devices // 4) + lax.div(expert, 2) * half
+    def first_copy(family, c, expert):
+        spot = lax.rem(expert, 2) * (devices // 4) + turned(lax.div(expert, 2)) * half
+        index = (first_of[family] + c) * stride + expert
         return pltpu.make_async_remote_copy(
-            src_ref=parts[c].at[expert, :, 1 - core],
-            dst_ref=recvs[c][0].at[pl.ds(spot, half)],
-            send_sem=dense_send.at[c * stride + expert],
-            recv_sem=dense_recv.at[c * stride + expert],
+            src_ref=parts[family].at[c, expert, :, 1 - core],
+            dst_ref=recvs[family][0].at[c, pl.ds(spot, half)],
+            send_sem=dense_send.at[index],
+            recv_sem=dense_recv.at[index],
             device_id=(mine, flip(rep, 0)),
             device_id_type=MESH_ID,
         )
 
-    def later_copy(c, phase):
+    def later_copy(family, c, phase):
         size = devices >> (phase + 1)
-        index = c * stride + experts + phase - 1
+        index = (first_of[family] + c) * stride + experts + phase - 1
         return pltpu.make_async_remote_copy(
-            src_ref=recvs[c][phase - 1].at[pl.ds((1 - my_bit[plan[phase]]) * size, size)],
-            dst_ref=recvs[c][phase],
+            src_ref=recvs[family][phase - 1].at[c, pl.ds((1 - my_bit[plan[phase]]) * size, size)],
+            dst_ref=recvs[family][phase].at[c],
             send_sem=dense_send.at[index],
             recv_sem=dense_recv.at[index],
             device_id=coordinates(flip(me, plan[phase]), reps),
             device_id_type=MESH_ID,
         )
 
-    def send_chunk(c):
+    def columns_of(c, kind):
+        return pl.ds(pl.multiple_of(c * LANES + kind * D, LANES), LANES)
+
+    def send_chunk(family, c):
         if not summed:
-            array, start, width = chunks[c]
-            pltpu.sync_copy(wide.at[:, :width], outs[array].at[:, pl.ds(start, width)])
+            if family == 1:
+                for kind in range(3):
+                    span = slice(kind * LANES, (kind + 1) * LANES)
+                    pltpu.sync_copy(wide.at[:, span], sum_qkv_ref.at[:, columns_of(c, kind)])
+            else:
+                out = sum_out_ref if family == 0 else sum_small_ref
+                pltpu.sync_copy(wide.at[:, : chunks[family][1]], out)
             return
-        fill(c)
+        fill(family, c)
 
         def one(expert, carry):
-            first_copy(c, expert).start()
+            first_copy(family, c, expert).start()
             return carry
 
         lax.fori_loop(0, experts, one, 0)
 
-    def absorb(c, phase):
+    def absorb(family, c, phase):
         if not summed:
             return
         size = devices >> (phase + 1)
-        into = recvs[c][phase]
+        into = recvs[family][phase]
         if phase == 0:
 
             def arrived(expert, carry):
-                first_copy(c, expert).wait_recv()
+                first_copy(family, c, expert).wait_recv()
                 return carry
 
             lax.fori_loop(0, experts, arrived, 0)
@@ -937,104 +1046,75 @@
             def held(i):
                 side = lax.div(i, devices // 4)
                 rest = lax.rem(i, devices // 4)
-                return parts[c][2 * lax.div(rest, half) + side, lax.rem(rest, half), core]
+                expert = 2 * turned(lax.div(rest, half)) + side
+                return parts[family][c, expert, lax.rem(rest, half), core]
         else:
-            later_copy(c, phase).wait_recv()
+            later_copy(family, c, phase).wait_recv()
             base = my_bit[plan[phase]] * size
 
             def held(i):
-                return recvs[c][phase - 1][base + i]
+                return recvs[family][phase - 1][c, base + i]
 
         if phase == bits - 1:
-            array, start, width = chunks[c]
-            outs[array][:, pl.ds(start, width)] = into[0].astype(jnp.float32) + held(0).astype(
-                jnp.float32
-            )
+            total = into[c, 0].astype(jnp.float32) + held(0).astype(jnp.float32)
+            if family == 1:
+                for kind in range(3):
+                    sum_qkv_ref[:, columns_of(c, kind)] = total[:, kind * LANES : (kind + 1) * LANES]
+            elif family == 0:
+                sum_out_ref[...] = total
+            else:
+                sum_small_ref[...] = total
             return
 
         def one(i, carry):
-            into[i] = (into[i].astype(jnp.float32) + held(i).astype(jnp.float32)).astype(
+            into[c, i] = (into[c, i].astype(jnp.float32) + held(i).astype(jnp.float32)).astype(
                 jnp.bfloat16
             )
             return carry
 
         lax.fori_loop(0, size, one, 0)
-        later_copy(c, phase + 1).start()
-
-    out_chunk = [c for c in range(len(chunks)) if chunks[c][0] == 1][0]
-    small_chunk = [c for c in range(len(chunks)) if chunks[c][0] == 2][0]
-    qkv_chunks = [c for c in range(len(chunks)) if chunks[c][0] == 0]
+        later_copy(family, c, phase + 1).start()
+
     wide[...] = lax.dot_general(
         mixed[...], grad_attn[...], contract_first, preferred_element_type=jnp.float32
     )
-    send_chunk(out_chunk)
+    send_chunk(0, 0)
     grad_mixed[...] = lax.dot_general(
         grad_attn[...], weights[:, 3 * D : 4 * D], contract_last, preferred_element_type=jnp.float32
     ).astype(jnp.bfloat16)
 
-    sums = ((own_back, other_back), (own_in, other_in))
-    kinds = ((0, 2), (1,))
-
-    def own_part(kind):
-        return (own_back.at[pl.ds(0, piece), :], own_in, own_back.at[pl.ds(piece, 16), :])[kind]
-
-    def landing(kind, owner):
-        if kind == 0:
-            return all_back_ref.at[pl.ds(pl.multiple_of(owner * piece, 16), piece), :]
-        if kind == 1:
-            return all_in_ref.at[:, pl.ds(pl.multiple_of(owner * piece, LANES), piece)]
-        return all_tail_ref.at[owner]
-
-    def spread(kind, source, owner, device, step):
-        return pltpu.make_async_remote_copy(
-            src_ref=source,
-            dst_ref=landing(kind, owner),
-            send_sem=all_send.at[kind, step],
-            recv_sem=all_recv.at[kind, step],
-            device_id=device,
-            device_id_type=MESH_ID,
-        )
-
-    def own_moves(kind):
-        moves = [pltpu.make_async_copy(own_part(kind), landing(kind, rep), own_sem.at[kind])]
-        for step in range(1, half):
-            other = lax.rem(along + step, half)
-            moves.append(spread(kind, own_part(kind), rep, (mine, 2 * other + core), step))
-        moves.append(spread(kind, own_part(kind), rep, (mine, flip(rep, 0)), 0))
-        return moves
-
-    def complete(number):
-        own, others = sums[number]
-        for step in range(1, half):
-            half_moves[step - 1][number].wait_recv()
+    def complete():
+        for move in half_moves:
+            move.wait_recv()
         size = 16
-        steps = own.shape[0] // size
 
         def one(step, carry):
             here = pl.ds(pl.multiple_of(step * size, 16), size)
-            total = own[here, :].astype(jnp.float32)
-            for step in range(1, half):
-                total = total + others[step - 1, here, :].astype(jnp.float32)
-            own[here, :] = total.astype(jnp.bfloat16)
+            total = own_in[here, :].astype(jnp.float32)
+            for came in range(half - 1):
+                total = total + other_in[came, here, :].astype(jnp.float32)
+            own_in[here, :] = total.astype(jnp.bfloat16)
             return carry
 
-        lax.fori_loop(0, steps, one, 0)
-        for kind in kinds[number]:
-            for move in own_moves(kind):
-                move.start()
-
-    complete(0)
-    absorb(out_chunk, 0)
-
-    def attend_back(pair, carry):
-        @pl.when(pair == 1)
-        def _():
-            absorb(out_chunk, 1)
-
-        @pl.when(pair == 3)
-        def _():
-            complete(1)
-
+        lax.fori_loop(0, own_in.shape[0] // size, one, 0)
+        for move in own_moves(1):
+            move.start()
+
+    partner = flip(rep, 0)
+
+    def passed_on(kind, step):
+        owner = 2 * lax.rem(along + half - step, half) + core
+        return spread(kind, landing(kind, owner), owner, (mine, partner), half + step - 1)
+
+    def pass_on(kind):
+        for step in range(1, half):
+            owner = 2 * lax.rem(along + half - step, half) + core
+            spread(kind, landing(kind, owner), owner, (mine, owner), step).wait_recv()
+            passed_on(kind, step).start()
+
+    pairs = HEADS // 2
+
+    def attend_back(pair):
         base = pl.multiple_of(pair * 2 * HEAD, 2 * HEAD)
         queries = qkv[:, pl.ds(base, 2 * HEAD)]
         keys = qkv[:, pl.ds(base + D, 2 * HEAD)]
@@ -1069,95 +1149,111 @@
             done.append(
                 (grad_query * HEAD ** (-0.5), grad_key * HEAD ** (-0.5), grad_value)
             )
+        block = jnp.concatenate(
+            [jnp.concatenate([done[0][kind], done[1][kind]], axis=1) for kind in range(3)], axis=1
+        ).astype(jnp.bfloat16)
         for kind in range(3):
-            grad_qkv[:, pl.ds(base + kind * D, 2 * HEAD)] = jnp.concatenate(
-                [done[0][kind], done[1][kind]], axis=1
-            ).astype(jnp.bfloat16)
+            grad_qkv[:, pl.ds(base + kind * D, 2 * HEAD)] = block[:, kind * LANES : (kind + 1) * LANES]
+        wide[:, : 3 * LANES] = lax.dot_general(
+            normed[...], block, contract_first, preferred_element_type=jnp.float32
+        )
+        send_chunk(1, pair)
+
+    def finish_tokens():
+        tall[...] = lax.dot_general(
+            grad_qkv[...], weights[:, : 3 * D], contract_last, preferred_element_type=jnp.float32
+        )
+
+        def first_norm(step, carry):
+            here = band(step)
+            grad_in, grad_gain, grad_bias = norm_back(
+                tokens[here, :].astype(jnp.float32), tall[here, :], vectors_ref[0:1, :]
+            )
+            grad_tokens_ref[here, :] = grad_resid[here, :] + grad_in
+            return (carry[0] + grad_gain, carry[1] + grad_bias)
+
+        gain_one, bias_one = lax.fori_loop(0, SLOTS // BAND, first_norm, (zero, zero))
+        lines[0:8, :] = gain_one
+        lines[8:16, :] = bias_one
+        wide[:, :LANES] = lax.dot_general(
+            routed[...], grad_logits[...], contract_first, preferred_element_type=jnp.float32
+        )
+        sums = [jnp.sum(lines[8 * k : 8 * k + 8, :], axis=0, keepdims=True) for k in range(4)]
+        lane = lax.broadcasted_iota(jnp.int32, (LANES, LANES), 1)
+        for part in range(D // LANES):
+            span = slice(part * LANES, (part + 1) * LANES)
+            block = wide[span, :LANES]
+            for k in range(4):
+                block = jnp.where(lane == experts + k, column_of(sums[k][:, span], LANES), block)
+            wide[span, :LANES] = block
+        send_chunk(2, 0)
+
+    def finish_output():
+        own_result.wait()
+
+        def result_arrived(step, carry):
+            result_copy(step).wait_recv()
+            result_copy(step).wait_send()
+            return carry
+
+        lax.fori_loop(1, experts, result_arrived, 0)
+        lane = lax.broadcasted_iota(jnp.int32, (SLOTS, LANES), 1)
+        probs = probs_ref[...]
+        gates = [
+            jnp.sum(jnp.where(lane == routes_ref[:, k : k + 1], probs, 0.0), axis=1, keepdims=True)
+            for k in range(2)
+        ]
+        tall[...] = resid[...] + gates[0] * jnp.dot(
+            first[...], returned[...], preferred_element_type=jnp.float32
+        )
+        output_ref[...] = (
+            tall[...]
+            + gates[1] * jnp.dot(second[...], returned[...], preferred_element_type=jnp.float32)
+        ).astype(jnp.bfloat16)
+
+    slack = (0, 1, 4, 5, 8)
+
+    def work(step, carry):
+        @pl.when(step == 2)
+        def _():
+            complete()
+
+        @pl.when(step < pairs)
+        def _():
+            attend_back(step)
+
+        @pl.when(step == pairs)
+        def _():
+            finish_tokens()
+
+        @pl.when(step == pairs + 1)
+        def _():
+            finish_output()
+
+        @pl.when(step == pairs + 4)
+        def _():
+            pass_on(0)
+            pass_on(2)
+
+        for phase in range(bits):
+            later = phase + slack[min(phase, 4)]
+
+            @pl.when(step == later)
+            def _():
+                absorb(0, 0, phase)
+
+            @pl.when(jnp.logical_and(step > later, step <= later + pairs))
+            def _():
+                absorb(1, step - 1 - later, phase)
+
+            @pl.when(step == pairs + max(1, slack[-1] - 1) + phase)
+            def _():
+                absorb(2, 0, phase)
+
         return carry
 
-    lax.fori_loop(0, HEADS // 2, attend_back, 0)
-
-    for position, c in enumerate(qkv_chunks):
-        start = chunks[c][1]
-        wide[...] = lax.dot_general(
-            normed[...], grad_qkv[:, start : start + D], contract_first, preferred_element_type=jnp.float32
-        )
-        send_chunk(c)
-        if position > 0:
-            absorb(qkv_chunks[position - 1], 0)
-    absorb(out_chunk, 2)
-    tall[...] = lax.dot_general(
-        grad_qkv[...], weights[:, : 3 * D], contract_last, preferred_element_type=jnp.float32
-    )
-    absorb(qkv_chunks[2], 0)
-    absorb(qkv_chunks[0], 1)
-
-    def first_norm(step, carry):
-        here = band(step)
-        grad_in, grad_gain, grad_bias = norm_back(
-            tokens[here, :].astype(jnp.float32), tall[here, :], vectors_ref[0:1, :]
-        )
-        grad_tokens_ref[here, :] = grad_resid[here, :] + grad_in
-        return (carry[0] + grad_gain, carry[1] + grad_bias)
-
-    gain_one, bias_one = lax.fori_loop(0, SLOTS // BAND, first_norm, (zero, zero))
-    wide[:, :LANES] = lax.dot_general(
-        routed[...], grad_logits[...], contract_first, preferred_element_type=jnp.float32
-    )
-    lines = [jnp.sum(v, axis=0, keepdims=True) for v in (gain_one, bias_one, gain_two, bias_two)]
-    lane = lax.broadcasted_iota(jnp.int32, (LANES, LANES), 1)
-    for part in range(D // LANES):
-        span = slice(part * LANES, (part + 1) * LANES)
-        block = wide[span, :LANES]
-        for k in range(4):
-            block = jnp.where(lane == experts + k, column_of(lines[k][:, span], LANES), block)
-        wide[span, :LANES] = block
-    send_chunk(small_chunk)
-
-    absorb(qkv_chunks[1], 1)
-    absorb(out_chunk, 3)
-
-    own_result.wait()
-
-    def result_arrived(step, carry):
-        result_copy(step).wait_recv()
-        result_copy(step).wait_send()
-        return carry
-
-    lax.fori_loop(1, experts, result_arrived, 0)
-    lane = lax.broadcasted_iota(jnp.int32, (SLOTS, LANES), 1)
-    probs = probs_ref[...]
-    gates = [
-        jnp.sum(jnp.where(lane == routes_ref[:, k : k + 1], probs, 0.0), axis=1, keepdims=True)
-        for k in range(2)
-    ]
-    tall[...] = resid[...] + gates[0] * jnp.dot(
-        first[...], returned[...], preferred_element_type=jnp.float32
-    )
-    output_ref[...] = (
-        tall[...]
-        + gates[1] * jnp.dot(second[...], returned[...], preferred_element_type=jnp.float32)
-    ).astype(jnp.bfloat16)
-
-    order = [out_chunk] + qkv_chunks + [small_chunk]
-    done = {out_chunk: 4, qkv_chunks[0]: 2, qkv_chunks[1]: 2, qkv_chunks[2]: 1, small_chunk: 0}
-    for step in range(bits + len(order) - 1):
-        for position, c in enumerate(order):
-            phase = step - position
-            if done[c] <= phase < bits:
-                absorb(c, phase)
-
-    partner = flip(rep, 0)
-
-    def passed_on(kind, step):
-        owner = 2 * lax.rem(along + half - step, half) + core
-        return spread(kind, landing(kind, owner), owner, (mine, partner), half + step - 1)
-
-    for kind in (0, 2, 1):
-        for step in range(1, half):
-            owner = 2 * lax.rem(along + half - step, half) + core
-            spread(kind, landing(kind, owner), owner, (mine, owner), step).wait_recv()
-            passed_on(kind, step).start()
+    lax.fori_loop(0, pairs + bits + max(1, slack[-1]), work, 0)
+    pass_on(1)
     for kind in (0, 2, 1):
         spread(kind, landing(kind, partner), partner, (mine, partner), 0).wait_recv()
         for step in range(1, half):
@@ -1171,21 +1267,26 @@
             move.wait_send()
         for step in range(1, half):
             passed_on(kind, step).wait_send()
-    for moves in half_moves:
-        for move in moves:
-            move.wait_send()
-
-    def dense_sent(c):
+    for move in half_moves:
+        move.wait_send()
+
+    def dense_sent(family, c):
         def one(expert, carry):
-            first_copy(c, expert).wait_send()
+            first_copy(family, c, expert).wait_send()
             return carry
 
         lax.fori_loop(0, experts, one, 0)
         for phase in range(1, bits):
-            later_copy(c, phase).wait_send()
-
-    for c in range(count):
-        dense_sent(c)
+            later_copy(family, c, phase).wait_send()
+
+    def pair_sent(c, carry):
+        dense_sent(1, c)
+        return carry
+
+    if summed:
+        dense_sent(0, 0)
+        lax.fori_loop(0, pairs, pair_sent, 0)
+        dense_sent(2, 0)
 
 
 def run_backward(operands, experts, reps, rows):
@@ -1218,8 +1319,8 @@
     low = jnp.bfloat16
     full = jnp.float32
     piece = half_in.shape[2]
-    tail_rows = half_back.shape[1]
-    chunks = [(0, k * D, D) for k in range(3)] + [(1, 0, D), (2, 0, LANES)]
+    tail_rows = half_back.shape[0]
+    chunks = [(1, D), (HEADS // 2, 3 * LANES), (1, LANES)]
     anywhere = pl.BlockSpec(memory_space=pl.ANY)
     inside = pl.BlockSpec(memory_space=pltpu.VMEM)
     slots = result.shape[0]
@@ -1244,26 +1345,25 @@
         pltpu.VMEM((SLOTS, D), low),
         pltpu.VMEM((SLOTS, 3 * D), low),
         pltpu.VMEM((SLOTS, LANES), low),
-        pltpu.VMEM((tail_rows, D), low),
         pltpu.VMEM((D, piece), low),
-        pltpu.VMEM((half - 1, tail_rows, D), low),
         pltpu.VMEM((half - 1, D, piece), low),
     ]
     summed = rows % 8 == 0
-    for _, _, width in chunks if summed else ():
-        scratch.append(pltpu.VMEM((experts, half, 2, rows, width), low))
-    for _, _, width in chunks if summed else ():
+    scratch.append(pltpu.VMEM((32, D), full))
+    for number, width in chunks if summed else ():
+        scratch.append(pltpu.VMEM((number, experts, half, 2, rows, width), low))
+    for number, width in chunks if summed else ():
         for phase in range(bits):
-            scratch.append(pltpu.VMEM((devices >> (phase + 1), rows, width), low))
-    dense = len(chunks) * (experts + bits - 1)
+            scratch.append(pltpu.VMEM((number, devices >> (phase + 1), rows, width), low))
+    dense = sum(number for number, _ in chunks) * (experts + bits - 1)
     scratch = scratch + [
-        pltpu.SemaphoreType.DMA((13,)),
+        pltpu.SemaphoreType.DMA((12,)),
         pltpu.SemaphoreType.DMA((experts,)),
         pltpu.SemaphoreType.DMA((experts,)),
         pltpu.SemaphoreType.DMA((dense,)),
         pltpu.SemaphoreType.DMA((dense,)),
-        pltpu.SemaphoreType.DMA((2, half - 1)),
-        pltpu.SemaphoreType.DMA((2, half - 1)),
+        pltpu.SemaphoreType.DMA((half - 1,)),
+        pltpu.SemaphoreType.DMA((half - 1,)),
         pltpu.SemaphoreType.DMA((3, reps)),
         pltpu.SemaphoreType.DMA((3, reps)),
         pltpu.SemaphoreType.DMA((3,)),

time: 367 us -> 350 us (0.954)
  Pallas kernels: 284 us -> 267 us
    pallas_call x1, Pallas kernels: 151 us -> 104 us  [run_backward(): gradients = list(call(*operands))]
    pallas_call x1, Pallas kernels: 81.6 us -> 111 us  [run_experts(): pl.pallas_call(functools.partial(expert_kernel, experts, capacity, padded...]
where the time goes in v5:
time: 350 us; the launch traced here: 345 us
  Pallas kernels  267 us (76%)
  other arithmetic  25.7 us (7%)
  local copies, waits for them, and re-layouts  21.8 us (6%)
  matrix products  19 us (5%)
  starting transfers between devices  6.24 us (2%)
  waiting for transfers between devices  3.66 us (1%)
    pallas_call x1, Pallas kernels, run_experts(): pl.pallas_call(functools.partial(expert_kernel, experts, capacity, padded...  111 us
    pallas_call x1, Pallas kernels, run_backward(): gradients = list(call(*operands))  104 us
    pallas_call x1, Pallas kernels, gather_blocks(): pl.pallas_call(functools.partial(gather_kernel, devices, reps), out_shape...  37.4 us
    pallas_call x1, Pallas kernels, attend(): pl.pallas_call(attend_kernel, grid=(pairs,), out_shape=jax.ShapeDtypeStru...  14.4 us
    unnamed x54, local copies, waits for them, and re-layouts  7.66 us
    convert_element_type x1, other arithmetic, on_device(): all_in[None].astype(jnp.float32)  7.52 us
  transfers between devices with their start and end apart: 1, of which 1 were waited for; matrix products, arithmetic and copies ran while one was open for 8% of the time, Pallas kernels for 4%

profile of v5, /device:TPU:0, one launch (start us, length us, event | category | flops | bytes accessed | tf_op | source)
XLA Modules:
  0.0 344.9 jit_solution(10160624296704717665)
XLA Ops:
  0.7 0.8 convert_element_type.146
  1.5 0.7 slice_reduce_fusion.5
  2.2 0.2 convert_reduce_fusion.1
  2.4 1.4 fusion.27
  3.8 0.7 compare_and_fusion.1
  4.5 0.8 add_reduce_fusion.2
  5.3 1.4 fusion.24
  6.8 0.1 copy.100
  6.9 0.1 copy.101
  7.0 0.1 copy.102
  7.1 0.1 copy.103
  7.2 0.1 copy.99
  7.3 0.1 concatenate.6
  7.4 0.7 fusion.55.own_ref
  8.1 37.4 %gather_dense.1 = bf16[32,24,3200]{2,1,0:T(8,128)(2,1)} custom-call(bf16[24,3200]{1,0:T(8,128)(2,1)} %fusion.55.own_ref), custom_call_target="tpu_custom_call" | custom-call | tf_op jit(solution)/shard_map/gather_dense/pallas_call | solution.py:151
  45.4 4.1 %slice.86 = bf16[768,2304]{1,0:T(8,128)(2,1)} slice(bf16[768,3200]{1,0:T(8,128)(2,1)} %bitcast.41), slice={[0:768], [0:2304]} | slice | bytes 7077888 | tf_op jit(solution)/shard_map/slice | solution.py:1439
  49.5 3.8 %convolution_convert_fusion.2 = bf16[1280,768]{1,0:T(8,128)(2,1)} fusion(bf16[576,768]{1,0:T(8,128)(2,1)S(1)} %copy-done.7, pred[576]{0:T(1024)(128)(4,1)S(1)} %compare_and_fusion, s32[576]{0:T(1024)S(1)} %add_reduce_fusion.1, s32[576]{0:T(1024)S(1)} %get-tuple-element.116, pred[576]{0:T(1024)(128)(4,1)S(1)} %get-tuple-element.119), kind=kOutput, calls=%fused_computation.4 | convolution fusion | flops 1140817920 | bytes 2856576 | tf_op jit(solution)/shard_map/dot_general | solution.py:1449
  53.3 6.2 %all-to-all-start = ((bf16[8,160,768]{2,1,0:T(8,128)(2,1)}), bf16[8,160,768]{2,1,0:T(8,128)(2,1)}, u32[]{:S(2)}, u32[]{:S(2)}) async-start(bf16[8,160,768]{2,1,0:T(8,128)(2,1)} %bitcast.8), calls=%async_computation | async-start | bytes 3932160 | tf_op jit(solution)/shard_map/all_to_all | solution.py:1405
  59.6 0.6 reshape.169.live_row
  60.2 0.2 reduce-window.8
  60.4 0.6 reshape.168.segment_row
  61.0 0.9 reshape.185.segment_col
  61.9 1.0 slice.83
  62.9 0.2 convert_reduce_fusion
  63.1 0.4 fusion.10
  63.5 0.1 copy.117
  63.7 0.4 fusion.13.normed_ref
  64.1 6.1 %convolution_convert_fusion.query_ref.keys_ref.values_ref.qkv_ref = bf16[576,2304]{1,0:T(8,128)(2,1)} fusion(bf16[576,768]{1,0:T(8,128)(2,1)S(1)} %fusion.13.normed_ref, bf16[768,2304]{1,0:T(8,128)(2,1)} %slice.86), kind=kOutput, calls=%fused_computation.2 | convolution fusion | flops 2039758848 | bytes 7077888 | tf_op jit(solution)/shard_map/dot_general | solution.py:1459
  70.2 14.4 %attend.1.mixed_ref = bf16[576,768]{1,0:T(8,128)(2,1)} custom-call(s32[576,1]{1,0:T(8,128)} %reshape.185.segment_col, s32[1,576]{1,0:T(1,128)} %reshape.168.segment_row, s32[1,576]{1,0:T(1,128)} %reshape.169.live_row, bf16[576,2304]{1,0:T(8,128)(2,1)} %convolution_convert_fusion.query_ref.keys_ref.values_ref.qkv_ref, ...), custom_call_target="tpu_custom_call" | custom-call | flops 4076863488 | bytes 4194304 | tf_op jit(solution)/shard_map/attend/pallas_call | solution.py:673
  84.6 2.5 fusion.80
  87.1 1.1 copy.111.routes_ref
  88.1 0.9 broadcast_in_dim.3.live_col
  89.0 0.6 convert_element_type.168.b_back_ref
  89.6 0.6 convert_element_type.167.b_in_ref
  90.2 0.3 multiply_reduce_fusion
  90.5 0.4 add_convert_fusion.routed_ref
  90.9 1.5 fusion.81
  92.4 0.1 copy.106
  92.6 0.3 fusion.47
  92.9 0.6 fusion.40
  93.4 1.5 add_reduce_fusion
  95.1 0.7 pad.19.probs_ref
  95.8 2.4 convolution_convert_fusion.1
  98.3 0.6 bitcast_convert_fusion.3.vectors_ref
  99.0 0.6 copy-done.21
  99.6 2.3 fusion.1
  101.9 3.7 %all-to-all-done = bf16[8,160,768]{2,1,0:T(8,128)(2,1)} async-done(((bf16[8,160,768]{2,1,0:T(8,128)(2,1)}), bf16[8,160,768]{2,1,0:T(8,128)(2,1)}, u32[]{:S(2)}, u32[]{:S(2)}) %all-to-all-start) | async-done | bytes 1966112 | tf_op jit(solution)/shard_map/all_to_all | solution.py:1405
  105.6 111.4 %experts.1 = (bf16[8,160,768]{2,1,0:T(8,128)(2,1)}, bf16[1280,768]{1,0:T(8,128)(2,1)}, bf16[784,768]{1,0:T(8,128)(2,1)}, bf16[2,768,768]{2,1,0:T(8,128)(2,1)}) custom-call(bf16[8,160,768]{2,1,0:T(8,128)(2,1)} %copy-done.21, bf16[1280,768]{1,0:T(8,128)(2,1)} %bitcast.13.grad_ref, bf16[768,3072]{1,0:T(8,128)(2,1)} %bitcast.55, bf16[3072,768]{1,0:T(8,128)(2,1)} %bitcast.56, ...), custom_call_target="tpu_custom_call" | custom-call | flops 36238786560 | bytes 41943040 | tf_op jit(solution)/shard_map/experts/pallas_call | solution.py:601
  217.0 0.8 slice_bitcast_fusion
  217.8 0.1 reshape.176
  217.9 0.6 pad.18.terms_ref
  218.5 103.9 %backward.1 = (bf16[576,768]{1,0:T(8,128)(2,1)}, f32[576,768]{1,0:T(8,128)}, f32[24,2304]{1,0:T(8,128)}, f32[24,768]{1,0:T(8,128)}, f32[24,128]{1,0:T(8,128)}, /...) custom-call(bf16[1280,768]{1,0:T(8,128)(2,1)} %bitcast.46, ...), custom_call_target="tpu_custom_call" | custom-call | tf_op jit(solution)/shard_map/backward/pallas_call | solution.py:1395
  322.4 1.3 bitcast_convert_fusion.2
  323.7 0.8 slice.81
  324.5 1.6 slice_reduce_fusion
  326.1 0.6 convert.24
  326.7 1.4 copy.114
  328.1 7.5 %bitcast_convert_fusion.1 = f32[1,768,3072]{2,1,0:T(8,128)} fusion(bf16[768,3072]{1,0:T(8,128)(2,1)} %get-tuple-element.38), kind=kLoop, calls=%fused_computation.1 | loop fusion | flops 2359296 | bytes 14155776 | tf_op jit(solution)/shard_map/convert_element_type | solution.py:1542
  335.6 4.5 %bitcast_convert_fusion = f32[1,3072,768]{2,1,0:T(8,128)} fusion(bf16[3072,768]{1,0:T(8,128)(2,1)S(1)} %copy-done.3), kind=kLoop, calls=%fused_computation | loop fusion | flops 2359296 | bytes 14155776 | tf_op jit(solution)/shard_map/convert_element_type | solution.py:1544
  340.1 0.9 copy.123
  341.0 0.9 copy-done.5
  341.9 1.2 copy.124
  343.1 0.7 copy.125
  343.8 0.6 copy.126
  (61 shorter events, 0.5 us)
Async XLA Ops:
  0.6 6.1 %copy-start.12 = (s32[576,2]{0,1:T(2,128)S(1)}, s32[576,2]{0,1:T(2,128)}, u32[]{:S(2)}) copy-start(s32[576,2]{0,1:T(2,128)} %param.30) | copy-start | bytes 13828
  0.7 6.1 %copy-start.17 = (bf16[24]{0:T(256)(128)(2,1)S(1)}, bf16[24]{0:T(256)(128)(2,1)}, u32[]{:S(2)}) copy-start(bf16[24]{0:T(256)(128)(2,1)} %param.18) | copy-start | bytes 148
  0.7 6.2 %copy-start.18 = (bf16[24]{0:T(256)(128)(2,1)S(1)}, bf16[24]{0:T(256)(128)(2,1)}, u32[]{:S(2)}) copy-start(bf16[24]{0:T(256)(128)(2,1)} %param.19) | copy-start | bytes 148
  0.7 6.3 %copy-start.19 = (bf16[24]{0:T(256)(128)(2,1)S(1)}, bf16[24]{0:T(256)(128)(2,1)}, u32[]{:S(2)}) copy-start(bf16[24]{0:T(256)(128)(2,1)} %param.22) | copy-start | bytes 148
  0.7 6.4 %copy-start.20 = (bf16[24]{0:T(256)(128)(2,1)S(1)}, bf16[24]{0:T(256)(128)(2,1)}, u32[]{:S(2)}) copy-start(bf16[24]{0:T(256)(128)(2,1)} %param.23) | copy-start | bytes 148
  0.7 6.5 %copy-start.16 = (bf16[24,8]{0,1:T(8,128)(2,1)S(1)}, bf16[24,8]{0,1:T(8,128)(2,1)}, u32[]{:S(2)}) copy-start(bf16[24,8]{0,1:T(8,128)(2,1)} %param.24) | copy-start | bytes 1156
  0.7 6.7 %copy-start.13 = (bf16[24,768]{1,0:T(8,128)(2,1)S(1)}, bf16[24,768]{1,0:T(8,128)(2,1)}, u32[]{:S(2)}) copy-start(bf16[24,768]{1,0:T(8,128)(2,1)} %param.21) | copy-start | bytes 110596
  0.7 6.7 %copy-start.9 = (bf16[24,2304]{1,0:T(8,128)(2,1)S(1)}, bf16[24,2304]{1,0:T(8,128)(2,1)}, u32[]{:S(2)}) copy-start(bf16[24,2304]{1,0:T(8,128)(2,1)} %param.20) | copy-start | bytes 331780
  45.4 4.1 %copy-start.7 = (bf16[576,768]{1,0:T(8,128)(2,1)S(1)}, bf16[576,768]{1,0:T(8,128)(2,1)}, u32[]{:S(2)}) copy-start(bf16[576,768]{1,0:T(8,128)(2,1)} %cotangent_ref.1) | copy-start | bytes 2654212
  53.3 6.3 %copy-start.11 = (s32[576]{0:T(1024)S(1)}, s32[576]{0:T(1024)}, u32[]{:S(2)}) copy-start(s32[576]{0:T(1024)} %param.32) | copy-start | bytes 6916
  53.3 6.8 %copy-start.22 = (s32[1,3]{1,0:T(1,128)S(1)}, s32[1,3]{1,0:T(1,128)}, u32[]{:S(2)}) copy-start(s32[1,3]{1,0:T(1,128)} %param.29) | copy-start | bytes 40
  53.3 9.6 %copy-start.1 = (bf16[576,768]{1,0:T(8,128)(2,1)S(1)}, bf16[576,768]{1,0:T(8,128)(2,1)}, u32[]{:S(2)}) copy-start(bf16[576,768]{1,0:T(8,128)(2,1)} %tokens_ref.1) | copy-start | bytes 2654212
  53.3 52.3 %all-to-all-start = ((bf16[8,160,768]{2,1,0:T(8,128)(2,1)}), bf16[8,160,768]{2,1,0:T(8,128)(2,1)}, u32[]{:S(2)}, u32[]{:S(2)}) async-start(bf16[8,160,768]{2,1,0:T(8,128)(2,1)} %bitcast.8), calls=%async_computation | async-start | bytes 3932160 | tf_op jit(solution)/shard_map/all_to_all | solution.py:1405
  64.1 6.1 %copy-start.4 = (bf16[576,768]{1,0:T(8,128)(2,1)}, bf16[576,768]{1,0:T(8,128)(2,1)S(1)}, u32[]{:S(2)}) copy-start(bf16[576,768]{1,0:T(8,128)(2,1)S(1)} %fusion.13.normed_ref) | copy-start | bytes 2654212
  84.6 4.4 %copy-start.15 = (bf16[1,768]{1,0:T(2,128)(2,1)S(1)}, bf16[1,768]{1,0:T(2,128)(2,1)}, u32[]{:S(2)}) copy-start(bf16[1,768]{1,0:T(2,128)(2,1)} %param.28) | copy-start | bytes 4612
  84.6 5.0 %copy-start.14 = (bf16[1,3072]{1,0:T(2,128)(2,1)S(1)}, bf16[1,3072]{1,0:T(2,128)(2,1)}, u32[]{:S(2)}) copy-start(bf16[1,3072]{1,0:T(2,128)(2,1)} %param.26) | copy-start | bytes 18436
  87.1 3.8 %copy-start = (f32[576,768]{1,0:T(8,128)}, f32[576,768]{1,0:T(8,128)S(1)}, u32[]{:S(2)}) copy-start(f32[576,768]{1,0:T(8,128)S(1)} %get-tuple-element.125.resid_ref) | copy-start | bytes 5308420
  90.9 7.3 %copy-start.2 = (bf16[576,768]{1,0:T(8,128)(2,1)}, bf16[576,768]{1,0:T(8,128)(2,1)S(1)}, u32[]{:S(2)}) copy-start(bf16[576,768]{1,0:T(8,128)(2,1)S(1)} %add_convert_fusion.routed_ref) | copy-start | bytes 2654212
  98.3 1.3 copy-start.21
  328.1 7.5 %copy-start.3 = (bf16[3072,768]{1,0:T(8,128)(2,1)S(1)}, bf16[3072,768]{1,0:T(8,128)(2,1)}, u32[]{:S(2)}) copy-start(bf16[3072,768]{1,0:T(8,128)(2,1)} %get-tuple-element.40) | copy-start | bytes 14155780
  335.6 4.5 %copy-start.6 = (bf16[576,768]{1,0:T(8,128)(2,1)S(1)}, bf16[576,768]{1,0:T(8,128)(2,1)}, u32[]{:S(2)}) copy-start(bf16[576,768]{1,0:T(8,128)(2,1)} %get-tuple-element.143) | copy-start | bytes 2654212
  340.1 1.8 copy-start.5
  341.9 1.2 copy-start.8
  341.9 1.9 copy-start.10

commit v6 on v5

--- a/solution.py
+++ b/solution.py
@@ -86,81 +86,106 @@
     return (number & -number).bit_length() - 1
 
 
-def gather_kernel(devices, reps, own_ref, all_ref, send_sem, recv_sem, local_sem):
+def gather_kernel(devices, reps, pieces, qkv_ref, rest_ref, all_qkv_ref, all_rest_ref, send_sem, recv_sem, local_sem):
     bits = bit_count(devices)
     me = lax.axis_index("exp") * reps + lax.axis_index("rep")
     greet(bits, me, reps)
-    local = pltpu.make_async_copy(own_ref, all_ref.at[me], local_sem)
-    local.start()
-
-    def owner_of(distance):
+    own = (qkv_ref, rest_ref)
+    everywhere = (all_qkv_ref, all_rest_ref)
+    locals_ = [
+        pltpu.make_async_copy(own[k], everywhere[k].at[me], local_sem.at[k]) for k in range(2)
+    ]
+    for copy in locals_:
+        copy.start()
+
+    def owner_of(distance, order):
         found = me
         for bit in range(bits):
             if distance >> bit & 1:
-                found = flip(found, bit)
+                found = flip(found, order[bit])
         return found
 
-    def transfer(source_ref, distance, bit):
-        owner = owner_of(distance)
+    def block(number, owner):
+        array, start, width, _ = pieces[number]
+        return everywhere[array].at[owner, :, pl.ds(start, width)]
+
+    def transfer(number, distance, bit):
+        array, start, width, order = pieces[number]
+        owner = owner_of(distance, order)
         index = distance + (1 << bit)
+        source = own[array].at[:, pl.ds(start, width)] if distance == 0 else block(number, owner)
         return pltpu.make_async_remote_copy(
-            src_ref=source_ref,
-            dst_ref=all_ref.at[owner],
-            send_sem=send_sem.at[index],
-            recv_sem=recv_sem.at[index],
-            device_id=coordinates(flip(me, bit), reps),
+            src_ref=source,
+            dst_ref=block(number, owner),
+            send_sem=send_sem.at[number, index],
+            recv_sem=recv_sem.at[number, index],
+            device_id=coordinates(flip(me, order[bit]), reps),
             device_id_type=MESH_ID,
         )
 
-    def arrival(distance):
-        owner = owner_of(distance)
+    def arrival(number, distance):
+        order = pieces[number][3]
+        owner = owner_of(distance, order)
         return pltpu.make_async_remote_copy(
-            src_ref=all_ref.at[owner],
-            dst_ref=all_ref.at[owner],
-            send_sem=send_sem.at[distance],
-            recv_sem=recv_sem.at[distance],
-            device_id=coordinates(flip(me, lowest_bit(distance)), reps),
+            src_ref=block(number, owner),
+            dst_ref=block(number, owner),
+            send_sem=send_sem.at[number, distance],
+            recv_sem=recv_sem.at[number, distance],
+            device_id=coordinates(flip(me, order[lowest_bit(distance)]), reps),
             device_id_type=MESH_ID,
         )
 
     sent = []
     for bit in range(bits):
-        copy = transfer(own_ref, 0, bit)
-        copy.start()
-        sent.append(copy)
-    order = sorted(range(1, devices), key=lambda d: (bin(d).count("1"), -d))
-    last = []
-    for distance in order:
-        low = lowest_bit(distance)
-        if low == 0:
-            last.append(distance)
-            continue
-        arrival(distance).wait_recv()
-        for bit in range(low):
-            copy = transfer(all_ref.at[owner_of(distance)], distance, bit)
+        for number in range(len(pieces)):
+            copy = transfer(number, 0, bit)
             copy.start()
             sent.append(copy)
-    for distance in last:
-        arrival(distance).wait_recv()
+    sequence = sorted(range(1, devices), key=lambda d: (bin(d).count("1"), -d))
+    last = []
+    for distance in sequence:
+        low = lowest_bit(distance)
+        for number in range(len(pieces)):
+            if low == 0:
+                last.append((number, distance))
+                continue
+            arrival(number, distance).wait_recv()
+            for bit in range(low):
+                copy = transfer(number, distance, bit)
+                copy.start()
+                sent.append(copy)
+    for number, distance in last:
+        arrival(number, distance).wait_recv()
     for copy in sent:
         copy.wait_send()
-    local.wait()
-
-
-def gather_blocks(block, devices, reps):
+    for copy in locals_:
+        copy.wait()
+
+
+def gather_blocks(qkv, rest, devices, reps):
+    bits = bit_count(devices)
+    plain = list(range(bits))
+    low = bit_count(reps)
+    turned = list(plain)
+    turned[low - 1], turned[low] = (plain[low], plain[low - 1])
+    pieces = [(0, 0, 2 * D, plain), (0, 2 * D, D, turned), (1, 0, rest.shape[1], turned)]
+    anywhere = pl.BlockSpec(memory_space=pl.ANY)
     return pl.pallas_call(
-        functools.partial(gather_kernel, devices, reps),
-        out_shape=jax.ShapeDtypeStruct((devices,) + block.shape, block.dtype),
-        in_specs=[pl.BlockSpec(memory_space=pl.ANY)],
-        out_specs=pl.BlockSpec(memory_space=pl.ANY),
+        functools.partial(gather_kernel, devices, reps, pieces),
+        out_shape=[
+            jax.ShapeDtypeStruct((devices,) + qkv.shape, qkv.dtype),
+            jax.ShapeDtypeStruct((devices,) + rest.shape, rest.dtype),
+        ],
+        in_specs=[anywhere] * 2,
+        out_specs=[anywhere] * 2,
         scratch_shapes=[
-            pltpu.SemaphoreType.DMA((devices,)),
-            pltpu.SemaphoreType.DMA((devices,)),
-            pltpu.SemaphoreType.DMA,
+            pltpu.SemaphoreType.DMA((len(pieces), devices)),
+            pltpu.SemaphoreType.DMA((len(pieces), devices)),
+            pltpu.SemaphoreType.DMA((2,)),
         ],
         compiler_params=pltpu.CompilerParams(collective_id=0, has_side_effects=True),
         name="gather_dense",
-    )(block)
+    )(qkv, rest)
 
 
 def row_of(column, width):
@@ -717,7 +742,8 @@
     routed_ref,
     qkv_ref,
     mixed_ref,
-    weights_ref,
+    qkv_weight_ref,
+    rest_weight_ref,
     vectors_ref,
     segment_col,
     segment_row,
@@ -753,7 +779,8 @@
         routed,
         qkv,
         mixed,
-        weights,
+        qkv_weight,
+        rest_weight,
         returned,
         bias,
         wide,
@@ -765,8 +792,8 @@
         grad_logits,
         own_in,
         other_in,
-    ) = refs[:22]
-    refs = refs[22:]
+    ) = refs[:23]
+    refs = refs[23:]
     lines, refs = (refs[0], refs[1:])
     count = len(chunks) if summed else 0
     parts, refs = (refs[:count], refs[count:])
@@ -806,13 +833,14 @@
         (first_ref, first),
         (second_ref, second),
         (routed_ref, routed),
-        (weights_ref, weights),
+        (rest_weight_ref, rest_weight),
         (resid_ref, resid),
         (cotangent_ref, cotangent),
         (mixed_ref, mixed),
         (qkv_ref, qkv),
         (normed_ref, normed),
         (tokens_ref, tokens),
+        (qkv_weight_ref, qkv_weight),
         (half_in_ref.at[along], own_in),
     ]
     loads = [
@@ -921,7 +949,7 @@
         probs * (grad_probs - jnp.sum(probs * grad_probs, axis=1, keepdims=True))
     ).astype(jnp.bfloat16)
     tall[...] += lax.dot_general(
-        grad_logits[...], weights[:, 4 * D :], contract_last, preferred_element_type=jnp.float32
+        grad_logits[...], rest_weight[:, D:], contract_last, preferred_element_type=jnp.float32
     )
     for copy in loads[5:]:
         copy.wait()
@@ -1080,7 +1108,7 @@
     )
     send_chunk(0, 0)
     grad_mixed[...] = lax.dot_general(
-        grad_attn[...], weights[:, 3 * D : 4 * D], contract_last, preferred_element_type=jnp.float32
+        grad_attn[...], rest_weight[:, :D], contract_last, preferred_element_type=jnp.float32
     ).astype(jnp.bfloat16)
 
     def complete():
@@ -1161,7 +1189,7 @@
 
     def finish_tokens():
         tall[...] = lax.dot_general(
-            grad_qkv[...], weights[:, : 3 * D], contract_last, preferred_element_type=jnp.float32
+            grad_qkv[...], qkv_weight[...], contract_last, preferred_element_type=jnp.float32
         )
 
         def first_norm(step, carry):
@@ -1308,7 +1336,8 @@
         routed,
         qkv,
         mixed,
-        weights,
+        qkv_weight,
+        rest_weight,
         vectors,
         segment_col,
         segment_row,
@@ -1335,7 +1364,8 @@
         pltpu.VMEM((SLOTS, D), low),
         pltpu.VMEM((SLOTS, 3 * D), low),
         pltpu.VMEM((SLOTS, D), low),
-        pltpu.VMEM(weights.shape, low),
+        pltpu.VMEM(qkv_weight.shape, low),
+        pltpu.VMEM(rest_weight.shape, low),
         pltpu.VMEM((slots, D), low),
         pltpu.VMEM((SLOTS, SLOTS), full),
         pltpu.VMEM((D, D), full),
@@ -1357,7 +1387,7 @@
             scratch.append(pltpu.VMEM((number, devices >> (phase + 1), rows, width), low))
     dense = sum(number for number, _ in chunks) * (experts + bits - 1)
     scratch = scratch + [
-        pltpu.SemaphoreType.DMA((12,)),
+        pltpu.SemaphoreType.DMA((13,)),
         pltpu.SemaphoreType.DMA((experts,)),
         pltpu.SemaphoreType.DMA((experts,)),
         pltpu.SemaphoreType.DMA((dense,)),
@@ -1382,7 +1412,7 @@
         ],
         in_specs=[anywhere] * 4
         + [inside] * 3
-        + [anywhere] * 8
+        + [anywhere] * 9
         + [inside] * 4
         + [anywhere] * 2,
         out_specs=[inside] * 2 + [inside if summed else anywhere] * 3 + [anywhere] * 3,
@@ -1434,12 +1464,13 @@
         [w_router, jnp.stack([ln1_gain, ln1_bias, ln2_gain, ln2_bias], axis=1)], axis=1
     )
     small = jnp.pad(small, ((0, 0), (0, LANES - small.shape[1])))
-    packed = jnp.concatenate([w_qkv, w_out, small], axis=1)
-    gathered = gather_blocks(packed, devices, reps).reshape(D, packed.shape[1])
-    qkv_weight = gathered[:, : 3 * D]
-    out_weight = gathered[:, 3 * D : 4 * D]
-    router_weight = gathered[:, 4 * D : 4 * D + experts]
-    vectors = gathered[:, 4 * D + experts : 4 * D + experts + 4].T
+    rest = jnp.concatenate([w_out, small], axis=1)
+    qkv_weight, rest_weight = gather_blocks(w_qkv, rest, devices, reps)
+    qkv_weight = qkv_weight.reshape(D, 3 * D)
+    rest_weight = rest_weight.reshape(D, rest.shape[1])
+    out_weight = rest_weight[:, :D]
+    router_weight = rest_weight[:, D : D + experts]
+    vectors = rest_weight[:, D + experts : D + experts + 4].T
     gain_one, bias_one, gain_two, bias_two = (vectors[0], vectors[1], vectors[2], vectors[3])
 
     first_hot, second_hot, pick_first, pick_second = dispatch_tables(
@@ -1514,7 +1545,8 @@
             routed,
             qkv[0],
             mixed_low,
-            gathered,
+            qkv_weight,
+            rest_weight,
             vectors.astype(jnp.float32),
             segments.reshape(SLOTS, 1),
             segments.reshape(1, SLOTS),

time: 350 us -> 339 us (0.969)
  Pallas kernels: 267 us -> 259 us
    pallas_call x1, Pallas kernels: 37.4 us -> 30.4 us  [gather_blocks(): pl.pallas_call(functools.partial(gather_kernel, devices, reps, pieces), o...]
    slice x2 -> x1, local copies, waits for them, and re-layouts: 5.14 us -> 1.05 us  [on_device(): vectors = rest_weight[:, D + experts:D + experts + 4].T]
    unnamed x54 -> x52, local copies, waits for them, and re-layouts: 7.66 us -> 8.52 us
where the time goes in v6:
time: 339 us; the launch traced here: 334 us
  Pallas kernels  259 us (76%)
  other arithmetic  25.7 us (8%)
  matrix products  18.6 us (5%)
  local copies, waits for them, and re-layouts  18.5 us (5%)
  starting transfers between devices  6.7 us (2%)
  waiting for transfers between devices  4.03 us (1%)
    pallas_call x1, Pallas kernels, run_experts(): pl.pallas_call(functools.partial(expert_kernel, experts, capacity, padded...  110 us
    pallas_call x1, Pallas kernels, run_backward(): gradients = list(call(*operands))  104 us
    pallas_call x1, Pallas kernels, gather_blocks(): pl.pallas_call(functools.partial(gather_kernel, devices, reps, pieces), o...  30.4 us
    pallas_call x1, Pallas kernels, attend(): pl.pallas_call(attend_kernel, grid=(pairs,), out_shape=jax.ShapeDtypeStru...  14.3 us
    unnamed x52, local copies, waits for them, and re-layouts  8.52 us
    convert_element_type x1, other arithmetic, on_device(): all_in[None].astype(jnp.float32)  7.52 us
  transfers between devices with their start and end apart: 1, of which 1 were waited for; matrix products, arithmetic and copies ran while one was open for 8% of the time, Pallas kernels for 4%

profile of v6, /device:TPU:0, one launch (start us, length us, event | category | flops | bytes accessed | tf_op | source)
XLA Modules:
  0.0 334.0 jit_solution(10717481861078619821)
XLA Ops:
  0.7 0.8 convert_element_type.146
  1.5 0.7 slice_reduce_fusion.5
  2.2 0.2 convert_reduce_fusion.1
  2.4 1.4 fusion.27
  3.8 0.7 compare_and_fusion.1
  4.5 0.8 add_reduce_fusion.2
  5.3 1.4 fusion.24
  6.8 0.1 copy.100
  6.9 0.1 copy.101
  7.0 0.1 copy.102
  7.1 0.1 copy.103
  7.2 0.1 copy.99
  7.3 0.1 concatenate.6
  7.4 0.6 fusion.68.rest_ref
  8.0 30.4 %gather_dense.1 = (bf16[32,24,2304]{2,1,0:T(8,128)(2,1)}, bf16[32,24,896]{2,1,0:T(8,128)(2,1)}) custom-call(bf16[24,2304]{1,0:T(8,128)(2,1)} %qkv_ref.1, bf16[24,896]{1,0:T(8,128)(2,1)} %fusion.68.rest_ref), custom_call_target="tpu_custom_call" | custom-call | tf_op jit(solution)/shard_map/gather_dense/pallas_call | solution.py:173
  38.4 3.7 %convolution_convert_fusion.2 = bf16[1280,768]{1,0:T(8,128)(2,1)} fusion(bf16[576,768]{1,0:T(8,128)(2,1)S(1)} %copy-done.7, pred[576]{0:T(1024)(128)(4,1)S(1)} %compare_and_fusion, s32[576]{0:T(1024)S(1)} %add_reduce_fusion.1, s32[576]{0:T(1024)S(1)} %get-tuple-element.120, pred[576]{0:T(1024)(128)(4,1)S(1)} %get-tuple-element.123), kind=kOutput, calls=%fused_computation.4 | convolution fusion | flops 1140817920 | bytes 2856576 | tf_op jit(solution)/shard_map/dot_general | solution.py:1480
  42.1 6.7 %all-to-all-start = ((bf16[8,160,768]{2,1,0:T(8,128)(2,1)}), bf16[8,160,768]{2,1,0:T(8,128)(2,1)}, u32[]{:S(2)}, u32[]{:S(2)}) async-start(bf16[8,160,768]{2,1,0:T(8,128)(2,1)} %bitcast.8), calls=%async_computation | async-start | bytes 3932160 | tf_op jit(solution)/shard_map/all_to_all | solution.py:1435
  48.8 0.6 reshape.172.live_row
  49.4 0.2 reduce-window.8
  49.7 0.6 reshape.171.segment_row
  50.3 0.9 reshape.189.segment_col
  51.1 0.2 convert_reduce_fusion
  51.4 0.4 fusion.10
  51.8 1.0 slice.79
  52.8 0.1 copy.117
  53.0 0.4 fusion.13.normed_ref
  53.4 0.9 copy-done.4
  54.3 5.7 %convolution_convert_fusion.query_ref.keys_ref.values_ref.qkv_ref = bf16[576,2304]{1,0:T(8,128)(2,1)} fusion(bf16[576,768]{1,0:T(8,128)(2,1)S(1)} %fusion.13.normed_ref, bf16[768,2304]{1,0:T(8,128)(2,1)} %bitcast.42), kind=kOutput, calls=%fused_computation.2 | convolution fusion | flops 2039758848 | bytes 7077888 | tf_op jit(solution)/shard_map/dot_general | solution.py:1490
  60.0 14.3 %attend.1.mixed_ref = bf16[576,768]{1,0:T(8,128)(2,1)} custom-call(s32[576,1]{1,0:T(8,128)} %reshape.189.segment_col, s32[1,576]{1,0:T(1,128)} %reshape.171.segment_row, s32[1,576]{1,0:T(1,128)} %reshape.172.live_row, bf16[576,2304]{1,0:T(8,128)(2,1)} %convolution_convert_fusion.query_ref.keys_ref.values_ref.qkv_ref, ...), custom_call_target="tpu_custom_call" | custom-call | flops 4076863488 | bytes 4194304 | tf_op jit(solution)/shard_map/attend/pallas_call | solution.py:698
  74.4 2.5 fusion.80
  76.9 1.1 copy.111.routes_ref
  78.0 0.9 broadcast_in_dim.3.live_col
  78.8 0.6 convert_element_type.168.b_back_ref
  79.4 0.6 convert_element_type.167.b_in_ref
  80.0 0.3 multiply_reduce_fusion
  80.4 0.4 add_convert_fusion.routed_ref
  80.8 1.5 fusion.81
  82.3 0.1 copy.106
  82.4 0.3 fusion.46
  82.7 0.6 fusion.39
  83.3 1.5 add_reduce_fusion
  84.9 0.7 pad.19.probs_ref
  85.7 2.4 convolution_convert_fusion.1
  88.2 0.7 bitcast_convert_fusion.3.vectors_ref
  88.8 0.6 copy-done.20
  89.4 2.3 fusion.1
  91.8 4.0 %all-to-all-done = bf16[8,160,768]{2,1,0:T(8,128)(2,1)} async-done(((bf16[8,160,768]{2,1,0:T(8,128)(2,1)}), bf16[8,160,768]{2,1,0:T(8,128)(2,1)}, u32[]{:S(2)}, u32[]{:S(2)}) %all-to-all-start) | async-done | bytes 1966112 | tf_op jit(solution)/shard_map/all_to_all | solution.py:1435
  95.8 110.1 %experts.1 = (bf16[8,160,768]{2,1,0:T(8,128)(2,1)}, bf16[1280,768]{1,0:T(8,128)(2,1)}, bf16[784,768]{1,0:T(8,128)(2,1)}, bf16[2,768,768]{2,1,0:T(8,128)(2,1)}) custom-call(bf16[8,160,768]{2,1,0:T(8,128)(2,1)} %copy-done.20, bf16[1280,768]{1,0:T(8,128)(2,1)} %bitcast.14.grad_ref, bf16[768,3072]{1,0:T(8,128)(2,1)} %bitcast.57, bf16[3072,768]{1,0:T(8,128)(2,1)} %bitcast.58, ...), custom_call_target="tpu_custom_call" | custom-call | flops 36238786560 | bytes 41943040 | tf_op jit(solution)/shard_map/experts/pallas_call | solution.py:626
  205.9 0.8 slice_bitcast_fusion
  206.6 0.1 reshape.180
  206.7 0.6 pad.18.terms_ref
  207.4 104.2 %backward.1 = (bf16[576,768]{1,0:T(8,128)(2,1)}, f32[576,768]{1,0:T(8,128)}, f32[24,2304]{1,0:T(8,128)}, f32[24,768]{1,0:T(8,128)}, f32[24,128]{1,0:T(8,128)}, /...) custom-call(bf16[1280,768]{1,0:T(8,128)(2,1)} %bitcast.48, ...), custom_call_target="tpu_custom_call" | custom-call | tf_op jit(solution)/shard_map/backward/pallas_call | solution.py:1425
  311.6 1.3 bitcast_convert_fusion.2
  312.9 0.8 slice.77
  313.7 1.6 slice_reduce_fusion
  315.3 0.6 convert.24
  315.9 1.4 copy.114
  317.3 7.5 %bitcast_convert_fusion.1 = f32[1,768,3072]{2,1,0:T(8,128)} fusion(bf16[768,3072]{1,0:T(8,128)(2,1)} %get-tuple-element.42), kind=kLoop, calls=%fused_computation.1 | loop fusion | flops 2359296 | bytes 14155776 | tf_op jit(solution)/shard_map/convert_element_type | solution.py:1574
  324.8 4.5 %bitcast_convert_fusion = f32[1,3072,768]{2,1,0:T(8,128)} fusion(bf16[3072,768]{1,0:T(8,128)(2,1)S(1)} %copy-done.3), kind=kLoop, calls=%fused_computation | loop fusion | flops 2359296 | bytes 14155776 | tf_op jit(solution)/shard_map/convert_element_type | solution.py:1576
  329.3 0.9 copy.123
  330.2 0.9 copy-done.5
  331.1 1.2 copy.124
  332.3 0.7 copy.125
  333.0 0.6 copy.126
  (58 shorter events, 0.5 us)
Async XLA Ops:
  0.6 6.1 %copy-start.11 = (s32[576,2]{0,1:T(2,128)S(1)}, s32[576,2]{0,1:T(2,128)}, u32[]{:S(2)}) copy-start(s32[576,2]{0,1:T(2,128)} %param.30) | copy-start | bytes 13828
  0.7 6.1 %copy-start.16 = (bf16[24]{0:T(256)(128)(2,1)S(1)}, bf16[24]{0:T(256)(128)(2,1)}, u32[]{:S(2)}) copy-start(bf16[24]{0:T(256)(128)(2,1)} %param.18) | copy-start | bytes 148
  0.7 6.2 %copy-start.17 = (bf16[24]{0:T(256)(128)(2,1)S(1)}, bf16[24]{0:T(256)(128)(2,1)}, u32[]{:S(2)}) copy-start(bf16[24]{0:T(256)(128)(2,1)} %param.19) | copy-start | bytes 148
  0.7 6.3 %copy-start.18 = (bf16[24]{0:T(256)(128)(2,1)S(1)}, bf16[24]{0:T(256)(128)(2,1)}, u32[]{:S(2)}) copy-start(bf16[24]{0:T(256)(128)(2,1)} %param.22) | copy-start | bytes 148
  0.7 6.4 %copy-start.19 = (bf16[24]{0:T(256)(128)(2,1)S(1)}, bf16[24]{0:T(256)(128)(2,1)}, u32[]{:S(2)}) copy-start(bf16[24]{0:T(256)(128)(2,1)} %param.23) | copy-start | bytes 148
  0.7 6.5 %copy-start.15 = (bf16[24,8]{0,1:T(8,128)(2,1)S(1)}, bf16[24,8]{0,1:T(8,128)(2,1)}, u32[]{:S(2)}) copy-start(bf16[24,8]{0,1:T(8,128)(2,1)} %param.24) | copy-start | bytes 1156
  0.7 6.7 %copy-start.12 = (bf16[24,768]{1,0:T(8,128)(2,1)S(1)}, bf16[24,768]{1,0:T(8,128)(2,1)}, u32[]{:S(2)}) copy-start(bf16[24,768]{1,0:T(8,128)(2,1)} %param.21) | copy-start | bytes 110596
  0.7 37.7 %copy-start.7 = (bf16[576,768]{1,0:T(8,128)(2,1)S(1)}, bf16[576,768]{1,0:T(8,128)(2,1)}, u32[]{:S(2)}) copy-start(bf16[576,768]{1,0:T(8,128)(2,1)} %cotangent_ref.1) | copy-start | bytes 2654212
  42.1 6.7 %copy-start.10 = (s32[576]{0:T(1024)S(1)}, s32[576]{0:T(1024)}, u32[]{:S(2)}) copy-start(s32[576]{0:T(1024)} %param.32) | copy-start | bytes 6916
  42.1 7.3 %copy-start.21 = (s32[1,3]{1,0:T(1,128)S(1)}, s32[1,3]{1,0:T(1,128)}, u32[]{:S(2)}) copy-start(s32[1,3]{1,0:T(1,128)} %param.29) | copy-start | bytes 40
  42.1 9.0 %copy-start.1 = (bf16[576,768]{1,0:T(8,128)(2,1)S(1)}, bf16[576,768]{1,0:T(8,128)(2,1)}, u32[]{:S(2)}) copy-start(bf16[576,768]{1,0:T(8,128)(2,1)} %tokens_ref.1) | copy-start | bytes 2654212
  42.1 53.7 %all-to-all-start = ((bf16[8,160,768]{2,1,0:T(8,128)(2,1)}), bf16[8,160,768]{2,1,0:T(8,128)(2,1)}, u32[]{:S(2)}, u32[]{:S(2)}) async-start(bf16[8,160,768]{2,1,0:T(8,128)(2,1)} %bitcast.8), calls=%async_computation | async-start | bytes 3932160 | tf_op jit(solution)/shard_map/all_to_all | solution.py:1435
  53.4 0.9 copy-start.4
  74.4 4.4 %copy-start.14 = (bf16[1,768]{1,0:T(2,128)(2,1)S(1)}, bf16[1,768]{1,0:T(2,128)(2,1)}, u32[]{:S(2)}) copy-start(bf16[1,768]{1,0:T(2,128)(2,1)} %param.28) | copy-start | bytes 4612
  74.4 5.0 %copy-start.13 = (bf16[1,3072]{1,0:T(2,128)(2,1)S(1)}, bf16[1,3072]{1,0:T(2,128)(2,1)}, u32[]{:S(2)}) copy-start(bf16[1,3072]{1,0:T(2,128)(2,1)} %param.26) | copy-start | bytes 18436
  76.9 3.8 %copy-start = (f32[576,768]{1,0:T(8,128)}, f32[576,768]{1,0:T(8,128)S(1)}, u32[]{:S(2)}) copy-start(f32[576,768]{1,0:T(8,128)S(1)} %get-tuple-element.129.resid_ref) | copy-start | bytes 5308420
  80.8 7.3 %copy-start.2 = (bf16[576,768]{1,0:T(8,128)(2,1)}, bf16[576,768]{1,0:T(8,128)(2,1)S(1)}, u32[]{:S(2)}) copy-start(bf16[576,768]{1,0:T(8,128)(2,1)S(1)} %add_convert_fusion.routed_ref) | copy-start | bytes 2654212
  88.1 1.3 copy-start.20
  317.3 7.5 %copy-start.3 = (bf16[3072,768]{1,0:T(8,128)(2,1)S(1)}, bf16[3072,768]{1,0:T(8,128)(2,1)}, u32[]{:S(2)}) copy-start(bf16[3072,768]{1,0:T(8,128)(2,1)} %get-tuple-element.44) | copy-start | bytes 14155780
  324.8 4.5 %copy-start.6 = (bf16[576,768]{1,0:T(8,128)(2,1)S(1)}, bf16[576,768]{1,0:T(8,128)(2,1)}, u32[]{:S(2)}) copy-start(bf16[576,768]{1,0:T(8,128)(2,1)} %get-tuple-element.147) | copy-start | bytes 2654212
  329.3 1.8 copy-start.5
  331.1 1.2 copy-start.8
  331.1 1.9 copy-start.9

commit v7 on v6

--- a/solution.py
+++ b/solution.py
@@ -571,12 +571,17 @@
         kept_in_copy(index).start()
         return carry
 
-    lax.fori_loop(1, half + 1, away_back_step, 0)
+
+    def back_step(step, carry):
+        away_back_step(step, 0)
+        kept_back_step(step, 0)
+        return carry
+
+    lax.fori_loop(1, half + 1, back_step, 0)
     if groups > 1:
         send_back_group(turn(groups - 1))
     else:
         going_back(neighbour).start()
-    lax.fori_loop(1, half + 1, kept_back_step, 0)
     lax.fori_loop(0, half, away_in_step, 0)
     lax.fori_loop(0, half, kept_in_step, 0)
     for step in range(1, half):

time: 339 us -> 339 us (level)
  no operation moved by 1% of the time
where the time goes in v7:
time: 339 us; the launch traced here: 334 us
  Pallas kernels  259 us (76%)
  other arithmetic  25.7 us (8%)
  matrix products  18.6 us (5%)
  local copies, waits for them, and re-layouts  18.5 us (5%)
  starting transfers between devices  6.7 us (2%)
  waiting for transfers between devices  4.03 us (1%)
    pallas_call x1, Pallas kernels, run_experts(): pl.pallas_call(functools.partial(expert_kernel, experts, capacity, padded...  108 us
    pallas_call x1, Pallas kernels, run_backward(): gradients = list(call(*operands))  106 us
    pallas_call x1, Pallas kernels, gather_blocks(): pl.pallas_call(functools.partial(gather_kernel, devices, reps, pieces), o...  30.4 us
    pallas_call x1, Pallas kernels, attend(): pl.pallas_call(attend_kernel, grid=(pairs,), out_shape=jax.ShapeDtypeStru...  14.3 us
    unnamed x52, local copies, waits for them, and re-layouts  8.52 us
    convert_element_type x1, other arithmetic, on_device(): all_in[None].astype(jnp.float32)  7.52 us
  transfers between devices with their start and end apart: 1, of which 1 were waited for; matrix products, arithmetic and copies ran while one was open for 8% of the time, Pallas kernels for 4%

profile of v7, /device:TPU:0, one launch (start us, length us, event | category | flops | bytes accessed | tf_op | source)
XLA Modules:
  0.0 333.7 jit_solution(6299591129708379526)
XLA Ops:
  0.7 0.8 convert_element_type.146
  1.5 0.7 slice_reduce_fusion.5
  2.2 0.2 convert_reduce_fusion.1
  2.4 1.4 fusion.27
  3.8 0.7 compare_and_fusion.1
  4.5 0.8 add_reduce_fusion.2
  5.3 1.4 fusion.24
  6.8 0.1 copy.100
  6.9 0.1 copy.101
  7.0 0.1 copy.102
  7.1 0.1 copy.103
  7.2 0.1 copy.99
  7.3 0.1 concatenate.6
  7.4 0.6 fusion.68.rest_ref
  8.0 30.4 %gather_dense.1 = (bf16[32,24,2304]{2,1,0:T(8,128)(2,1)}, bf16[32,24,896]{2,1,0:T(8,128)(2,1)}) custom-call(bf16[24,2304]{1,0:T(8,128)(2,1)} %qkv_ref.1, bf16[24,896]{1,0:T(8,128)(2,1)} %fusion.68.rest_ref), custom_call_target="tpu_custom_call" | custom-call | tf_op jit(solution)/shard_map/gather_dense/pallas_call | solution.py:173
  38.4 3.7 %convolution_convert_fusion.2 = bf16[1280,768]{1,0:T(8,128)(2,1)} fusion(bf16[576,768]{1,0:T(8,128)(2,1)S(1)} %copy-done.7, pred[576]{0:T(1024)(128)(4,1)S(1)} %compare_and_fusion, s32[576]{0:T(1024)S(1)} %add_reduce_fusion.1, s32[576]{0:T(1024)S(1)} %get-tuple-element.120, pred[576]{0:T(1024)(128)(4,1)S(1)} %get-tuple-element.123), kind=kOutput, calls=%fused_computation.4 | convolution fusion | flops 1140817920 | bytes 2856576 | tf_op jit(solution)/shard_map/dot_general | solution.py:1485
  42.1 6.7 %all-to-all-start = ((bf16[8,160,768]{2,1,0:T(8,128)(2,1)}), bf16[8,160,768]{2,1,0:T(8,128)(2,1)}, u32[]{:S(2)}, u32[]{:S(2)}) async-start(bf16[8,160,768]{2,1,0:T(8,128)(2,1)} %bitcast.8), calls=%async_computation | async-start | bytes 3932160 | tf_op jit(solution)/shard_map/all_to_all | solution.py:1440
  48.8 0.6 reshape.172.live_row
  49.4 0.2 reduce-window.8
  49.7 0.6 reshape.171.segment_row
  50.3 0.9 reshape.189.segment_col
  51.1 0.2 convert_reduce_fusion
  51.4 0.4 fusion.10
  51.8 1.0 slice.79
  52.8 0.1 copy.117
  53.0 0.4 fusion.13.normed_ref
  53.4 0.9 copy-done.4
  54.3 5.7 %convolution_convert_fusion.query_ref.keys_ref.values_ref.qkv_ref = bf16[576,2304]{1,0:T(8,128)(2,1)} fusion(bf16[576,768]{1,0:T(8,128)(2,1)S(1)} %fusion.13.normed_ref, bf16[768,2304]{1,0:T(8,128)(2,1)} %bitcast.42), kind=kOutput, calls=%fused_computation.2 | convolution fusion | flops 2039758848 | bytes 7077888 | tf_op jit(solution)/shard_map/dot_general | solution.py:1495
  60.0 14.3 %attend.1.mixed_ref = bf16[576,768]{1,0:T(8,128)(2,1)} custom-call(s32[576,1]{1,0:T(8,128)} %reshape.189.segment_col, s32[1,576]{1,0:T(1,128)} %reshape.171.segment_row, s32[1,576]{1,0:T(1,128)} %reshape.172.live_row, bf16[576,2304]{1,0:T(8,128)(2,1)} %convolution_convert_fusion.query_ref.keys_ref.values_ref.qkv_ref, ...), custom_call_target="tpu_custom_call" | custom-call | flops 4076863488 | bytes 4194304 | tf_op jit(solution)/shard_map/attend/pallas_call | solution.py:703
  74.4 2.5 fusion.80
  76.9 1.1 copy.111.routes_ref
  78.0 0.9 broadcast_in_dim.3.live_col
  78.8 0.6 convert_element_type.168.b_back_ref
  79.4 0.6 convert_element_type.167.b_in_ref
  80.0 0.3 multiply_reduce_fusion
  80.4 0.4 add_convert_fusion.routed_ref
  80.8 1.5 fusion.81
  82.3 0.1 copy.106
  82.4 0.3 fusion.46
  82.7 0.6 fusion.39
  83.3 1.5 add_reduce_fusion
  84.9 0.7 pad.19.probs_ref
  85.7 2.4 convolution_convert_fusion.1
  88.2 0.7 bitcast_convert_fusion.3.vectors_ref
  88.8 0.6 copy-done.20
  89.4 2.3 fusion.1
  91.8 4.0 %all-to-all-done = bf16[8,160,768]{2,1,0:T(8,128)(2,1)} async-done(((bf16[8,160,768]{2,1,0:T(8,128)(2,1)}), bf16[8,160,768]{2,1,0:T(8,128)(2,1)}, u32[]{:S(2)}, u32[]{:S(2)}) %all-to-all-start) | async-done | bytes 1966112 | tf_op jit(solution)/shard_map/all_to_all | solution.py:1440
  95.8 107.8 %experts.1 = (bf16[8,160,768]{2,1,0:T(8,128)(2,1)}, bf16[1280,768]{1,0:T(8,128)(2,1)}, bf16[784,768]{1,0:T(8,128)(2,1)}, bf16[2,768,768]{2,1,0:T(8,128)(2,1)}) custom-call(bf16[8,160,768]{2,1,0:T(8,128)(2,1)} %copy-done.20, bf16[1280,768]{1,0:T(8,128)(2,1)} %bitcast.14.grad_ref, bf16[768,3072]{1,0:T(8,128)(2,1)} %bitcast.57, bf16[3072,768]{1,0:T(8,128)(2,1)} %bitcast.58, ...), custom_call_target="tpu_custom_call" | custom-call | flops 36238786560 | bytes 41943040 | tf_op jit(solution)/shard_map/experts/pallas_call | solution.py:631
  203.6 0.8 slice_bitcast_fusion
  204.4 0.1 reshape.180
  204.5 0.6 pad.18.terms_ref
  205.1 106.1 %backward.1 = (bf16[576,768]{1,0:T(8,128)(2,1)}, f32[576,768]{1,0:T(8,128)}, f32[24,2304]{1,0:T(8,128)}, f32[24,768]{1,0:T(8,128)}, f32[24,128]{1,0:T(8,128)}, /...) custom-call(bf16[1280,768]{1,0:T(8,128)(2,1)} %bitcast.48, ...), custom_call_target="tpu_custom_call" | custom-call | tf_op jit(solution)/shard_map/backward/pallas_call | solution.py:1430
  311.2 1.3 bitcast_convert_fusion.2
  312.5 0.8 slice.77
  313.3 1.6 slice_reduce_fusion
  314.9 0.6 convert.24
  315.5 1.4 copy.114
  316.9 7.5 %bitcast_convert_fusion.1 = f32[1,768,3072]{2,1,0:T(8,128)} fusion(bf16[768,3072]{1,0:T(8,128)(2,1)} %get-tuple-element.42), kind=kLoop, calls=%fused_computation.1 | loop fusion | flops 2359296 | bytes 14155776 | tf_op jit(solution)/shard_map/convert_element_type | solution.py:1579
  324.4 4.5 %bitcast_convert_fusion = f32[1,3072,768]{2,1,0:T(8,128)} fusion(bf16[3072,768]{1,0:T(8,128)(2,1)S(1)} %copy-done.3), kind=kLoop, calls=%fused_computation | loop fusion | flops 2359296 | bytes 14155776 | tf_op jit(solution)/shard_map/convert_element_type | solution.py:1581
  328.9 0.9 copy.123
  329.8 0.9 copy-done.5
  330.7 1.2 copy.124
  331.9 0.7 copy.125
  332.6 0.6 copy.126
  (58 shorter events, 0.5 us)
Async XLA Ops:
  0.6 6.1 %copy-start.11 = (s32[576,2]{0,1:T(2,128)S(1)}, s32[576,2]{0,1:T(2,128)}, u32[]{:S(2)}) copy-start(s32[576,2]{0,1:T(2,128)} %param.30) | copy-start | bytes 13828
  0.7 6.1 %copy-start.16 = (bf16[24]{0:T(256)(128)(2,1)S(1)}, bf16[24]{0:T(256)(128)(2,1)}, u32[]{:S(2)}) copy-start(bf16[24]{0:T(256)(128)(2,1)} %param.18) | copy-start | bytes 148
  0.7 6.2 %copy-start.17 = (bf16[24]{0:T(256)(128)(2,1)S(1)}, bf16[24]{0:T(256)(128)(2,1)}, u32[]{:S(2)}) copy-start(bf16[24]{0:T(256)(128)(2,1)} %param.19) | copy-start | bytes 148
  0.7 6.3 %copy-start.18 = (bf16[24]{0:T(256)(128)(2,1)S(1)}, bf16[24]{0:T(256)(128)(2,1)}, u32[]{:S(2)}) copy-start(bf16[24]{0:T(256)(128)(2,1)} %param.22) | copy-start | bytes 148
  0.7 6.4 %copy-start.19 = (bf16[24]{0:T(256)(128)(2,1)S(1)}, bf16[24]{0:T(256)(128)(2,1)}, u32[]{:S(2)}) copy-start(bf16[24]{0:T(256)(128)(2,1)} %param.23) | copy-start | bytes 148
  0.7 6.5 %copy-start.15 = (bf16[24,8]{0,1:T(8,128)(2,1)S(1)}, bf16[24,8]{0,1:T(8,128)(2,1)}, u32[]{:S(2)}) copy-start(bf16[24,8]{0,1:T(8,128)(2,1)} %param.24) | copy-start | bytes 1156
  0.7 6.7 %copy-start.12 = (bf16[24,768]{1,0:T(8,128)(2,1)S(1)}, bf16[24,768]{1,0:T(8,128)(2,1)}, u32[]{:S(2)}) copy-start(bf16[24,768]{1,0:T(8,128)(2,1)} %param.21) | copy-start | bytes 110596
  0.7 37.7 %copy-start.7 = (bf16[576,768]{1,0:T(8,128)(2,1)S(1)}, bf16[576,768]{1,0:T(8,128)(2,1)}, u32[]{:S(2)}) copy-start(bf16[576,768]{1,0:T(8,128)(2,1)} %cotangent_ref.1) | copy-start | bytes 2654212
  42.1 6.7 %copy-start.10 = (s32[576]{0:T(1024)S(1)}, s32[576]{0:T(1024)}, u32[]{:S(2)}) copy-start(s32[576]{0:T(1024)} %param.32) | copy-start | bytes 6916
  42.1 7.3 %copy-start.21 = (s32[1,3]{1,0:T(1,128)S(1)}, s32[1,3]{1,0:T(1,128)}, u32[]{:S(2)}) copy-start(s32[1,3]{1,0:T(1,128)} %param.29) | copy-start | bytes 40
  42.1 9.0 %copy-start.1 = (bf16[576,768]{1,0:T(8,128)(2,1)S(1)}, bf16[576,768]{1,0:T(8,128)(2,1)}, u32[]{:S(2)}) copy-start(bf16[576,768]{1,0:T(8,128)(2,1)} %tokens_ref.1) | copy-start | bytes 2654212
  42.1 53.7 %all-to-all-start = ((bf16[8,160,768]{2,1,0:T(8,128)(2,1)}), bf16[8,160,768]{2,1,0:T(8,128)(2,1)}, u32[]{:S(2)}, u32[]{:S(2)}) async-start(bf16[8,160,768]{2,1,0:T(8,128)(2,1)} %bitcast.8), calls=%async_computation | async-start | bytes 3932160 | tf_op jit(solution)/shard_map/all_to_all | solution.py:1440
  53.4 0.9 copy-start.4
  74.4 4.4 %copy-start.14 = (bf16[1,768]{1,0:T(2,128)(2,1)S(1)}, bf16[1,768]{1,0:T(2,128)(2,1)}, u32[]{:S(2)}) copy-start(bf16[1,768]{1,0:T(2,128)(2,1)} %param.28) | copy-start | bytes 4612
  74.4 5.0 %copy-start.13 = (bf16[1,3072]{1,0:T(2,128)(2,1)S(1)}, bf16[1,3072]{1,0:T(2,128)(2,1)}, u32[]{:S(2)}) copy-start(bf16[1,3072]{1,0:T(2,128)(2,1)} %param.26) | copy-start | bytes 18436
  76.9 3.8 %copy-start = (f32[576,768]{1,0:T(8,128)}, f32[576,768]{1,0:T(8,128)S(1)}, u32[]{:S(2)}) copy-start(f32[576,768]{1,0:T(8,128)S(1)} %get-tuple-element.129.resid_ref) | copy-start | bytes 5308420
  80.8 7.3 %copy-start.2 = (bf16[576,768]{1,0:T(8,128)(2,1)}, bf16[576,768]{1,0:T(8,128)(2,1)S(1)}, u32[]{:S(2)}) copy-start(bf16[576,768]{1,0:T(8,128)(2,1)S(1)} %add_convert_fusion.routed_ref) | copy-start | bytes 2654212
  88.1 1.3 copy-start.20
  316.9 7.5 %copy-start.3 = (bf16[3072,768]{1,0:T(8,128)(2,1)S(1)}, bf16[3072,768]{1,0:T(8,128)(2,1)}, u32[]{:S(2)}) copy-start(bf16[3072,768]{1,0:T(8,128)(2,1)} %get-tuple-element.44) | copy-start | bytes 14155780
  324.4 4.5 %copy-start.6 = (bf16[576,768]{1,0:T(8,128)(2,1)S(1)}, bf16[576,768]{1,0:T(8,128)(2,1)}, u32[]{:S(2)}) copy-start(bf16[576,768]{1,0:T(8,128)(2,1)} %get-tuple-element.147) | copy-start | bytes 2654212
  328.9 1.8 copy-start.5
  330.7 1.2 copy-start.8
  330.7 1.9 copy-start.9
